TPU v7x, 32 devices: a whole 2x2x4 slice. The times are simulated.
32 devices in a mesh: field: 8 (over y, x, core), point: 4 (over z).
Axes of the slice: x: 2, y: 2, z: 4, core: 2. Of those that a mesh axis runs over, the one named last changes fastest.
Arguments:
- residual_in: bfloat16 [8, 1024, 2048], P('field', 'point'), may hold values from -6 to 6
- coefs_in: bfloat16 [8, 1024, 4, 256], P('field', 'point'), may hold values from 0 to 1
- dictionary: bfloat16 [2048, 2048], P('field'), may hold values from -0.125 to 0.125
- owner_order: int32 [8], replicated, may hold values from 0 to 7, each once
- pixel_of: int32 [8, 1024], P('field', 'point'), may hold values from 0 to 1023, each once within a row
Outputs:
- maps: float32 [8, 4, 256, 8, 128], P('field', None, 'point')
Inputs may be any that keep to these rules, and one draw needn't show every extreme that they name: `owner_order`: A permutation of the dictionary blocks. `pixel_of`: each field's row is a permutation of its scan points over the 8 x 128 pixels.
All inputs are finite; a program needn't handle non-finite values.
Results may differ from a plain program's by a relative error of at most 0.00045.
Values may be sent and summed in bfloat16 or wider, within the bound.
No kernel may reach another device: no remote copies, remote signals or barrier semaphores. Data moves between devices by JAX's collectives and lax.ppermute only.
A program may use at most 64 MiB of HBM per device.

v0:
```python
import jax
import jax.numpy as jnp
from jax import lax
from jax.sharding import PartitionSpec as P

TURNS = 4
SWEEPS = 4
MAP_W = 128


time_step = 0.2
edge_scale = 0.5


def from_root(value, axis, source):
    kept = jnp.where(lax.axis_index(axis) == source, value, 0).astype(value.dtype)
    return lax.psum(kept, axis)


def block_steps(templates):
    gram = lax.dot_general(
        templates, templates, (((1,), (1,)), ((), ())), preferred_element_type=jnp.float32
    )
    return 1.0 / jnp.sum(jnp.abs(gram), axis=1)


def diffuse(grids):
    for repeat in range(SWEEPS):
        padded = jnp.pad(grids, ((0, 0), (1, 1), (1, 1)), mode="edge")
        summed = jnp.zeros_like(grids)
        for neighbour in (
            padded[:, :-2, 1:-1],
            padded[:, 2:, 1:-1],
            padded[:, 1:-1, :-2],
            padded[:, 1:-1, 2:],
        ):
            differ = neighbour - grids
            scaled = differ / edge_scale
            summed = summed + differ / (1.0 + scaled * scaled)
        grids = grids + time_step * summed
    return grids


def build_maps(moved, pixel_ids):
    points = moved.shape[0]
    count = moved.shape[1]
    local_kb = moved.shape[2]
    values = moved.reshape(points, count * local_kb).T
    flat = jnp.zeros((count * local_kb, points), jnp.float32).at[:, pixel_ids].set(values)
    grids = diffuse(flat.reshape(count * local_kb, points // MAP_W, MAP_W))
    return grids.reshape(count, local_kb, points // MAP_W, MAP_W)


def per_device(residual_in, coefs_in, dictionary, owner_order, pixel_of):
    residual = residual_in[0]
    coefs = coefs_in[0].astype(jnp.float32)
    pixel_ids = lax.all_gather(pixel_of[0], "point", axis=0, tiled=True)
    own_steps = block_steps(dictionary)
    updated = []
    for turn_index in range(TURNS):
        owner = owner_order[turn_index]
        templates = from_root(dictionary, "field", owner)
        step_size = from_root(own_steps, "field", owner)
        correlation = lax.dot_general(
            residual, templates, (((1,), (1,)), ((), ())), preferred_element_type=jnp.float32
        )
        before = coefs[:, turn_index, :]
        after = jnp.maximum(before + step_size[None, :] * correlation, 0.0)
        updated.append(after)
        if turn_index + 1 < TURNS:
            change = (after - before).astype(jnp.bfloat16)
            residual = (
                residual.astype(jnp.float32)
                - jnp.dot(change, templates, preferred_element_type=jnp.float32)
            ).astype(jnp.bfloat16)
    stacked = jnp.stack(updated, axis=1)
    maps = build_maps(
        lax.all_to_all(stacked, "point", split_axis=2, concat_axis=0, tiled=True), pixel_ids
    )
    return maps[None]


def solution(mesh):
    placed = (
        P("field", "point", None),
        P("field", "point", None, None),
        P("field", None),
        P(),
        P("field", "point"),
    )
    return jax.shard_map(
        per_device,
        mesh=mesh,
        in_specs=placed,
        out_specs=P("field", None, "point", None, None),
        check_vma=False,
    )
```

profile of v0, /device:TPU:10, one launch (start us, length us, event | category | flops | bytes accessed | tf_op | source)
XLA Modules:
  0.0 155.9 jit_solution(16890992155468359398)
XLA Ops:
  6.5 0.0 all-reduce.4.cloned.1.call-start
  6.5 1.4 fusion.65
  10.4 3.3 %broadcast_select_fusion.3 = (bf16[256,2048]{1,0:T(8,128)(2,1)}, bf16[256,2048]{1,0:T(8,128)(2,1)}, bf16[256,2048]{1,0:T(8,128)(2,1)}, bf16[256,2048]{1,0:T(8,128)(2,1)}) fusion(bf16[256,2048]{1,0:T(8,128)(2,1)} %param.7, pred[]{:T(512)S(6)} %eq.16, pred[]{:T(512)S(6)} %eq.17, pred[]{:T(512)S(6)} %eq.19, pred[]{:T(512)S(6)} %eq.18), kind=kLoop, calls=%fused_computation.117 | loop fusion | flops 2097152 | bytes 5242884 | tf_op jit(solution)/shard_map/jit(_where)/select_n | solution.py:16
  13.8 0.0 copy-start.5
  13.8 0.0 all-reduce.4.cloned.1.call-update
  13.8 1.0 copy-done.5
  14.8 0.0 copy-start.3
  14.8 0.3 copy.19
  15.1 0.9 copy-done.3
  16.0 0.5 fusion.15
  16.5 0.0 copy-start
  16.6 11.6 %all-reduce = (f32[256]{0:T(256)S(1)}, f32[256]{0:T(256)S(1)}, f32[256]{0:T(256)S(1)}, f32[256]{0:T(256)S(1)}) all-reduce(f32[256]{0:T(256)S(1)} %get-tuple-element.29, f32[256]{0:T(256)S(1)} %get-tuple-element.28, f32[256]{0:T(256)S(1)} %get-tuple-element.27, ...), channel_id=1, replica_groups=mesh['field'=8,'point'=4] {'field'}, use_global_device_ids=true, to_apply=%region_1.2 | all-reduce | flops 1024 | bytes 8192 | tf_op jit(solution)/shard_map/psum | solution.py:17
  28.1 0.1 bitcast_convert_fusion
  28.2 67.9 %all-reduce.4.cloned.1.call-done = (bf16[256,2048]{1,0:T(8,128)(2,1)}, bf16[256,2048]{1,0:T(8,128)(2,1)}, bf16[256,2048]{1,0:T(8,128)(2,1)}, bf16[256,2048]{1,0:T(8,128)(2,1)}) async-done(((bf16[256,2048]{1,0:T(8,128)(2,1)}, bf16[256,2048]{1,0:T(8,128)(2,1)}, bf16[256,2048]{1,0:T(8,128)(2,1)}, bf16[256,2048]{1,0:T(8,128)(2,1)}), (bf16[256,2048]{1,0:T(8,128)(2,1)}, bf16[256,2048]{1,0:T(8,128)(2,1)}, ...) | async-done | bytes 4194320 | tf_op jit(solution)/shard_map/psum | solution.py:17
  96.1 0.0 copy-done
  96.2 0.0 copy-start.2
  96.2 1.8 %fusion.14 = f32[256,256]{0,1:T(8,128)S(1)} fusion(bf16[256,2048]{1,0:T(8,128)(2,1)} %get-tuple-element.12, bf16[1,256,2048]{2,1,0:T(8,128)(2,1)S(1)} %copy-done, f32[256,4,256]{0,2,1:T(8,128)S(1)} %bitcast_convert_fusion, f32[256]{0:T(256)S(1)} %get-tuple-element.5), kind=kOutput, calls=%fused_computation.37 | convolution fusion | flops 268632064 | bytes 2622464 | tf_op jit(solution)/shard_map/dot_general | solution.py:64
  97.9 0.0 copy-done.2
  98.0 0.0 copy-start.1
  98.0 0.5 fusion
  98.4 0.7 copy-done.1
  99.2 0.5 fusion.11
  99.7 0.0 copy-start.4
  99.7 0.5 fusion.1
  100.1 0.7 copy-done.4
  100.9 0.5 fusion.9
  101.4 2.5 %fusion.7 = f32[256,1,256]{0,2,1:T(8,128)S(1)} fusion(bf16[256,2048]{1,0:T(8,128)(2,1)} %get-tuple-element.9, bf16[256,2048]{1,0:T(8,128)(2,1)} %get-tuple-element.10, bf16[256,2048]{1,0:T(8,128)(2,1)S(1)} %fusion.1, f32[256,4,256]{0,2,1:T(8,128)S(1)} %bitcast_convert_fusion, f32[256,256]{0,1:T(8,128)S(1)} %fusion.9, f32[256]{0:T(256)S(1)} %get-tuple-element.8), kind=kOutput, calls=%fused_computation.27 | convolution fusion | flops 538771456 | bytes 4195328 | tf_op jit(solution)/shard_map/dot_general | solution.py:64
  103.9 0.1 pad_maximum_fusion.24
  103.9 1.6 %copy.23 = f32[256,4,256]{0,1,2:T(4,128)} copy(f32[256,4,256]{0,2,1:T(8,128)S(1)} %pad_maximum_fusion.24) | data formatting | bytes 2097152 | tf_op jit(solution)/shard_map/stack | solution.py:76
  105.6 0.0 copy-start.6
  105.6 5.3 %all-to-all-start = ((f32[256,4,256]{0,1,2:T(4,128)}), f32[256,4,256]{0,1,2:T(4,128)S(1)}, u32[]{:S(2)}, u32[]{:S(2)}) async-start(f32[256,4,256]{0,1,2:T(4,128)} %copy.23), calls=%async_computation | async-start | bytes 2097152 | tf_op jit(solution)/shard_map/all_to_all | solution.py:78
  110.9 0.0 copy-done.6
  110.9 25.4 %all-gather = s32[1,1024]{1,0:T(1,128)S(1)} all-gather(s32[1,256]{1,0:T(1,128)S(1)} %copy-done.6), channel_id=2, replica_groups=mesh['field'=8,'point'=4] {'point'}, dimensions={1}, use_global_device_ids=true | all-gather | bytes 5120 | tf_op jit(solution)/shard_map/all_gather | solution.py:57
  136.3 0.0 all-to-all-done
  136.3 0.7 copy.24
  136.9 0.2 copy.30
  137.2 0.3 copy.25
  137.5 5.0 %scatter_custom_fusion = f32[256,1024]{0,1:T(8,128)S(1)} fusion(s32[1024]{0:T(1024)S(1)} %compare_select_fusion, f32[1024,256]{1,0:T(8,128)S(1)} %copy.25, f32[]{:T(128)} %constant.32.clone.1), kind=kCustom, calls=%fused_computation.119 | custom fusion | bytes 1048580 | tf_op jit(solution)/shard_map/scatter | solution.py:49
  142.6 1.3 multiply_add_fusion.3
  143.9 1.3 multiply_add_fusion.2
  145.2 1.3 multiply_add_fusion.1
  146.5 1.3 multiply_add_fusion
  147.8 1.3 copy.26
  (7 shorter events, 0.1 us)
Async XLA Ops:
  6.5 89.6 %all-reduce.4.cloned.1.call-start = ((), (), s32[]{:S(2)}) async-start(), calls=%async_computation.1 | async-start | bytes 8388608 | tf_op jit(solution)/shard_map/psum | solution.py:17
  13.8 1.0 copy-start.5
  14.8 1.2 copy-start.3
  16.5 79.6 %copy-start = (bf16[1,256,2048]{2,1,0:T(8,128)(2,1)S(1)}, bf16[1,256,2048]{2,1,0:T(8,128)(2,1)}, u32[]{:S(2)}) copy-start(bf16[1,256,2048]{2,1,0:T(8,128)(2,1)} %param.5) | copy-start | bytes 3145732
  96.2 1.8 %copy-start.2 = (bf16[256,2048]{1,0:T(8,128)(2,1)S(1)}, bf16[256,2048]{1,0:T(8,128)(2,1)}, u32[]{:S(2)}) copy-start(bf16[256,2048]{1,0:T(8,128)(2,1)} %get-tuple-element.12) | copy-start | bytes 3145732
  98.0 1.2 copy-start.1
  99.7 1.2 copy-start.4
  105.6 5.3 %copy-start.6 = (s32[1,256]{1,0:T(1,128)S(1)}, s32[1,256]{1,0:T(1,128)}, u32[]{:S(2)}) copy-start(s32[1,256]{1,0:T(1,128)} %param.9) | copy-start | bytes 3076
  105.6 30.7 %all-to-all-start = ((f32[256,4,256]{0,1,2:T(4,128)}), f32[256,4,256]{0,1,2:T(4,128)S(1)}, u32[]{:S(2)}, u32[]{:S(2)}) async-start(f32[256,4,256]{0,1,2:T(4,128)} %copy.23), calls=%async_computation | async-start | bytes 2097152 | tf_op jit(solution)/shard_map/all_to_all | solution.py:78
Sparse Core Ops, SparseCore 0:
  13.9 82.1 all-reduce.3
where the time goes:
time: 158 us; the launch traced here: 156 us
  waiting for transfers between devices  67.9 us (43%)
  blocking collectives  37 us (23%)
  between operations  16.1 us (10%)
  local copies, waits for them, and re-layouts  14.5 us (9%)
  other arithmetic  8.6 us (5%)
  matrix products  6.62 us (4%)
  starting transfers between devices  5.27 us (3%)
    psum x1, waiting for transfers between devices, from_root(): return lax.psum(kept, axis)  67.9 us
    all_gather x1, blocking collectives, per_device(): pixel_ids = lax.all_gather(pixel_of[0], 'point', axis=0, tiled=True)  25.4 us
    psum x1, blocking collectives, from_root(): return lax.psum(kept, axis)  11.6 us
    all_to_all x1, starting transfers between devices, per_device(): lax.all_to_all(stacked, 'point', split_axis=2, concat_axis=0, tiled=True)  5.26 us
    dot_general x4, matrix products, per_device(): lax.dot_general(residual, templates, (((1,), (1,)), ((), ())), preferred_...  5.21 us
    add x4, other arithmetic, diffuse(): grids = grids + time_step * summed  5.1 us
    scatter x1, local copies, waits for them, and re-layouts, build_maps(): jnp.zeros((count * local_kb, points), jnp.float32).at[:, pixel_ids]  5.05 us
    unnamed x16, local copies, waits for them, and re-layouts  3.94 us
  transfers between devices with their start and end apart: 2, of which 1 were waited for; matrix products, arithmetic and copies ran while one was open for 1% of the time, Pallas kernels for 0%

commit v1 on v0

v1 whole, which is shorter than its diff:
```python
import functools

import jax
import jax.numpy as jnp
from jax import lax
from jax.experimental import pallas as pl
from jax.experimental.pallas import tpu as pltpu
from jax.sharding import PartitionSpec as P

TURNS = 4
SWEEPS = 4
MAP_W = 128
SUBLANES = 8
PARTS = 3

time_step = 0.2

GROUPS = ((0, 1), (2, 3))

ANY = pl.BlockSpec(memory_space=pl.ANY)
VMEM = pl.BlockSpec(memory_space=pltpu.VMEM)
SMEM = pl.BlockSpec(memory_space=pltpu.SMEM)


def place_of_device():
    index = lax.axis_index("field")
    return index // 2, index % 2


def slice_kernel(chips, block_ref, *refs):
    keep, give, sems = refs[:chips], refs[chips : 2 * chips], refs[2 * chips]
    chip, core = place_of_device()
    rows, half = keep[0].shape
    copies = []
    for k in range(chips):
        top = pl.multiple_of((chip ^ k) * rows, rows)
        for number, (out, which) in enumerate(((give[k], 1 - core), (keep[k], core))):
            left = pl.multiple_of(which * half, half)
            copy = pltpu.make_async_copy(
                block_ref.at[pl.ds(top, rows), pl.ds(left, half)], out, sems.at[2 * k + number]
            )
            copy.start()
            copies.append(copy)
    for copy in copies:
        copy.wait()


def cut_block(block, chips):
    kb, features = block.shape
    piece = jax.ShapeDtypeStruct((kb // chips, features // 2), block.dtype)
    outs = pl.pallas_call(
        functools.partial(slice_kernel, chips),
        out_shape=[piece] * (2 * chips),
        in_specs=[ANY],
        out_specs=[VMEM] * (2 * chips),
        scratch_shapes=[pltpu.SemaphoreType.DMA((2 * chips,))],
        name="cut",
    )(block)
    return outs[:chips], outs[chips:]


def pick_kernel(chips, order_ref, *refs):
    same, other = refs[:chips], refs[chips : 2 * chips]
    outs, sems = refs[2 * chips : 2 * chips + TURNS], refs[2 * chips + TURNS]
    chip, core = place_of_device()
    for turn in range(TURNS):
        owner = order_ref[turn]
        distance = (owner // 2) ^ chip
        mine = owner % 2 == core
        for k in range(chips):

            @pl.when((distance == k) & mine)
            def _():
                pltpu.make_async_copy(same[k], outs[turn], sems.at[turn]).start()

            @pl.when((distance == k) & jnp.logical_not(mine))
            def _():
                pltpu.make_async_copy(other[k], outs[turn], sems.at[turn]).start()

    for turn in range(TURNS):
        pltpu.make_async_copy(same[0], outs[turn], sems.at[turn]).wait()


def pick_turns(owner_order, same, other):
    chips = len(same)
    piece = jax.ShapeDtypeStruct(same[0].shape, same[0].dtype)
    return pl.pallas_call(
        functools.partial(pick_kernel, chips),
        out_shape=[piece] * TURNS,
        in_specs=[SMEM] + [ANY] * (2 * chips),
        out_specs=[VMEM] * TURNS,
        scratch_shapes=[pltpu.SemaphoreType.DMA((TURNS,))],
        name="pick",
    )(owner_order, *same, *other)


def turn_kernel(turns, chips, parts, last, with_pixels, *refs):
    count = len(turns)
    refs = list(refs)
    residual_ref, coefs_ref = refs.pop(0), refs.pop(0)
    pixel_ref = refs.pop(0) if with_pixels else None
    pieces = [[refs.pop(0) for _ in range(2 * chips)] for _ in turns]
    residual_out = None if last else refs.pop(0)
    sends = [refs.pop(0) for _ in range(parts)]
    blocks, values, held, sems = refs

    chip, core = place_of_device()
    slot = lax.axis_index("point")
    rows, half = pieces[0][0].shape
    kb = rows * chips
    local_kb = kb // parts
    copies = []
    for position in range(count):
        for number, piece in enumerate(pieces[position]):
            k, which = number % chips, number // chips
            top = pl.multiple_of((chip ^ k) * rows, rows)
            left = pl.multiple_of((core if which == 0 else 1 - core) * half, half)
            copy = pltpu.make_async_copy(
                piece,
                blocks.at[position, pl.ds(top, rows), pl.ds(left, half)],
                sems.at[position, number],
            )
            copy.start()
            copies.append((position, copy))

    source = residual_ref
    for position, turn in enumerate(turns):
        for where, copy in copies:
            if where == position:
                copy.wait()
        block = blocks.at[position]
        templates = block[...]
        gram = lax.dot_general(
            templates, templates, (((1,), (1,)), ((), ())), preferred_element_type=jnp.float32
        )
        step = 1.0 / jnp.sum(jnp.abs(gram), axis=0, keepdims=True)
        correlation = lax.dot_general(
            source[...], templates, (((1,), (1,)), ((), ())), preferred_element_type=jnp.float32
        )
        before = coefs_ref[:, turn * kb : (turn + 1) * kb].astype(jnp.float32)
        after = jnp.maximum(before + step * correlation, 0.0)
        if turn + 1 < TURNS:
            change = (after - before).astype(jnp.bfloat16)
            features = 2 * half
            width = features // 4
            target = residual_out if position + 1 == count else held
            for start in range(0, features, width):
                columns = slice(start, start + width)
                moved = jnp.dot(change, block[:, columns], preferred_element_type=jnp.float32)
                target[:, columns] = (source[:, columns].astype(jnp.float32) - moved).astype(
                    jnp.bfloat16
                )
            source = target
        values[...] = after.T
        for m in range(parts):
            top = pl.multiple_of((slot ^ m) * local_kb, local_kb)
            sends[m][position * local_kb : (position + 1) * local_kb, :] = values[
                pl.ds(top, local_kb), :
            ]
    if with_pixels:
        row = jnp.broadcast_to(pixel_ref[...].astype(jnp.float32), (SUBLANES, values.shape[1]))
        for m in range(parts):
            sends[m][count * local_kb :, :] = row


def run_turns(turns, residual, coefs, pixels, pieces, parts):
    count = len(turns)
    last = turns[-1] + 1 == TURNS
    chips = len(pieces[0]) // 2
    rows, half = pieces[0][0].shape
    points, features = residual.shape
    kb = rows * chips
    local_kb = kb // parts
    height = count * local_kb + (SUBLANES if pixels is not None else 0)
    send = jax.ShapeDtypeStruct((height, points), jnp.float32)
    flat = [piece for turn in pieces for piece in turn]
    first = [] if last else [jax.ShapeDtypeStruct(residual.shape, residual.dtype)]
    extra = [] if pixels is None else [pixels]
    flops = count * 2 * kb * features * (kb + 2 * points)
    outs = pl.pallas_call(
        functools.partial(turn_kernel, turns, chips, parts, last, pixels is not None),
        out_shape=first + [send] * parts,
        in_specs=[VMEM, VMEM] + [VMEM] * len(extra) + [ANY] * len(flat),
        out_specs=[VMEM] * (len(first) + parts),
        scratch_shapes=[
            pltpu.VMEM((count, kb, features), residual.dtype),
            pltpu.VMEM((kb, points), jnp.float32),
            pltpu.VMEM(residual.shape, residual.dtype),
            pltpu.SemaphoreType.DMA((count, 2 * chips)),
        ],
        cost_estimate=pl.CostEstimate(
            flops=flops, bytes_accessed=2 * features * (2 * points + count * kb), transcendentals=0
        ),
        name="turns_" + str(turns[0]),
    )(residual, coefs, *extra, *flat)
    outs = list(outs)
    return (None if last else outs.pop(0)), outs


def spread(whole):
    rows = len(whole)
    lane = lax.broadcasted_iota(jnp.int32, whole[0].shape, 1)
    inner = lane < MAP_W - 1

    def flow(differ):
        scaled = differ + differ
        return differ / (1.0 + scaled * scaled)

    down = [flow(whole[r + 1] - whole[r]) for r in range(rows - 1)]
    new = []
    for r in range(rows):
        right = flow(pltpu.roll(whole[r], MAP_W - 1, 1) - whole[r])
        right = jnp.where(inner, right, 0.0)
        total = right - pltpu.roll(right, 1, 1)
        if r > 0:
            total = total - down[r - 1]
        if r + 1 < rows:
            total = total + down[r]
        new.append(whole[r] + time_step * total)
    return new


def map_kernel(turns, parts, local_kb, first, *refs):
    count = len(turns)
    refs = list(refs)
    received = [refs.pop(0) for _ in range(parts)]
    pixel_refs = received if first else [refs.pop(0) for _ in range(parts)]
    if not first:
        refs.pop(0)
    out_ref, grids, staged, sem = refs
    rows = grids.shape[0]
    height = count * local_kb
    pieces = []
    for m in range(parts):
        left = received[m][:height, :]
        columns = []
        for part in range(PARTS):
            top = left.astype(jnp.bfloat16)
            columns.append(top)
            if part + 1 < PARTS:
                left = left - top.astype(jnp.float32)
        pieces.append(jnp.concatenate(columns, axis=0))
    values = jnp.concatenate(pieces, axis=1)
    depth = pixel_refs[0].shape[0]
    targets = jnp.concatenate([ref[depth - 1 : depth, :] for ref in pixel_refs], axis=1)
    targets = targets.astype(jnp.int32)
    pixel = lax.broadcasted_iota(jnp.int32, (MAP_W, targets.shape[1]), 0)
    for r in range(rows):
        chosen = jnp.where(pixel == targets - r * MAP_W, 1.0, 0.0).astype(jnp.bfloat16)
        moved = lax.dot_general(
            values, chosen, (((1,), (1,)), ((), ())), preferred_element_type=jnp.float32
        )
        total = moved[:height]
        for part in range(1, PARTS):
            total = total + moved[part * height : (part + 1) * height]
        grids[r] = total

    def one(group, carry):
        top = pl.multiple_of(group * SUBLANES, SUBLANES)
        whole = [grids[r, pl.ds(top, SUBLANES), :] for r in range(rows)]
        for _ in range(SWEEPS):
            whole = spread(whole)
        for r in range(rows):
            staged[pl.ds(group * (SUBLANES * rows) + r, SUBLANES, stride=rows), :] = whole[r]
        return carry

    lax.fori_loop(0, height // SUBLANES, one, 0)
    copy = pltpu.make_async_copy(staged, out_ref.at[pl.ds(turns[0] * local_kb * rows, height * rows)], sem)
    copy.start()
    copy.wait()


def run_maps(turns, received, pixels, buffer, local_kb):
    parts = len(received)
    points = received[0].shape[1]
    rows = parts * points // MAP_W
    first = buffer is None
    height = len(turns) * local_kb
    extra = [] if first else list(pixels) + [buffer]
    return pl.pallas_call(
        functools.partial(map_kernel, turns, parts, local_kb, first),
        out_shape=jax.ShapeDtypeStruct((TURNS * local_kb * rows, MAP_W), jnp.float32),
        in_specs=[VMEM] * (parts if first else 2 * parts) + ([] if first else [ANY]),
        out_specs=ANY,
        scratch_shapes=[
            pltpu.VMEM((rows, height, MAP_W), jnp.float32),
            pltpu.VMEM((height * rows, MAP_W), jnp.float32),
            pltpu.SemaphoreType.DMA,
        ],
        input_output_aliases={} if first else {2 * parts: 0},
        cost_estimate=pl.CostEstimate(
            flops=2 * PARTS * height * (parts * points) ** 2,
            bytes_accessed=8 * height * parts * points,
            transcendentals=0,
        ),
        name="maps_" + str(turns[0]),
    )(*received, *extra)


def exchange(value, axis, size, distance):
    return lax.ppermute(value, axis, [(i, i ^ distance) for i in range(size)])


def per_device(fields, parts, residual_in, coefs_in, dictionary, owner_order, pixel_of):
    residual = residual_in[0]
    points = residual.shape[0]
    coefs = coefs_in[0].reshape(points, -1)
    kb = dictionary.shape[0]
    local_kb = kb // parts
    chips = fields // 2
    over_chips = lambda value, k: exchange(value, "field", fields, 2 * k)
    over_cores = lambda value: exchange(value, "field", fields, 1)

    give, keep = None, None
    keep, give = cut_block(dictionary, chips)
    got = [over_cores(value) for value in give]
    same = [keep[0]] + [over_chips(keep[k], k) for k in range(1, chips)]
    other = [got[0]] + [over_chips(got[k], k) for k in range(1, chips)]
    chosen = pick_turns(owner_order, same, other)

    def gather(turn):
        held = [chosen[turn]]
        for k in range(1, chips):
            low = k & -k
            high = 1 << (k.bit_length() - 1)
            bit = high if turn % 2 == 0 else low
            held.append(over_chips(held[k ^ bit], bit))
        return held + [over_cores(value) for value in held]

    pixels = pixel_of.reshape(1, points)
    buffer, ids = None, None
    for turns in GROUPS:
        pieces = [gather(turn) for turn in turns]
        first = buffer is None
        residual, sends = run_turns(turns, residual, coefs, pixels if first else None, pieces, parts)
        received = [sends[0]] + [exchange(sends[m], "point", parts, m) for m in range(1, parts)]
        if first:
            ids = received
        buffer = run_maps(turns, received, ids, buffer, local_kb)
    rows = parts * points // MAP_W
    return buffer.reshape(1, TURNS, local_kb, rows, MAP_W)


def solution(mesh):
    placed = (
        P("field", "point", None),
        P("field", "point", None, None),
        P("field", None),
        P(),
        P("field", "point"),
    )
    return jax.shard_map(
        functools.partial(per_device, mesh.shape["field"], mesh.shape["point"]),
        mesh=mesh,
        in_specs=placed,
        out_specs=P("field", None, "point", None, None),
        check_vma=False,
    )
```

time: 158 us -> 110 us (0.70)
  Pallas kernels: 0 us -> 44.5 us
  blocking collectives: 37 us -> 0 us
  waiting for transfers between devices: 67.9 us -> 32.5 us
  starting transfers between devices: 5.27 us -> 27.8 us
  between operations: 16.1 us -> 0.47 us
  local copies, waits for them, and re-layouts: 14.5 us -> 4.3 us
  other arithmetic: 8.6 us -> 0 us
  matrix products: 6.62 us -> 0 us
    psum x1 -> x0, waiting for transfers between devices: 67.9 us -> none  [from_root(): return lax.psum(kept, axis)]
    pallas_call x0 -> x6, Pallas kernels: none -> 44.5 us  [the longest x2 27.4 us: run_maps(): pl.pallas_call(functools.partial(map_kernel, turns, parts, local_kb, firs...]
    ppermute x0 -> x44, waiting for transfers between devices: none -> 32.5 us  [exchange(): return lax.ppermute(value, axis, [(i, i ^ distance) for i in range(size)])]
    ppermute x0 -> x44, starting transfers between devices: none -> 27.8 us  [exchange(): return lax.ppermute(value, axis, [(i, i ^ distance) for i in range(size)])]
    all_gather x1 -> x0, blocking collectives: 25.4 us -> none  [per_device(): pixel_ids = lax.all_gather(pixel_of[0], 'point', axis=0, tiled=True)]
    psum x1 -> x0, blocking collectives: 11.6 us -> none  [from_root(): return lax.psum(kept, axis)]
    dot_general x7 -> x0, matrix products: 6.62 us -> none  [the longest x4 5.21 us: per_device(): lax.dot_general(residual, templates, (((1,), (1,)), ((), ())), preferred_...]
    all_to_all x1 -> x0, starting transfers between devices: 5.26 us -> none  [per_device(): lax.all_to_all(stacked, 'point', split_axis=2, concat_axis=0, tiled=True)]
  transfers between devices with their start and end apart: 2 -> 44, of which waited for: 1 -> 16; matrix products, arithmetic and copies ran while one was open for 1% -> 1% of each run, Pallas kernels for 0% -> 23%
where the time goes in v1:
time: 110 us; the launch traced here: 109 us
  Pallas kernels  44.5 us (40%)
  waiting for transfers between devices  32.5 us (30%)
  starting transfers between devices  27.8 us (25%)
  local copies, waits for them, and re-layouts  4.3 us (4%)
    ppermute x44, waiting for transfers between devices, exchange(): return lax.ppermute(value, axis, [(i, i ^ distance) for i in range(size)])  32.5 us
    ppermute x44, starting transfers between devices, exchange(): return lax.ppermute(value, axis, [(i, i ^ distance) for i in range(size)])  27.8 us
    pallas_call x2, Pallas kernels, run_maps(): pl.pallas_call(functools.partial(map_kernel, turns, parts, local_kb, firs...  27.4 us
    pallas_call x2, Pallas kernels, run_turns(): pl.pallas_call(functools.partial(turn_kernel, turns, chips, parts, last,...  12.1 us
    unnamed x85, local copies, waits for them, and re-layouts  4.3 us
    pallas_call x1, Pallas kernels, pick_turns(): pl.pallas_call(functools.partial(pick_kernel, chips), out_shape=[piece] *...  2.75 us
    pallas_call x1, Pallas kernels, cut_block(): pl.pallas_call(functools.partial(slice_kernel, chips), out_shape=[piece]...  2.3 us
  transfers between devices with their start and end apart: 44, of which 16 were waited for; matrix products, arithmetic and copies ran while one was open for 1% of the time, Pallas kernels for 23%

profile of v1, /device:TPU:10, one launch (start us, length us, event | category | flops | bytes accessed | tf_op | source)
XLA Modules:
  0.0 109.5 jit_solution(8272391695342910404)
XLA Ops:
  0.0 2.3 %cut.1 = (bf16[64,1024]{1,0:T(8,128)(2,1)}, bf16[64,1024]{1,0:T(8,128)(2,1)}, bf16[64,1024]{1,0:T(8,128)(2,1)}, bf16[64,1024]{1,0:T(8,128)(2,1)}, bf16[64,1024]{...) custom-call(bf16[256,2048]{1,0:T(8,128)(2,1)} %block_ref.1), custom_call_target="tpu_custom_call" | custom-call | tf_op jit(solution)/shard_map/cut/pallas_call | solution.py:51
  2.3 0.6 collective-permute-start
  2.9 1.5 %collective-permute-start.1 = (bf16[64,1024]{1,0:T(8,128)(2,1)}, bf16[64,1024]{1,0:T(8,128)(2,1)S(1)}, u32[]{:S(2)}, u32[]{:S(2)}) collective-permute-start(bf16[64,1024]{1,0:T(8,128)(2,1)} %get-tuple-element.28), channel_id=1, source_target_pairs={{0,16},{4,20},{8,24},{12,28},{16,0},{20,4},{24,8},{28,12},{1,17},{... | collective-permute-start | bytes 393224 | tf_op jit(solution)/shard_map/ppermute | solution.py:301
  4.4 0.5 collective-permute-start.6
  4.9 2.9 %collective-permute-done.refs_1_ = bf16[64,1024]{1,0:T(8,128)(2,1)S(1)} collective-permute-done((bf16[64,1024]{1,0:T(8,128)(2,1)}, bf16[64,1024]{1,0:T(8,128)(2,1)S(1)}, u32[]{:S(2)}, u32[]{:S(2)}) %collective-permute-start) | collective-permute-done | bytes 131104 | tf_op jit(solution)/shard_map/ppermute | solution.py:301
  7.8 1.5 %collective-permute-start.2 = (bf16[64,1024]{1,0:T(8,128)(2,1)}, bf16[64,1024]{1,0:T(8,128)(2,1)S(1)}, u32[]{:S(2)}, u32[]{:S(2)}) collective-permute-start(bf16[64,1024]{1,0:T(8,128)(2,1)} %get-tuple-element.29), channel_id=1, source_target_pairs={{0,24},{4,28},{8,16},{12,20},{16,8},{20,12},{24,0},{28,4},{1,25},{... | collective-permute-start | bytes 393224 | tf_op jit(solution)/shard_map/ppermute | solution.py:301
  9.3 1.6 %collective-permute-start.5 = (bf16[64,1024]{1,0:T(8,128)(2,1)S(1)}, bf16[64,1024]{1,0:T(8,128)(2,1)S(1)}, u32[]{:S(2)}, u32[]{:S(2)}) collective-permute-start(bf16[64,1024]{1,0:T(8,128)(2,1)S(1)} %collective-permute-done.4), channel_id=1, source_target_pairs={{0,8},{4,12},{8,0},{12,4},{16,24},{20,28},{24,16},{28,20},{1,9},{5... | collective-permute-start | bytes 393224 | tf_op jit(solution)/shard_map/ppermute | solution.py:301
  10.9 0.5 collective-permute-start.7
  11.4 1.5 %collective-permute-start.9 = (bf16[64,1024]{1,0:T(8,128)(2,1)S(1)}, bf16[64,1024]{1,0:T(8,128)(2,1)S(1)}, u32[]{:S(2)}, u32[]{:S(2)}) collective-permute-start(bf16[64,1024]{1,0:T(8,128)(2,1)S(1)} %collective-permute-done.8), channel_id=1, source_target_pairs={{0,24},{4,28},{8,16},{12,20},{16,8},{20,12},{24,0},{28,4},{1,25},{... | collective-permute-start | bytes 393224 | tf_op jit(solution)/shard_map/ppermute | solution.py:301
  12.9 2.5 %collective-permute-done.2.refs_3_ = bf16[64,1024]{1,0:T(8,128)(2,1)S(1)} collective-permute-done((bf16[64,1024]{1,0:T(8,128)(2,1)}, bf16[64,1024]{1,0:T(8,128)(2,1)S(1)}, u32[]{:S(2)}, u32[]{:S(2)}) %collective-permute-start.2) | collective-permute-done | bytes 131104 | tf_op jit(solution)/shard_map/ppermute | solution.py:301
  15.4 2.6 %collective-permute-done.5.refs_5_ = bf16[64,1024]{1,0:T(8,128)(2,1)S(1)} collective-permute-done((bf16[64,1024]{1,0:T(8,128)(2,1)S(1)}, bf16[64,1024]{1,0:T(8,128)(2,1)S(1)}, u32[]{:S(2)}, u32[]{:S(2)}) %collective-permute-start.5) | collective-permute-done | bytes 131104 | tf_op jit(solution)/shard_map/ppermute | solution.py:301
  18.1 2.0 %collective-permute-done.7.refs_6_ = bf16[64,1024]{1,0:T(8,128)(2,1)S(1)} collective-permute-done((bf16[64,1024]{1,0:T(8,128)(2,1)S(1)}, bf16[64,1024]{1,0:T(8,128)(2,1)S(1)}, u32[]{:S(2)}, u32[]{:S(2)}) %collective-permute-start.7) | collective-permute-done | bytes 131104 | tf_op jit(solution)/shard_map/ppermute | solution.py:301
  20.1 0.6 copy-done.12
  20.8 2.7 %pick.1 = (bf16[64,1024]{1,0:T(8,128)(2,1)}, bf16[64,1024]{1,0:T(8,128)(2,1)}, bf16[64,1024]{1,0:T(8,128)(2,1)}, bf16[64,1024]{1,0:T(8,128)(2,1)}) custom-call(s32[8]{0:T(128)} %order_ref.1, bf16[64,1024]{1,0:T(8,128)(2,1)} %get-tuple-element.26.refs_0_, bf16[64,1024]{1,0:T(8,128)(2,1)} %copy-done.7, bf16[64,1024]{1,0:T(8,128)(2,1)} %copy-done.8, ...), custom_call_target="tpu_custom_call" | custom-call | tf_op jit(solution)/shard_map/pick/pallas_call | solution.py:87
  23.7 1.1 collective-permute-start.11
  25.1 0.8 collective-permute-start.18
  25.9 1.9 %collective-permute-start.17 = (bf16[64,1024]{1,0:T(8,128)(2,1)}, bf16[64,1024]{1,0:T(8,128)(2,1)S(1)}, u32[]{:S(2)}, u32[]{:S(2)}) collective-permute-start(bf16[64,1024]{1,0:T(8,128)(2,1)} %get-tuple-element.35.refs_11_), channel_id=1, source_target_pairs={{0,8},{4,12},{8,0},{12,4},{16,24},{20,28},{24,16},{28,20},{1,9},{5... | collective-permute-start | bytes 393224 | tf_op jit(solution)/shard_map/ppermute | solution.py:301
  27.8 2.5 %collective-permute-done.11.refs_5_ = bf16[64,1024]{1,0:T(8,128)(2,1)S(1)} collective-permute-done((bf16[64,1024]{1,0:T(8,128)(2,1)}, bf16[64,1024]{1,0:T(8,128)(2,1)S(1)}, u32[]{:S(2)}, u32[]{:S(2)}) %collective-permute-start.11) | collective-permute-done | bytes 131104 | tf_op jit(solution)/shard_map/ppermute | solution.py:301
  30.3 1.0 collective-permute-done.10.refs_4_
  31.3 1.0 collective-permute-start.25
  32.6 0.7 collective-permute-done.17.refs_12_
  33.3 1.0 collective-permute-start.32
  34.3 1.2 %collective-permute-start.31 = (bf16[64,1024]{1,0:T(8,128)(2,1)}, bf16[64,1024]{1,0:T(8,128)(2,1)S(1)}, u32[]{:S(2)}, u32[]{:S(2)}) collective-permute-start(bf16[64,1024]{1,0:T(8,128)(2,1)} %get-tuple-element.38.refs_10_), channel_id=1, source_target_pairs={{0,8},{4,12},{8,0},{12,4},{16,24},{20,28},{24,16},{28,20},{1,9},{5... | collective-permute-start | bytes 393224 | tf_op jit(solution)/shard_map/ppermute | solution.py:301
  35.5 1.6 %collective-permute-done.25.refs_4_ = bf16[64,1024]{1,0:T(8,128)(2,1)S(1)} collective-permute-done((bf16[64,1024]{1,0:T(8,128)(2,1)}, bf16[64,1024]{1,0:T(8,128)(2,1)S(1)}, u32[]{:S(2)}, u32[]{:S(2)}) %collective-permute-start.25) | collective-permute-done | bytes 131104 | tf_op jit(solution)/shard_map/ppermute | solution.py:301
  37.1 1.2 %collective-permute-done.24.refs_3_ = bf16[64,1024]{1,0:T(8,128)(2,1)S(1)} collective-permute-done((bf16[64,1024]{1,0:T(8,128)(2,1)}, bf16[64,1024]{1,0:T(8,128)(2,1)S(1)}, u32[]{:S(2)}, u32[]{:S(2)}) %collective-permute-start.24) | collective-permute-done | bytes 131104 | tf_op jit(solution)/shard_map/ppermute | solution.py:301
  38.3 1.1 collective-permute-start.12
  39.6 0.7 collective-permute-done.31.refs_11_
  40.3 0.9 collective-permute-start.19
  41.3 0.5 collective-permute-start.29
  41.8 2.5 %collective-permute-done.12.refs_6_ = bf16[64,1024]{1,0:T(8,128)(2,1)S(1)} collective-permute-done((bf16[64,1024]{1,0:T(8,128)(2,1)S(1)}, bf16[64,1024]{1,0:T(8,128)(2,1)S(1)}, u32[]{:S(2)}, u32[]{:S(2)}) %collective-permute-start.12) | collective-permute-done | bytes 131104 | tf_op jit(solution)/shard_map/ppermute | solution.py:301
  44.2 1.0 collective-permute-start.26
  45.9 0.9 copy.7
  47.1 2.1 %collective-permute-done.26.refs_5_ = bf16[64,1024]{1,0:T(8,128)(2,1)S(1)} collective-permute-done((bf16[64,1024]{1,0:T(8,128)(2,1)S(1)}, bf16[64,1024]{1,0:T(8,128)(2,1)S(1)}, u32[]{:S(2)}, u32[]{:S(2)}) %collective-permute-start.26) | collective-permute-done | bytes 131104 | tf_op jit(solution)/shard_map/ppermute | solution.py:301
  49.2 1.0 collective-permute-done.33.refs_13_
  50.3 0.5 collective-permute-start.30
  51.4 6.3 %turns_0.1 = (bf16[256,2048]{1,0:T(8,128)(2,1)}, f32[136,256]{1,0:T(8,128)}, f32[136,256]{1,0:T(8,128)}, f32[136,256]{1,0:T(8,128)}, f32[136,256]{1,0:T(8,128)}) custom-call(bf16[256,2048]{1,0:T(8,128)(2,1)} %bitcast.8, bf16[256,1024]{1,0:T(8,128)(2,1)} %bitcast.6, s32[1,256]{1,0:T(1,128)} %refs_2_.1, bf16[64,1024]{1,0:T(8,128)(2,1)} %get-tuple-element.34.refs_3_, ...), custom_call_target="tpu_custom_call" | custom-call | flops 1610612736 | bytes 4194304 | tf_op jit(solution)/shard_map/turns_0/pallas_call | solution.py:180
  57.8 0.5 collective-permute-start.41
  58.3 2.6 %collective-permute-start.42 = (f32[136,256]{1,0:T(8,128)}, f32[136,256]{1,0:T(8,128)S(1)}, u32[]{:S(2)}, u32[]{:S(2)}) collective-permute-start(f32[136,256]{1,0:T(8,128)} %get-tuple-element.45), channel_id=1, source_target_pairs={{0,2},{1,3},{2,0},{3,1},{4,6},{5,7},{6,4},{7,5},{8,10},{9,11},{10,... | collective-permute-start | bytes 417800 | tf_op jit(solution)/shard_map/ppermute | solution.py:301
  61.6 0.5 copy-done.38
  62.1 5.7 %turns_2.1 = (f32[128,256]{1,0:T(8,128)}, f32[128,256]{1,0:T(8,128)}, f32[128,256]{1,0:T(8,128)}, f32[128,256]{1,0:T(8,128)}) custom-call(bf16[256,2048]{1,0:T(8,128)(2,1)} %get-tuple-element.36.refs_0_, bf16[256,1024]{1,0:T(8,128)(2,1)} %bitcast.7, bf16[64,1024]{1,0:T(8,128)(2,1)} %get-tuple-element.37.refs_2_, bf16[64,1024]{1,0:T(8,128)(2,1)} %copy-done.16, ...), custom_call_target="tpu_custom_call" | custom-call | flops 1610612736 | bytes 4194304 | tf_op jit(solution)/shard_map/turns_2/pallas_call | solution.py:180
  67.8 1.3 %collective-permute-start.38 = (f32[128,256]{1,0:T(8,128)}, f32[128,256]{1,0:T(8,128)S(1)}, u32[]{:S(2)}, u32[]{:S(2)}) collective-permute-start(f32[128,256]{1,0:T(8,128)} %get-tuple-element.40), channel_id=1, source_target_pairs={{0,1},{1,0},{2,3},{3,2},{4,5},{5,4},{6,7},{7,6},{8,9},{9,8},{10,11... | collective-permute-start | bytes 393224 | tf_op jit(solution)/shard_map/ppermute | solution.py:301
  69.2 2.3 %collective-permute-start.39 = (f32[128,256]{1,0:T(8,128)}, f32[128,256]{1,0:T(8,128)S(1)}, u32[]{:S(2)}, u32[]{:S(2)}) collective-permute-start(f32[128,256]{1,0:T(8,128)} %get-tuple-element.41), channel_id=1, source_target_pairs={{0,2},{1,3},{2,0},{3,1},{4,6},{5,7},{6,4},{7,5},{8,10},{9,11},{10,... | collective-permute-start | bytes 393224 | tf_op jit(solution)/shard_map/ppermute | solution.py:301
  71.5 0.6 collective-permute-start.40
  72.1 8.6 %collective-permute-done.43.refs_3_.refs_7_ = f32[136,256]{1,0:T(8,128)S(1)} collective-permute-done((f32[136,256]{1,0:T(8,128)}, f32[136,256]{1,0:T(8,128)S(1)}, u32[]{:S(2)}, u32[]{:S(2)}) %collective-permute-start.43) | collective-permute-done | bytes 139296 | tf_op jit(solution)/shard_map/ppermute | solution.py:301
  80.7 0.7 copy-done.3
  81.3 13.6 %maps_0.1.refs_8_ = f32[2048,128]{1,0:T(8,128)} custom-call(f32[136,256]{1,0:T(8,128)} %get-tuple-element.43.refs_0_.refs_4_, f32[136,256]{1,0:T(8,128)} %copy-done.1, f32[136,256]{1,0:T(8,128)} %copy-done.2, f32[136,256]{1,0:T(8,128)} %copy-done.3), custom_call_target="tpu_custom_call" | custom-call | flops 805306368 | bytes 1048576 | tf_op jit(solution)/shard_map/maps_0/pallas_call | solution.py:280
  95.0 0.6 copy-done.4
  95.7 13.8 %maps_2.1 = f32[2048,128]{1,0:T(8,128)} custom-call(f32[128,256]{1,0:T(8,128)} %get-tuple-element.39.refs_0_, f32[128,256]{1,0:T(8,128)} %copy-done.4, f32[128,256]{1,0:T(8,128)} %copy-done.5, f32[128,256]{1,0:T(8,128)} %copy-done.6, f32[136,256]{1,0:T(8,128)} %get-tuple-element.43.refs_0_.refs_4_, ...), custom_call_target="tpu_custom_call", output_to_operand_aliasing={{}: (8, {})} | custom-call | flops 805306368 | bytes 1048576 | tf_op jit(solution)/shard_map/maps_2/pallas_call | solution.py:280
  (131 shorter events, 3.3 us)
Async XLA Ops:
  2.3 5.5 %collective-permute-start = (bf16[64,1024]{1,0:T(8,128)(2,1)}, bf16[64,1024]{1,0:T(8,128)(2,1)S(1)}, u32[]{:S(2)}, u32[]{:S(2)}) collective-permute-start(bf16[64,1024]{1,0:T(8,128)(2,1)} %get-tuple-element.27), channel_id=1, source_target_pairs={{0,8},{4,12},{8,0},{12,4},{16,24},{20,28},{24,16},{28,20},{1,9},{5... | collective-permute-start | bytes 393224 | tf_op jit(solution)/shard_map/ppermute | solution.py:301
  2.9 6.4 %collective-permute-start.1 = (bf16[64,1024]{1,0:T(8,128)(2,1)}, bf16[64,1024]{1,0:T(8,128)(2,1)S(1)}, u32[]{:S(2)}, u32[]{:S(2)}) collective-permute-start(bf16[64,1024]{1,0:T(8,128)(2,1)} %get-tuple-element.28), channel_id=1, source_target_pairs={{0,16},{4,20},{8,24},{12,28},{16,0},{20,4},{24,8},{28,12},{1,17},{... | collective-permute-start | bytes 393224 | tf_op jit(solution)/shard_map/ppermute | solution.py:301
  4.4 4.9 %collective-permute-start.4 = (bf16[64,1024]{1,0:T(8,128)(2,1)}, bf16[64,1024]{1,0:T(8,128)(2,1)S(1)}, u32[]{:S(2)}, u32[]{:S(2)}) collective-permute-start(bf16[64,1024]{1,0:T(8,128)(2,1)} %get-tuple-element.31), channel_id=1, source_target_pairs={{0,4},{4,0},{8,12},{12,8},{16,20},{20,16},{24,28},{28,24},{1,5},{5... | collective-permute-start | bytes 393224 | tf_op jit(solution)/shard_map/ppermute | solution.py:301
  4.4 6.5 %collective-permute-start.6 = (bf16[64,1024]{1,0:T(8,128)(2,1)}, bf16[64,1024]{1,0:T(8,128)(2,1)S(1)}, u32[]{:S(2)}, u32[]{:S(2)}) collective-permute-start(bf16[64,1024]{1,0:T(8,128)(2,1)} %get-tuple-element.32), channel_id=1, source_target_pairs={{0,4},{4,0},{8,12},{12,8},{16,20},{20,16},{24,28},{28,24},{1,5},{5... | collective-permute-start | bytes 393224 | tf_op jit(solution)/shard_map/ppermute | solution.py:301
  4.9 6.5 %collective-permute-start.8 = (bf16[64,1024]{1,0:T(8,128)(2,1)}, bf16[64,1024]{1,0:T(8,128)(2,1)S(1)}, u32[]{:S(2)}, u32[]{:S(2)}) collective-permute-start(bf16[64,1024]{1,0:T(8,128)(2,1)} %get-tuple-element.33), channel_id=1, source_target_pairs={{0,4},{4,0},{8,12},{12,8},{16,20},{20,16},{24,28},{28,24},{1,5},{5... | collective-permute-start | bytes 393224 | tf_op jit(solution)/shard_map/ppermute | solution.py:301
  7.8 7.6 %collective-permute-start.2 = (bf16[64,1024]{1,0:T(8,128)(2,1)}, bf16[64,1024]{1,0:T(8,128)(2,1)S(1)}, u32[]{:S(2)}, u32[]{:S(2)}) collective-permute-start(bf16[64,1024]{1,0:T(8,128)(2,1)} %get-tuple-element.29), channel_id=1, source_target_pairs={{0,24},{4,28},{8,16},{12,20},{16,8},{20,12},{24,0},{28,4},{1,25},{... | collective-permute-start | bytes 393224 | tf_op jit(solution)/shard_map/ppermute | solution.py:301
  9.3 6.1 %collective-permute-start.3 = (bf16[64,1024]{1,0:T(8,128)(2,1)}, bf16[64,1024]{1,0:T(8,128)(2,1)S(1)}, u32[]{:S(2)}, u32[]{:S(2)}) collective-permute-start(bf16[64,1024]{1,0:T(8,128)(2,1)} %get-tuple-element.30), channel_id=1, source_target_pairs={{0,4},{4,0},{8,12},{12,8},{16,20},{20,16},{24,28},{28,24},{1,5},{5... | collective-permute-start | bytes 393224 | tf_op jit(solution)/shard_map/ppermute | solution.py:301
  9.3 8.7 %collective-permute-start.5 = (bf16[64,1024]{1,0:T(8,128)(2,1)S(1)}, bf16[64,1024]{1,0:T(8,128)(2,1)S(1)}, u32[]{:S(2)}, u32[]{:S(2)}) collective-permute-start(bf16[64,1024]{1,0:T(8,128)(2,1)S(1)} %collective-permute-done.4), channel_id=1, source_target_pairs={{0,8},{4,12},{8,0},{12,4},{16,24},{20,28},{24,16},{28,20},{1,9},{5... | collective-permute-start | bytes 393224 | tf_op jit(solution)/shard_map/ppermute | solution.py:301
  10.9 9.2 %collective-permute-start.7 = (bf16[64,1024]{1,0:T(8,128)(2,1)S(1)}, bf16[64,1024]{1,0:T(8,128)(2,1)S(1)}, u32[]{:S(2)}, u32[]{:S(2)}) collective-permute-start(bf16[64,1024]{1,0:T(8,128)(2,1)S(1)} %collective-permute-done.6), channel_id=1, source_target_pairs={{0,16},{4,20},{8,24},{12,28},{16,0},{20,4},{24,8},{28,12},{1,17},{... | collective-permute-start | bytes 393224 | tf_op jit(solution)/shard_map/ppermute | solution.py:301
  11.4 8.7 %collective-permute-start.9 = (bf16[64,1024]{1,0:T(8,128)(2,1)S(1)}, bf16[64,1024]{1,0:T(8,128)(2,1)S(1)}, u32[]{:S(2)}, u32[]{:S(2)}) collective-permute-start(bf16[64,1024]{1,0:T(8,128)(2,1)S(1)} %collective-permute-done.8), channel_id=1, source_target_pairs={{0,24},{4,28},{8,16},{12,20},{16,8},{20,12},{24,0},{28,4},{1,25},{... | collective-permute-start | bytes 393224 | tf_op jit(solution)/shard_map/ppermute | solution.py:301
  20.8 25.1 %copy-start = (bf16[1,256,4,256]{3,2,1,0:T(4,128)(2,1)S(1)}, bf16[1,256,4,256]{3,2,1,0:T(4,128)(2,1)}, u32[]{:S(2)}) copy-start(bf16[1,256,4,256]{3,2,1,0:T(4,128)(2,1)} %param.6) | copy-start | bytes 1572868
  23.6 2.3 %collective-permute-start.13 = (bf16[64,1024]{1,0:T(8,128)(2,1)}, bf16[64,1024]{1,0:T(8,128)(2,1)S(1)}, u32[]{:S(2)}, u32[]{:S(2)}) collective-permute-start(bf16[64,1024]{1,0:T(8,128)(2,1)} %get-tuple-element.34.refs_3_), channel_id=1, source_target_pairs={{0,4},{4,0},{8,12},{12,8},{16,20},{20,16},{24,28},{28,24},{1,5},{5... | collective-permute-start | bytes 393224 | tf_op jit(solution)/shard_map/ppermute | solution.py:301
  23.7 6.6 %collective-permute-start.11 = (bf16[64,1024]{1,0:T(8,128)(2,1)}, bf16[64,1024]{1,0:T(8,128)(2,1)S(1)}, u32[]{:S(2)}, u32[]{:S(2)}) collective-permute-start(bf16[64,1024]{1,0:T(8,128)(2,1)} %get-tuple-element.34.refs_3_), channel_id=1, source_target_pairs={{0,16},{4,20},{8,24},{12,28},{16,0},{20,4},{24,8},{28,12},{1,17},{... | collective-permute-start | bytes 393224 | tf_op jit(solution)/shard_map/ppermute | solution.py:301
  24.7 6.6 %collective-permute-start.10 = (bf16[64,1024]{1,0:T(8,128)(2,1)}, bf16[64,1024]{1,0:T(8,128)(2,1)S(1)}, u32[]{:S(2)}, u32[]{:S(2)}) collective-permute-start(bf16[64,1024]{1,0:T(8,128)(2,1)} %get-tuple-element.34.refs_3_), channel_id=1, source_target_pairs={{0,8},{4,12},{8,0},{12,4},{16,24},{20,28},{24,16},{28,20},{1,9},{5... | collective-permute-start | bytes 393224 | tf_op jit(solution)/shard_map/ppermute | solution.py:301
  25.1 7.2 %collective-permute-start.20 = (bf16[64,1024]{1,0:T(8,128)(2,1)}, bf16[64,1024]{1,0:T(8,128)(2,1)S(1)}, u32[]{:S(2)}, u32[]{:S(2)}) collective-permute-start(bf16[64,1024]{1,0:T(8,128)(2,1)} %get-tuple-element.35.refs_11_), channel_id=1, source_target_pairs={{0,4},{4,0},{8,12},{12,8},{16,20},{20,16},{24,28},{28,24},{1,5},{5... | collective-permute-start | bytes 393224 | tf_op jit(solution)/shard_map/ppermute | solution.py:301
  25.1 7.4 %collective-permute-start.18 = (bf16[64,1024]{1,0:T(8,128)(2,1)}, bf16[64,1024]{1,0:T(8,128)(2,1)S(1)}, u32[]{:S(2)}, u32[]{:S(2)}) collective-permute-start(bf16[64,1024]{1,0:T(8,128)(2,1)} %get-tuple-element.35.refs_11_), channel_id=1, source_target_pairs={{0,16},{4,20},{8,24},{12,28},{16,0},{20,4},{24,8},{28,12},{1,17},{... | collective-permute-start | bytes 393224 | tf_op jit(solution)/shard_map/ppermute | solution.py:301
  25.9 20.9 %copy-start.17 = (bf16[64,1024]{1,0:T(8,128)(2,1)}, bf16[64,1024]{1,0:T(8,128)(2,1)S(1)}, u32[]{:S(2)}) copy-start(bf16[64,1024]{1,0:T(8,128)(2,1)S(1)} %collective-permute-done.13.refs_7_) | copy-start | bytes 393220
  25.9 7.4 %collective-permute-start.17 = (bf16[64,1024]{1,0:T(8,128)(2,1)}, bf16[64,1024]{1,0:T(8,128)(2,1)S(1)}, u32[]{:S(2)}, u32[]{:S(2)}) collective-permute-start(bf16[64,1024]{1,0:T(8,128)(2,1)} %get-tuple-element.35.refs_11_), channel_id=1, source_target_pairs={{0,8},{4,12},{8,0},{12,4},{16,24},{20,28},{24,16},{28,20},{1,9},{5... | collective-permute-start | bytes 393224 | tf_op jit(solution)/shard_map/ppermute | solution.py:301
  30.3 16.5 %copy-start.19 = (bf16[64,1024]{1,0:T(8,128)(2,1)}, bf16[64,1024]{1,0:T(8,128)(2,1)S(1)}, u32[]{:S(2)}) copy-start(bf16[64,1024]{1,0:T(8,128)(2,1)S(1)} %collective-permute-done.11.refs_5_) | copy-start | bytes 393220
  30.3 4.0 %collective-permute-start.27 = (bf16[64,1024]{1,0:T(8,128)(2,1)}, bf16[64,1024]{1,0:T(8,128)(2,1)S(1)}, u32[]{:S(2)}, u32[]{:S(2)}) collective-permute-start(bf16[64,1024]{1,0:T(8,128)(2,1)} %get-tuple-element.37.refs_2_), channel_id=1, source_target_pairs={{0,4},{4,0},{8,12},{12,8},{16,20},{20,16},{24,28},{28,24},{1,5},{5... | collective-permute-start | bytes 393224 | tf_op jit(solution)/shard_map/ppermute | solution.py:301
  31.3 15.5 %copy-start.20 = (bf16[64,1024]{1,0:T(8,128)(2,1)}, bf16[64,1024]{1,0:T(8,128)(2,1)S(1)}, u32[]{:S(2)}) copy-start(bf16[64,1024]{1,0:T(8,128)(2,1)S(1)} %collective-permute-done.10.refs_4_) | copy-start | bytes 393220
  31.3 5.8 %collective-permute-start.25 = (bf16[64,1024]{1,0:T(8,128)(2,1)}, bf16[64,1024]{1,0:T(8,128)(2,1)S(1)}, u32[]{:S(2)}, u32[]{:S(2)}) collective-permute-start(bf16[64,1024]{1,0:T(8,128)(2,1)} %get-tuple-element.37.refs_2_), channel_id=1, source_target_pairs={{0,16},{4,20},{8,24},{12,28},{16,0},{20,4},{24,8},{28,12},{1,17},{... | collective-permute-start | bytes 393224 | tf_op jit(solution)/shard_map/ppermute | solution.py:301
  32.3 6.0 %collective-permute-start.24 = (bf16[64,1024]{1,0:T(8,128)(2,1)}, bf16[64,1024]{1,0:T(8,128)(2,1)S(1)}, u32[]{:S(2)}, u32[]{:S(2)}) collective-permute-start(bf16[64,1024]{1,0:T(8,128)(2,1)} %get-tuple-element.37.refs_2_), channel_id=1, source_target_pairs={{0,8},{4,12},{8,0},{12,4},{16,24},{20,28},{24,16},{28,20},{1,9},{5... | collective-permute-start | bytes 393224 | tf_op jit(solution)/shard_map/ppermute | solution.py:301
  32.6 5.7 %collective-permute-start.34 = (bf16[64,1024]{1,0:T(8,128)(2,1)}, bf16[64,1024]{1,0:T(8,128)(2,1)S(1)}, u32[]{:S(2)}, u32[]{:S(2)}) collective-permute-start(bf16[64,1024]{1,0:T(8,128)(2,1)} %get-tuple-element.38.refs_10_), channel_id=1, source_target_pairs={{0,4},{4,0},{8,12},{12,8},{16,20},{20,16},{24,28},{28,24},{1,5},{5... | collective-permute-start | bytes 393224 | tf_op jit(solution)/shard_map/ppermute | solution.py:301
  33.3 6.1 %collective-permute-start.32 = (bf16[64,1024]{1,0:T(8,128)(2,1)}, bf16[64,1024]{1,0:T(8,128)(2,1)S(1)}, u32[]{:S(2)}, u32[]{:S(2)}) collective-permute-start(bf16[64,1024]{1,0:T(8,128)(2,1)} %get-tuple-element.38.refs_10_), channel_id=1, source_target_pairs={{0,16},{4,20},{8,24},{12,28},{16,0},{20,4},{24,8},{28,12},{1,17},{... | collective-permute-start | bytes 393224 | tf_op jit(solution)/shard_map/ppermute | solution.py:301
  34.3 6.0 %collective-permute-start.31 = (bf16[64,1024]{1,0:T(8,128)(2,1)}, bf16[64,1024]{1,0:T(8,128)(2,1)S(1)}, u32[]{:S(2)}, u32[]{:S(2)}) collective-permute-start(bf16[64,1024]{1,0:T(8,128)(2,1)} %get-tuple-element.38.refs_10_), channel_id=1, source_target_pairs={{0,8},{4,12},{8,0},{12,4},{16,24},{20,28},{24,16},{28,20},{1,9},{5... | collective-permute-start | bytes 393224 | tf_op jit(solution)/shard_map/ppermute | solution.py:301
  37.1 4.1 %collective-permute-start.15 = (bf16[64,1024]{1,0:T(8,128)(2,1)S(1)}, bf16[64,1024]{1,0:T(8,128)(2,1)S(1)}, u32[]{:S(2)}, u32[]{:S(2)}) collective-permute-start(bf16[64,1024]{1,0:T(8,128)(2,1)S(1)} %collective-permute-done.11.refs_5_), channel_id=1, source_target_pairs={{0,4},{4,0},{8,12},{12,8},{16,20},{20,16},{24,28},{28,24},{1,5},{5... | collective-permute-start | bytes 393224 | tf_op jit(solution)/shard_map/ppermute | solution.py:301
  38.3 2.9 %collective-permute-start.14 = (bf16[64,1024]{1,0:T(8,128)(2,1)S(1)}, bf16[64,1024]{1,0:T(8,128)(2,1)S(1)}, u32[]{:S(2)}, u32[]{:S(2)}) collective-permute-start(bf16[64,1024]{1,0:T(8,128)(2,1)S(1)} %collective-permute-done.10.refs_4_), channel_id=1, source_target_pairs={{0,4},{4,0},{8,12},{12,8},{16,20},{20,16},{24,28},{28,24},{1,5},{5... | collective-permute-start | bytes 393224 | tf_op jit(solution)/shard_map/ppermute | solution.py:301
  38.3 5.9 %collective-permute-start.12 = (bf16[64,1024]{1,0:T(8,128)(2,1)S(1)}, bf16[64,1024]{1,0:T(8,128)(2,1)S(1)}, u32[]{:S(2)}, u32[]{:S(2)}) collective-permute-start(bf16[64,1024]{1,0:T(8,128)(2,1)S(1)} %collective-permute-done.10.refs_4_), channel_id=1, source_target_pairs={{0,16},{4,20},{8,24},{12,28},{16,0},{20,4},{24,8},{28,12},{1,17},{... | collective-permute-start | bytes 393224 | tf_op jit(solution)/shard_map/ppermute | solution.py:301
  39.4 5.8 %collective-permute-start.22 = (bf16[64,1024]{1,0:T(8,128)(2,1)S(1)}, bf16[64,1024]{1,0:T(8,128)(2,1)S(1)}, u32[]{:S(2)}, u32[]{:S(2)}) collective-permute-start(bf16[64,1024]{1,0:T(8,128)(2,1)S(1)} %collective-permute-done.18.refs_13_), channel_id=1, source_target_pairs={{0,4},{4,0},{8,12},{12,8},{16,20},{20,16},{24,28},{28,24},{1,5},{5... | collective-permute-start | bytes 393224 | tf_op jit(solution)/shard_map/ppermute | solution.py:301
  40.3 5.0 %collective-permute-start.19 = (bf16[64,1024]{1,0:T(8,128)(2,1)S(1)}, bf16[64,1024]{1,0:T(8,128)(2,1)S(1)}, u32[]{:S(2)}, u32[]{:S(2)}) collective-permute-start(bf16[64,1024]{1,0:T(8,128)(2,1)S(1)} %collective-permute-done.18.refs_13_), channel_id=1, source_target_pairs={{0,8},{4,12},{8,0},{12,4},{16,24},{20,28},{24,16},{28,20},{1,9},{5... | collective-permute-start | bytes 393224 | tf_op jit(solution)/shard_map/ppermute | solution.py:301
  41.3 4.1 %collective-permute-start.21 = (bf16[64,1024]{1,0:T(8,128)(2,1)S(1)}, bf16[64,1024]{1,0:T(8,128)(2,1)S(1)}, u32[]{:S(2)}, u32[]{:S(2)}) collective-permute-start(bf16[64,1024]{1,0:T(8,128)(2,1)S(1)} %collective-permute-done.17.refs_12_), channel_id=1, source_target_pairs={{0,4},{4,0},{8,12},{12,8},{16,20},{20,16},{24,28},{28,24},{1,5},{5... | collective-permute-start | bytes 393224 | tf_op jit(solution)/shard_map/ppermute | solution.py:301
  41.3 5.6 %collective-permute-start.29 = (bf16[64,1024]{1,0:T(8,128)(2,1)S(1)}, bf16[64,1024]{1,0:T(8,128)(2,1)S(1)}, u32[]{:S(2)}, u32[]{:S(2)}) collective-permute-start(bf16[64,1024]{1,0:T(8,128)(2,1)S(1)} %collective-permute-done.25.refs_4_), channel_id=1, source_target_pairs={{0,4},{4,0},{8,12},{12,8},{16,20},{20,16},{24,28},{28,24},{1,5},{5... | collective-permute-start | bytes 393224 | tf_op jit(solution)/shard_map/ppermute | solution.py:301
  44.2 5.0 %collective-permute-start.26 = (bf16[64,1024]{1,0:T(8,128)(2,1)S(1)}, bf16[64,1024]{1,0:T(8,128)(2,1)S(1)}, u32[]{:S(2)}, u32[]{:S(2)}) collective-permute-start(bf16[64,1024]{1,0:T(8,128)(2,1)S(1)} %collective-permute-done.24.refs_3_), channel_id=1, source_target_pairs={{0,16},{4,20},{8,24},{12,28},{16,0},{20,4},{24,8},{28,12},{1,17},{... | collective-permute-start | bytes 393224 | tf_op jit(solution)/shard_map/ppermute | solution.py:301
  45.3 5.0 %collective-permute-start.33 = (bf16[64,1024]{1,0:T(8,128)(2,1)S(1)}, bf16[64,1024]{1,0:T(8,128)(2,1)S(1)}, u32[]{:S(2)}, u32[]{:S(2)}) collective-permute-start(bf16[64,1024]{1,0:T(8,128)(2,1)S(1)} %collective-permute-done.32.refs_12_), channel_id=1, source_target_pairs={{0,8},{4,12},{8,0},{12,4},{16,24},{20,28},{24,16},{28,20},{1,9},{5... | collective-permute-start | bytes 393224 | tf_op jit(solution)/shard_map/ppermute | solution.py:301
  45.4 4.9 %collective-permute-start.16 = (bf16[64,1024]{1,0:T(8,128)(2,1)S(1)}, bf16[64,1024]{1,0:T(8,128)(2,1)S(1)}, u32[]{:S(2)}, u32[]{:S(2)}) collective-permute-start(bf16[64,1024]{1,0:T(8,128)(2,1)S(1)} %collective-permute-done.12.refs_6_), channel_id=1, source_target_pairs={{0,4},{4,0},{8,12},{12,8},{16,20},{20,16},{24,28},{28,24},{1,5},{5... | collective-permute-start | bytes 393224 | tf_op jit(solution)/shard_map/ppermute | solution.py:301
  45.4 5.4 %collective-permute-start.23 = (bf16[64,1024]{1,0:T(8,128)(2,1)S(1)}, bf16[64,1024]{1,0:T(8,128)(2,1)S(1)}, u32[]{:S(2)}, u32[]{:S(2)}) collective-permute-start(bf16[64,1024]{1,0:T(8,128)(2,1)S(1)} %collective-permute-done.19.refs_14_), channel_id=1, source_target_pairs={{0,4},{4,0},{8,12},{12,8},{16,20},{20,16},{24,28},{28,24},{1,5},{5... | collective-permute-start | bytes 393224 | tf_op jit(solution)/shard_map/ppermute | solution.py:301
  46.9 10.9 %collective-permute-start.28 = (bf16[64,1024]{1,0:T(8,128)(2,1)S(1)}, bf16[64,1024]{1,0:T(8,128)(2,1)S(1)}, u32[]{:S(2)}, u32[]{:S(2)}) collective-permute-start(bf16[64,1024]{1,0:T(8,128)(2,1)S(1)} %collective-permute-done.24.refs_3_), channel_id=1, source_target_pairs={{0,4},{4,0},{8,12},{12,8},{16,20},{20,16},{24,28},{28,24},{1,5},{5... | collective-permute-start | bytes 393224 | tf_op jit(solution)/shard_map/ppermute | solution.py:301
  49.2 9.1 %collective-permute-start.36 = (bf16[64,1024]{1,0:T(8,128)(2,1)S(1)}, bf16[64,1024]{1,0:T(8,128)(2,1)S(1)}, u32[]{:S(2)}, u32[]{:S(2)}) collective-permute-start(bf16[64,1024]{1,0:T(8,128)(2,1)S(1)} %collective-permute-done.32.refs_12_), channel_id=1, source_target_pairs={{0,4},{4,0},{8,12},{12,8},{16,20},{20,16},{24,28},{28,24},{1,5},{5... | collective-permute-start | bytes 393224 | tf_op jit(solution)/shard_map/ppermute | solution.py:301
  50.2 10.7 %collective-permute-start.35 = (bf16[64,1024]{1,0:T(8,128)(2,1)S(1)}, bf16[64,1024]{1,0:T(8,128)(2,1)S(1)}, u32[]{:S(2)}, u32[]{:S(2)}) collective-permute-start(bf16[64,1024]{1,0:T(8,128)(2,1)S(1)} %collective-permute-done.31.refs_11_), channel_id=1, source_target_pairs={{0,4},{4,0},{8,12},{12,8},{16,20},{20,16},{24,28},{28,24},{1,5},{5... | collective-permute-start | bytes 393224 | tf_op jit(solution)/shard_map/ppermute | solution.py:301
  50.3 11.1 %collective-permute-start.30 = (bf16[64,1024]{1,0:T(8,128)(2,1)S(1)}, bf16[64,1024]{1,0:T(8,128)(2,1)S(1)}, u32[]{:S(2)}, u32[]{:S(2)}) collective-permute-start(bf16[64,1024]{1,0:T(8,128)(2,1)S(1)} %collective-permute-done.26.refs_5_), channel_id=1, source_target_pairs={{0,4},{4,0},{8,12},{12,8},{16,20},{20,16},{24,28},{28,24},{1,5},{5... | collective-permute-start | bytes 393224 | tf_op jit(solution)/shard_map/ppermute | solution.py:301
  50.8 10.6 %collective-permute-start.37 = (bf16[64,1024]{1,0:T(8,128)(2,1)S(1)}, bf16[64,1024]{1,0:T(8,128)(2,1)S(1)}, u32[]{:S(2)}, u32[]{:S(2)}) collective-permute-start(bf16[64,1024]{1,0:T(8,128)(2,1)S(1)} %collective-permute-done.33.refs_13_), channel_id=1, source_target_pairs={{0,4},{4,0},{8,12},{12,8},{16,20},{20,16},{24,28},{28,24},{1,5},{5... | collective-permute-start | bytes 393224 | tf_op jit(solution)/shard_map/ppermute | solution.py:301
  57.8 13.7 %collective-permute-start.41 = (f32[136,256]{1,0:T(8,128)}, f32[136,256]{1,0:T(8,128)S(1)}, u32[]{:S(2)}, u32[]{:S(2)}) collective-permute-start(f32[136,256]{1,0:T(8,128)} %get-tuple-element.44), channel_id=1, source_target_pairs={{0,1},{1,0},{2,3},{3,2},{4,5},{5,4},{6,7},{7,6},{8,9},{9,8},{10,11... | collective-permute-start | bytes 417800 | tf_op jit(solution)/shard_map/ppermute | solution.py:301
  58.3 13.8 %collective-permute-start.42 = (f32[136,256]{1,0:T(8,128)}, f32[136,256]{1,0:T(8,128)S(1)}, u32[]{:S(2)}, u32[]{:S(2)}) collective-permute-start(f32[136,256]{1,0:T(8,128)} %get-tuple-element.45), channel_id=1, source_target_pairs={{0,2},{1,3},{2,0},{3,1},{4,6},{5,7},{6,4},{7,5},{8,10},{9,11},{10,... | collective-permute-start | bytes 417800 | tf_op jit(solution)/shard_map/ppermute | solution.py:301
  60.9 19.8 %collective-permute-start.43 = (f32[136,256]{1,0:T(8,128)}, f32[136,256]{1,0:T(8,128)S(1)}, u32[]{:S(2)}, u32[]{:S(2)}) collective-permute-start(f32[136,256]{1,0:T(8,128)} %get-tuple-element.46), channel_id=1, source_target_pairs={{0,3},{1,2},{2,1},{3,0},{4,7},{5,6},{6,5},{7,4},{8,11},{9,10},{10,... | collective-permute-start | bytes 417800 | tf_op jit(solution)/shard_map/ppermute | solution.py:301
  67.8 27.1 %collective-permute-start.38 = (f32[128,256]{1,0:T(8,128)}, f32[128,256]{1,0:T(8,128)S(1)}, u32[]{:S(2)}, u32[]{:S(2)}) collective-permute-start(f32[128,256]{1,0:T(8,128)} %get-tuple-element.40), channel_id=1, source_target_pairs={{0,1},{1,0},{2,3},{3,2},{4,5},{5,4},{6,7},{7,6},{8,9},{9,8},{10,11... | collective-permute-start | bytes 393224 | tf_op jit(solution)/shard_map/ppermute | solution.py:301
  69.2 25.8 %collective-permute-start.39 = (f32[128,256]{1,0:T(8,128)}, f32[128,256]{1,0:T(8,128)S(1)}, u32[]{:S(2)}, u32[]{:S(2)}) collective-permute-start(f32[128,256]{1,0:T(8,128)} %get-tuple-element.41), channel_id=1, source_target_pairs={{0,2},{1,3},{2,0},{3,1},{4,6},{5,7},{6,4},{7,5},{8,10},{9,11},{10,... | collective-permute-start | bytes 393224 | tf_op jit(solution)/shard_map/ppermute | solution.py:301
  71.5 23.5 %collective-permute-start.40 = (f32[128,256]{1,0:T(8,128)}, f32[128,256]{1,0:T(8,128)S(1)}, u32[]{:S(2)}, u32[]{:S(2)}) collective-permute-start(f32[128,256]{1,0:T(8,128)} %get-tuple-element.42), channel_id=1, source_target_pairs={{0,3},{1,2},{2,1},{3,0},{4,7},{5,6},{6,5},{7,4},{8,11},{9,10},{10,... | collective-permute-start | bytes 393224 | tf_op jit(solution)/shard_map/ppermute | solution.py:301
  (38 other events, 213.2 us)

commit v2 on v1

v2 whole, which is shorter than its diff:
```python
import functools

import jax
import jax.numpy as jnp
from jax import lax
from jax.experimental import pallas as pl
from jax.experimental.pallas import tpu as pltpu
from jax.sharding import PartitionSpec as P


TURNS = 4
SWEEPS = 4
MAP_W = 128
SUBLANES = 8
UNROLL = 4
TILE_ROWS = 16
GRANT = 16 * 1024 * 1024


time_step = 0.2

GROUPS = ((0, 1), (2, 3))

ANY = pl.BlockSpec(memory_space=pl.ANY)
VMEM = pl.BlockSpec(memory_space=pltpu.VMEM)
SMEM = pl.BlockSpec(memory_space=pltpu.SMEM)


def place_of_device():
    index = lax.axis_index("field")
    return index // 2, index % 2


def slice_kernel(chips, block_ref, *refs):
    keep, give, sems = refs[:chips], refs[chips : 2 * chips], refs[2 * chips]
    chip, core = place_of_device()
    rows, half = keep[0].shape
    copies = []
    for k in range(chips):
        top = pl.multiple_of((chip ^ k) * rows, rows)
        for number, (out, which) in enumerate(((give[k], 1 - core), (keep[k], core))):
            left = pl.multiple_of(which * half, half)
            copy = pltpu.make_async_copy(
                block_ref.at[pl.ds(top, rows), pl.ds(left, half)], out, sems.at[2 * k + number]
            )
            copy.start()
            copies.append(copy)
    for copy in copies:
        copy.wait()


def cut_block(block, chips):
    kb, features = block.shape
    piece = jax.ShapeDtypeStruct((kb // chips, features // 2), block.dtype)
    outs = pl.pallas_call(
        functools.partial(slice_kernel, chips),
        out_shape=[piece] * (2 * chips),
        in_specs=[ANY],
        out_specs=[VMEM] * (2 * chips),
        scratch_shapes=[pltpu.SemaphoreType.DMA((2 * chips,))],
        compiler_params=pltpu.CompilerParams(vmem_limit_bytes=GRANT),
        name="cut",
    )(block)
    return outs[:chips], outs[chips:]


def pick_kernel(chips, order_ref, *refs):
    same, other = refs[:chips], refs[chips : 2 * chips]
    outs, sems = refs[2 * chips : 2 * chips + TURNS], refs[2 * chips + TURNS]
    chip, core = place_of_device()
    for turn in range(TURNS):
        owner = order_ref[turn]
        distance = (owner // 2) ^ chip
        mine = owner % 2 == core
        for k in range(chips):

            @pl.when((distance == k) & mine)
            def _():
                pltpu.make_async_copy(same[k], outs[turn], sems.at[turn]).start()

            @pl.when((distance == k) & jnp.logical_not(mine))
            def _():
                pltpu.make_async_copy(other[k], outs[turn], sems.at[turn]).start()

    for turn in range(TURNS):
        pltpu.make_async_copy(same[0], outs[turn], sems.at[turn]).wait()


def pick_turns(owner_order, same, other):
    chips = len(same)
    piece = jax.ShapeDtypeStruct(same[0].shape, same[0].dtype)
    return pl.pallas_call(
        functools.partial(pick_kernel, chips),
        out_shape=[piece] * TURNS,
        in_specs=[SMEM] + [ANY] * (2 * chips),
        out_specs=[VMEM] * TURNS,
        scratch_shapes=[pltpu.SemaphoreType.DMA((TURNS,))],
        compiler_params=pltpu.CompilerParams(vmem_limit_bytes=GRANT),
        name="pick",
    )(owner_order, *same, *other)


def lay_kernel(parts, coefs_ref, pixel_ref, *refs):
    sends, turned = refs[:parts], refs[parts]
    slot = lax.axis_index("point")
    height, points = sends[0].shape
    local_kb = (height - TILE_ROWS) // TURNS
    turned[...] = coefs_ref[...].astype(jnp.float32).T.astype(jnp.bfloat16)
    pixel = pixel_ref[...]
    half = TILE_ROWS // 2
    row = jnp.broadcast_to((pixel // MAP_W).astype(jnp.float32), (half, points))
    lane = jnp.broadcast_to((pixel % MAP_W).astype(jnp.float32), (half, points))
    both = jnp.concatenate([row, lane], axis=0).astype(jnp.bfloat16)
    for m in range(parts):
        for turn in range(TURNS):
            top = pl.multiple_of((turn * parts + (slot ^ m)) * local_kb, local_kb)
            sends[m][turn * local_kb : (turn + 1) * local_kb, :] = turned[pl.ds(top, local_kb), :]
        sends[m][TURNS * local_kb :, :] = both


def lay_coefs(coefs, pixels, parts):
    points, width = coefs.shape
    send = jax.ShapeDtypeStruct((width // parts + TILE_ROWS, points), jnp.bfloat16)
    outs = pl.pallas_call(
        functools.partial(lay_kernel, parts),
        out_shape=[send] * parts + [jax.ShapeDtypeStruct((width, points), jnp.bfloat16)],
        in_specs=[VMEM, VMEM],
        out_specs=[VMEM] * (parts + 1),
        compiler_params=pltpu.CompilerParams(vmem_limit_bytes=GRANT),
        name="lay",
    )(coefs, pixels)
    return outs[:parts], outs[parts]


def turn_kernel(turns, chips, parts, last, *refs):
    count = len(turns)
    refs = list(refs)
    residual_ref, coefs_ref = refs.pop(0), refs.pop(0)
    pieces = [[refs.pop(0) for _ in range(2 * chips)] for _ in turns]
    residual_out = None if last else refs.pop(0)
    sends = [refs.pop(0) for _ in range(parts)]
    values, held = refs

    chip, core = place_of_device()
    slot = lax.axis_index("point")
    rows, half = pieces[0][0].shape
    kb = rows * chips
    local_kb = kb // parts
    sides = [pl.ds(pl.multiple_of(which * half, half), half) for which in (core, 1 - core)]
    tops = [pl.multiple_of((chip ^ k) * rows, rows) for k in range(chips)]

    source = residual_ref
    for position, turn in enumerate(turns):
        halves = [
            jnp.concatenate([piece[...] for piece in pieces[position][side * chips : (side + 1) * chips]], axis=0)
            for side in range(2)
        ]
        across = lambda left, right: lax.dot_general(
            left, right, (((1,), (1,)), ((), ())), preferred_element_type=jnp.float32
        )
        gram = across(halves[0], halves[0]) + across(halves[1], halves[1])
        step = 1.0 / jnp.sum(jnp.abs(gram), axis=1, keepdims=True)
        correlation = across(halves[0], source[:, sides[0]]) + across(halves[1], source[:, sides[1]])
        before = jnp.concatenate(
            [coefs_ref[pl.ds(pl.multiple_of(turn * kb + top, rows), rows), :] for top in tops], axis=0
        ).astype(jnp.float32)
        after = jnp.maximum(before + step * correlation, 0.0)
        change = (after - before).astype(jnp.bfloat16)
        for k in range(chips):
            values[pl.ds(tops[k], rows), :] = change[k * rows : (k + 1) * rows, :]
        if turn + 1 < TURNS:
            target = residual_out if position + 1 == count else held
            for side, part in zip(sides, halves):
                moved = lax.dot_general(
                    change, part, (((0,), (0,)), ((), ())), preferred_element_type=jnp.float32
                )
                target[:, side] = (source[:, side].astype(jnp.float32) - moved).astype(jnp.bfloat16)
            source = target
        for m in range(parts):
            top = pl.multiple_of((slot ^ m) * local_kb, local_kb)
            sends[m][position * local_kb : (position + 1) * local_kb, :] = values[
                pl.ds(top, local_kb), :
            ]


def run_turns(turns, residual, coefs, pieces, parts):
    count = len(turns)
    last = turns[-1] + 1 == TURNS
    chips = len(pieces[0]) // 2
    rows, _ = pieces[0][0].shape
    points, features = residual.shape
    kb = rows * chips
    local_kb = kb // parts
    send = jax.ShapeDtypeStruct((count * local_kb, points), jnp.bfloat16)
    flat = [piece for turn in pieces for piece in turn]
    first = [] if last else [jax.ShapeDtypeStruct(residual.shape, residual.dtype)]
    flops = count * 2 * kb * features * (kb + 2 * points)
    outs = pl.pallas_call(
        functools.partial(turn_kernel, turns, chips, parts, last),
        out_shape=first + [send] * parts,
        in_specs=[VMEM] * (2 + len(flat)),
        out_specs=[VMEM] * (len(first) + parts),
        scratch_shapes=[
            pltpu.VMEM((kb, points), jnp.bfloat16),
            pltpu.VMEM(residual.shape, residual.dtype),
        ],
        cost_estimate=pl.CostEstimate(
            flops=flops, bytes_accessed=2 * features * (2 * points + count * kb), transcendentals=0
        ),
        compiler_params=pltpu.CompilerParams(vmem_limit_bytes=GRANT),
    )(residual, coefs, *flat)
    outs = list(outs)
    return (None if last else outs.pop(0)), outs


def spread(wholes):
    lane = lax.broadcasted_iota(jnp.int32, wholes[0][0].shape, 1)
    inner = lane < MAP_W - 1

    def flow(differ):
        return differ / (1.0 + differ * differ)

    shifted = [[pltpu.roll(row, MAP_W - 1, 1) for row in whole] for whole in wholes]
    rights = [
        [jnp.where(inner, flow(right - row), 0.0) for row, right in zip(whole, moved)]
        for whole, moved in zip(wholes, shifted)
    ]
    lefts = [[pltpu.roll(right, 1, 1) for right in row] for row in rights]
    news = []
    for whole, right, left in zip(wholes, rights, lefts):
        rows = len(whole)
        down = [flow(whole[r + 1] - whole[r]) for r in range(rows - 1)]
        new = []
        for r in range(rows):
            total = right[r] - left[r]
            if r > 0:
                total = total - down[r - 1]
            if r + 1 < rows:
                total = total + down[r]
            new.append(whole[r] + time_step * total)
        news.append(new)
    return news


def map_kernel(turns, parts, local_kb, first, *refs):
    count = len(turns)
    refs = list(refs)
    changes = [refs.pop(0) for _ in range(parts)]
    coefs = [refs.pop(0) for _ in range(parts)]
    if not first:
        refs.pop(0)
    out_ref, grids, staged, sem = refs
    rows = grids.shape[0]
    height = count * local_kb
    top = turns[0] * local_kb
    before = jnp.concatenate([ref[top : top + height, :] for ref in coefs], axis=1)
    values = jnp.concatenate([before, jnp.concatenate([ref[...] for ref in changes], axis=1)], axis=0)
    depth, half = TURNS * local_kb, TILE_ROWS // 2
    where = [ref[depth:, :].astype(jnp.float32) for ref in coefs]
    row = jnp.concatenate([value[:1] for value in where], axis=1)
    lane = jnp.concatenate([value[half : half + 1] for value in where], axis=1)
    targets = (row * MAP_W + lane).astype(jnp.int32)
    pair = 2 if rows % 2 == 0 else 1
    pixel = lax.broadcasted_iota(jnp.int32, (pair * MAP_W, targets.shape[1]), 0)
    for r in range(0, rows, pair):
        chosen = jnp.where(pixel == targets - r * MAP_W, 2.0, 0.0).astype(jnp.bfloat16)
        moved = lax.dot_general(
            values, chosen, (((1,), (1,)), ((), ())), preferred_element_type=jnp.float32
        )
        total = moved[:height] + moved[height:]
        for i in range(pair):
            grids[r + i] = total[:, i * MAP_W : (i + 1) * MAP_W]
    groups = height // SUBLANES
    together = UNROLL if groups % UNROLL == 0 and rows * UNROLL <= 32 else 1
    chunk = together * SUBLANES * rows
    start = turns[0] * local_kb * rows

    def one(step, carry):
        wholes = []
        for i in range(together):
            at = pl.multiple_of((step * together + i) * SUBLANES, SUBLANES)
            wholes.append([grids[r, pl.ds(at, SUBLANES), :] for r in range(rows)])
        for _ in range(SWEEPS):
            wholes = spread(wholes)
        at = step * chunk
        for i, whole in enumerate(wholes):
            for r in range(rows):
                staged[pl.ds(at + i * SUBLANES * rows + r, SUBLANES, stride=rows), :] = 0.5 * whole[r]
        pltpu.make_async_copy(
            staged.at[pl.ds(pl.multiple_of(at, chunk), chunk)],
            out_ref.at[pl.ds(pl.multiple_of(start + at, chunk), chunk)],
            sem,
        ).start()
        return carry

    lax.fori_loop(0, groups // together, one, 0)
    pltpu.make_async_copy(staged, out_ref.at[pl.ds(start, height * rows)], sem).wait()


def run_maps(turns, changes, coefs, buffer):
    parts = len(changes)
    count, points = len(turns), changes[0].shape[1]
    local_kb = changes[0].shape[0] // count
    rows = parts * points // MAP_W
    first = buffer is None
    height = count * local_kb
    extra = [] if first else [buffer]
    return pl.pallas_call(
        functools.partial(map_kernel, turns, parts, local_kb, first),
        out_shape=jax.ShapeDtypeStruct((TURNS * local_kb * rows, MAP_W), jnp.float32),
        in_specs=[VMEM] * (2 * parts) + [ANY] * len(extra),
        out_specs=ANY,
        scratch_shapes=[
            pltpu.VMEM((rows, height, MAP_W), jnp.float32),
            pltpu.VMEM((height * rows, MAP_W), jnp.float32),
            pltpu.SemaphoreType.DMA,
        ],
        input_output_aliases={} if first else {2 * parts: 0},
        cost_estimate=pl.CostEstimate(
            flops=4 * height * (parts * points) ** 2,
            bytes_accessed=8 * height * parts * points,
            transcendentals=0,
        ),
        compiler_params=pltpu.CompilerParams(vmem_limit_bytes=GRANT),
    )(*changes, *coefs, *extra)


def exchange(value, axis, size, distance):
    return lax.ppermute(value, axis, [(i, i ^ distance) for i in range(size)])


def hop(turn, k):
    low = k & -k
    high = 1 << (k.bit_length() - 1)
    return high if turn % 2 == 0 else low


def per_device(fields, parts, residual_in, coefs_in, dictionary, owner_order, pixel_of):
    residual = residual_in[0]
    points = residual.shape[0]
    coefs = coefs_in[0].reshape(points, -1)
    chips = fields // 2
    over_chips = lambda value, k: exchange(value, "field", fields, 2 * k)
    over_cores = lambda value: exchange(value, "field", fields, 1)
    over_points = lambda value, m: exchange(value, "point", parts, m)

    keep, give = cut_block(dictionary, chips)
    got = [over_cores(give[k]) for k in range(chips)]
    same = [keep[0]] + [over_chips(keep[k], k) for k in range(1, chips)]
    other = [got[0]] + [over_chips(got[k], k) for k in range(1, chips)]
    laid, turned = lay_coefs(coefs, pixel_of.reshape(1, points), parts)
    laid = [laid[0]] + [over_points(laid[m], m) for m in range(1, parts)]
    chosen = pick_turns(owner_order, same, other)

    def gather(turn):
        held = [chosen[turn]]
        for k in range(1, chips):
            bit = hop(turn, k)
            held.append(over_chips(held[k ^ bit], bit))
        return held + [over_cores(value) for value in held]

    buffer = None
    for turns in GROUPS:
        pieces = [gather(turn) for turn in turns]
        residual, sends = run_turns(turns, residual, turned, pieces, parts)
        changes = [sends[0]] + [over_points(sends[m], m) for m in range(1, parts)]
        buffer = run_maps(turns, changes, laid, buffer)
    rows = parts * points // MAP_W
    return buffer.reshape(1, TURNS, -1, rows, MAP_W)


def wrapped(fields, parts, *args):
    return per_device(fields, parts, *args)


def solution(mesh):
    placed = (
        P("field", "point", None),
        P("field", "point", None, None),
        P("field", None),
        P(),
        P("field", "point"),
    )
    fields, parts = mesh.shape["field"], mesh.shape["point"]
    return jax.shard_map(
        functools.partial(wrapped, fields, parts),
        mesh=mesh,
        in_specs=placed,
        out_specs=P("field", None, "point", None, None),
        check_vma=False,
    )
```

time: 110 us -> 82.5 us (0.75)
  the two profiles are of different devices: /device:TPU:10 before, /device:TPU:0 now
where the time goes in v2:
time: 82.5 us; the launch traced here: 82.3 us
  starting transfers between devices  44.4 us (54%)
  waiting for transfers between devices  21.1 us (26%)
  Pallas kernels  14.6 us (18%)
  local copies, waits for them, and re-layouts  2.07 us (3%)
    ppermute x47, starting transfers between devices, exchange(): return lax.ppermute(value, axis, [(i, i ^ distance) for i in range(size)])  44.4 us
    ppermute x47, waiting for transfers between devices, exchange(): return lax.ppermute(value, axis, [(i, i ^ distance) for i in range(size)])  21.1 us
    pallas_call x2, Pallas kernels, run_maps(): pl.pallas_call(functools.partial(map_kernel, turns, parts, local_kb, firs...  8.36 us
    pallas_call x2, Pallas kernels, run_turns(): pl.pallas_call(functools.partial(turn_kernel, turns, chips, parts, last),...  4.26 us
    unnamed x11, local copies, waits for them, and re-layouts  2.07 us
  transfers between devices with their start and end apart: 47, of which 13 were waited for; matrix products, arithmetic and copies ran while one was open for 0% of the time, Pallas kernels for 12%

profile of v2, /device:TPU:0, one launch (start us, length us, event | category | flops | bytes accessed | tf_op | source)
XLA Modules:
  0.0 82.3 jit_solution(16713388712547947146)
XLA Ops:
  0.0 1.2 %copy-done = bf16[256,2048]{1,0:T(8,128)(2,1)S(1)} copy-done((bf16[256,2048]{1,0:T(8,128)(2,1)S(1)}, bf16[256,2048]{1,0:T(8,128)(2,1)}, u32[]{:S(2)}) %copy-start) | copy-done | bytes 1048600
  1.5 3.0 %collective-permute-start = (bf16[64,1024]{1,0:T(8,128)(2,1)S(1)}, bf16[64,1024]{1,0:T(8,128)(2,1)S(1)}, u32[]{:S(2)}, u32[]{:S(2)}) collective-permute-start(bf16[64,1024]{1,0:T(8,128)(2,1)S(1)} %get-tuple-element.33), channel_id=1, source_target_pairs={{0,8},{4,12},{8,0},{12,4},{16,24},{20,28},{24,16},{28,20},{1,9},{5... | collective-permute-start | bytes 393224 | tf_op jit(solution)/shard_map/ppermute | solution.py:329
  4.5 1.5 %collective-permute-start.1 = (bf16[64,1024]{1,0:T(8,128)(2,1)S(1)}, bf16[64,1024]{1,0:T(8,128)(2,1)S(1)}, u32[]{:S(2)}, u32[]{:S(2)}) collective-permute-start(bf16[64,1024]{1,0:T(8,128)(2,1)S(1)} %get-tuple-element.34), channel_id=1, source_target_pairs={{0,16},{4,20},{8,24},{12,28},{16,0},{20,4},{24,8},{28,12},{1,17},{... | collective-permute-start | bytes 393224 | tf_op jit(solution)/shard_map/ppermute | solution.py:329
  6.1 0.5 collective-permute-start.6
  6.6 1.5 %collective-permute-done.refs_1_ = bf16[64,1024]{1,0:T(8,128)(2,1)S(1)} collective-permute-done((bf16[64,1024]{1,0:T(8,128)(2,1)S(1)}, bf16[64,1024]{1,0:T(8,128)(2,1)S(1)}, u32[]{:S(2)}, u32[]{:S(2)}) %collective-permute-start) | collective-permute-done | bytes 131104 | tf_op jit(solution)/shard_map/ppermute | solution.py:329
  8.0 2.7 %collective-permute-start.2 = (bf16[64,1024]{1,0:T(8,128)(2,1)S(1)}, bf16[64,1024]{1,0:T(8,128)(2,1)S(1)}, u32[]{:S(2)}, u32[]{:S(2)}) collective-permute-start(bf16[64,1024]{1,0:T(8,128)(2,1)S(1)} %get-tuple-element.35), channel_id=1, source_target_pairs={{0,24},{4,28},{8,16},{12,20},{16,8},{20,12},{24,0},{28,4},{1,25},{... | collective-permute-start | bytes 393224 | tf_op jit(solution)/shard_map/ppermute | solution.py:329
  10.7 0.6 collective-permute-start.5
  11.6 2.7 %collective-permute-start.9 = (bf16[64,1024]{1,0:T(8,128)(2,1)S(1)}, bf16[64,1024]{1,0:T(8,128)(2,1)S(1)}, u32[]{:S(2)}, u32[]{:S(2)}) collective-permute-start(bf16[64,1024]{1,0:T(8,128)(2,1)S(1)} %collective-permute-done.8), channel_id=1, source_target_pairs={{0,24},{4,28},{8,16},{12,20},{16,8},{20,12},{24,0},{28,4},{1,25},{... | collective-permute-start | bytes 393224 | tf_op jit(solution)/shard_map/ppermute | solution.py:329
  14.4 0.7 copy-done.1
  15.4 1.7 %collective-permute-start.41 = (bf16[272,256]{1,0:T(8,128)(2,1)S(1)}, bf16[272,256]{1,0:T(8,128)(2,1)S(1)}, u32[]{:S(2)}, u32[]{:S(2)}) collective-permute-start(bf16[272,256]{1,0:T(8,128)(2,1)S(1)} %get-tuple-element.50), channel_id=1, source_target_pairs={{0,1},{1,0},{2,3},{3,2},{4,5},{5,4},{6,7},{7,6},{8,9},{9,8},{10,11... | collective-permute-start | bytes 417800 | tf_op jit(solution)/shard_map/ppermute | solution.py:329
  17.1 0.3 collective-permute-done.5.refs_5_
  17.4 2.3 %collective-permute-done.7.refs_6_ = bf16[64,1024]{1,0:T(8,128)(2,1)S(1)} collective-permute-done((bf16[64,1024]{1,0:T(8,128)(2,1)S(1)}, bf16[64,1024]{1,0:T(8,128)(2,1)S(1)}, u32[]{:S(2)}, u32[]{:S(2)}) %collective-permute-start.7) | collective-permute-done | bytes 131104 | tf_op jit(solution)/shard_map/ppermute | solution.py:329
  19.7 1.5 %pick.1 = (bf16[64,1024]{1,0:T(8,128)(2,1)S(1)}, bf16[64,1024]{1,0:T(8,128)(2,1)S(1)}, bf16[64,1024]{1,0:T(8,128)(2,1)S(1)}, bf16[64,1024]{1,0:T(8,128)(2,1)S(1)}) custom-call(s32[8]{0:T(128)S(1)} %copy-done.2, bf16[64,1024]{1,0:T(8,128)(2,1)S(1)} %get-tuple-element.32.refs_0_, bf16[64,1024]{1,0:T(8,128)(2,1)S(1)} %collective-permute-done.refs_1_, ...), custom_call_target="tpu_custom_call" | custom-call | tf_op jit(solution)/shard_map/pick/pallas_call | solution.py:92
  21.3 1.6 %collective-permute-start.11 = (bf16[64,1024]{1,0:T(8,128)(2,1)S(1)}, bf16[64,1024]{1,0:T(8,128)(2,1)S(1)}, u32[]{:S(2)}, u32[]{:S(2)}) collective-permute-start(bf16[64,1024]{1,0:T(8,128)(2,1)S(1)} %get-tuple-element.40.refs_2_), channel_id=1, source_target_pairs={{0,16},{4,20},{8,24},{12,28},{16,0},{20,4},{24,8},{28,12},{1,17},{... | collective-permute-start | bytes 393224 | tf_op jit(solution)/shard_map/ppermute | solution.py:329
  22.9 1.6 %collective-permute-start.10 = (bf16[64,1024]{1,0:T(8,128)(2,1)S(1)}, bf16[64,1024]{1,0:T(8,128)(2,1)S(1)}, u32[]{:S(2)}, u32[]{:S(2)}) collective-permute-start(bf16[64,1024]{1,0:T(8,128)(2,1)S(1)} %get-tuple-element.40.refs_2_), channel_id=1, source_target_pairs={{0,8},{4,12},{8,0},{12,4},{16,24},{20,28},{24,16},{28,20},{1,9},{5... | collective-permute-start | bytes 393224 | tf_op jit(solution)/shard_map/ppermute | solution.py:329
  24.5 1.1 %collective-permute-start.18 = (bf16[64,1024]{1,0:T(8,128)(2,1)S(1)}, bf16[64,1024]{1,0:T(8,128)(2,1)S(1)}, u32[]{:S(2)}, u32[]{:S(2)}) collective-permute-start(bf16[64,1024]{1,0:T(8,128)(2,1)S(1)} %get-tuple-element.41.refs_10_), channel_id=1, source_target_pairs={{0,16},{4,20},{8,24},{12,28},{16,0},{20,4},{24,8},{28,12},{1,17},{... | collective-permute-start | bytes 393224 | tf_op jit(solution)/shard_map/ppermute | solution.py:329
  25.8 1.4 %collective-permute-done.11.refs_4_ = bf16[64,1024]{1,0:T(8,128)(2,1)S(1)} collective-permute-done((bf16[64,1024]{1,0:T(8,128)(2,1)S(1)}, bf16[64,1024]{1,0:T(8,128)(2,1)S(1)}, u32[]{:S(2)}, u32[]{:S(2)}) %collective-permute-start.11) | collective-permute-done | bytes 131104 | tf_op jit(solution)/shard_map/ppermute | solution.py:329
  27.2 1.3 %collective-permute-done.10.refs_3_ = bf16[64,1024]{1,0:T(8,128)(2,1)S(1)} collective-permute-done((bf16[64,1024]{1,0:T(8,128)(2,1)S(1)}, bf16[64,1024]{1,0:T(8,128)(2,1)S(1)}, u32[]{:S(2)}, u32[]{:S(2)}) %collective-permute-start.10) | collective-permute-done | bytes 131104 | tf_op jit(solution)/shard_map/ppermute | solution.py:329
  28.5 1.0 %collective-permute-start.25 = (bf16[64,1024]{1,0:T(8,128)(2,1)S(1)}, bf16[64,1024]{1,0:T(8,128)(2,1)S(1)}, u32[]{:S(2)}, u32[]{:S(2)}) collective-permute-start(bf16[64,1024]{1,0:T(8,128)(2,1)S(1)} %get-tuple-element.43.refs_2_), channel_id=1, source_target_pairs={{0,16},{4,20},{8,24},{12,28},{16,0},{20,4},{24,8},{28,12},{1,17},{... | collective-permute-start | bytes 393224 | tf_op jit(solution)/shard_map/ppermute | solution.py:329
  29.5 2.5 %collective-permute-start.24 = (bf16[64,1024]{1,0:T(8,128)(2,1)S(1)}, bf16[64,1024]{1,0:T(8,128)(2,1)S(1)}, u32[]{:S(2)}, u32[]{:S(2)}) collective-permute-start(bf16[64,1024]{1,0:T(8,128)(2,1)S(1)} %get-tuple-element.43.refs_2_), channel_id=1, source_target_pairs={{0,8},{4,12},{8,0},{12,4},{16,24},{20,28},{24,16},{28,20},{1,9},{5... | collective-permute-start | bytes 393224 | tf_op jit(solution)/shard_map/ppermute | solution.py:329
  32.0 1.0 %collective-permute-start.32 = (bf16[64,1024]{1,0:T(8,128)(2,1)S(1)}, bf16[64,1024]{1,0:T(8,128)(2,1)S(1)}, u32[]{:S(2)}, u32[]{:S(2)}) collective-permute-start(bf16[64,1024]{1,0:T(8,128)(2,1)S(1)} %get-tuple-element.44.refs_10_), channel_id=1, source_target_pairs={{0,16},{4,20},{8,24},{12,28},{16,0},{20,4},{24,8},{28,12},{1,17},{... | collective-permute-start | bytes 393224 | tf_op jit(solution)/shard_map/ppermute | solution.py:329
  33.0 0.9 %collective-permute-start.31 = (bf16[64,1024]{1,0:T(8,128)(2,1)S(1)}, bf16[64,1024]{1,0:T(8,128)(2,1)S(1)}, u32[]{:S(2)}, u32[]{:S(2)}) collective-permute-start(bf16[64,1024]{1,0:T(8,128)(2,1)S(1)} %get-tuple-element.44.refs_10_), channel_id=1, source_target_pairs={{0,8},{4,12},{8,0},{12,4},{16,24},{20,28},{24,16},{28,20},{1,9},{5... | collective-permute-start | bytes 393224 | tf_op jit(solution)/shard_map/ppermute | solution.py:329
  34.0 1.4 %collective-permute-done.24.refs_3_ = bf16[64,1024]{1,0:T(8,128)(2,1)S(1)} collective-permute-done((bf16[64,1024]{1,0:T(8,128)(2,1)S(1)}, bf16[64,1024]{1,0:T(8,128)(2,1)S(1)}, u32[]{:S(2)}, u32[]{:S(2)}) %collective-permute-start.24) | collective-permute-done | bytes 131104 | tf_op jit(solution)/shard_map/ppermute | solution.py:329
  35.3 0.9 %collective-permute-start.12 = (bf16[64,1024]{1,0:T(8,128)(2,1)S(1)}, bf16[64,1024]{1,0:T(8,128)(2,1)S(1)}, u32[]{:S(2)}, u32[]{:S(2)}) collective-permute-start(bf16[64,1024]{1,0:T(8,128)(2,1)S(1)} %collective-permute-done.10.refs_3_), channel_id=1, source_target_pairs={{0,16},{4,20},{8,24},{12,28},{16,0},{20,4},{24,8},{28,12},{1,17},{... | collective-permute-start | bytes 393224 | tf_op jit(solution)/shard_map/ppermute | solution.py:329
  36.2 1.7 %collective-permute-done.32.refs_12_ = bf16[64,1024]{1,0:T(8,128)(2,1)S(1)} collective-permute-done((bf16[64,1024]{1,0:T(8,128)(2,1)S(1)}, bf16[64,1024]{1,0:T(8,128)(2,1)S(1)}, u32[]{:S(2)}, u32[]{:S(2)}) %collective-permute-start.32) | collective-permute-done | bytes 131104 | tf_op jit(solution)/shard_map/ppermute | solution.py:329
  37.9 0.7 collective-permute-done.31.refs_11_
  38.6 1.2 %collective-permute-start.19 = (bf16[64,1024]{1,0:T(8,128)(2,1)S(1)}, bf16[64,1024]{1,0:T(8,128)(2,1)S(1)}, u32[]{:S(2)}, u32[]{:S(2)}) collective-permute-start(bf16[64,1024]{1,0:T(8,128)(2,1)S(1)} %collective-permute-done.18.refs_12_), channel_id=1, source_target_pairs={{0,8},{4,12},{8,0},{12,4},{16,24},{20,28},{24,16},{28,20},{1,9},{5... | collective-permute-start | bytes 393224 | tf_op jit(solution)/shard_map/ppermute | solution.py:329
  39.8 0.5 collective-permute-start.29
  40.3 1.0 %collective-permute-done.12.refs_5_ = bf16[64,1024]{1,0:T(8,128)(2,1)S(1)} collective-permute-done((bf16[64,1024]{1,0:T(8,128)(2,1)S(1)}, bf16[64,1024]{1,0:T(8,128)(2,1)S(1)}, u32[]{:S(2)}, u32[]{:S(2)}) %collective-permute-start.12) | collective-permute-done | bytes 131104 | tf_op jit(solution)/shard_map/ppermute | solution.py:329
  41.3 0.9 %collective-permute-start.26 = (bf16[64,1024]{1,0:T(8,128)(2,1)S(1)}, bf16[64,1024]{1,0:T(8,128)(2,1)S(1)}, u32[]{:S(2)}, u32[]{:S(2)}) collective-permute-start(bf16[64,1024]{1,0:T(8,128)(2,1)S(1)} %collective-permute-done.24.refs_3_), channel_id=1, source_target_pairs={{0,16},{4,20},{8,24},{12,28},{16,0},{20,4},{24,8},{28,12},{1,17},{... | collective-permute-start | bytes 393224 | tf_op jit(solution)/shard_map/ppermute | solution.py:329
  42.1 2.5 %collective-permute-start.33 = (bf16[64,1024]{1,0:T(8,128)(2,1)S(1)}, bf16[64,1024]{1,0:T(8,128)(2,1)S(1)}, u32[]{:S(2)}, u32[]{:S(2)}) collective-permute-start(bf16[64,1024]{1,0:T(8,128)(2,1)S(1)} %collective-permute-done.32.refs_12_), channel_id=1, source_target_pairs={{0,8},{4,12},{8,0},{12,4},{16,24},{20,28},{24,16},{28,20},{1,9},{5... | collective-permute-start | bytes 393224 | tf_op jit(solution)/shard_map/ppermute | solution.py:329
  44.6 0.5 collective-permute-start.23
  45.2 1.1 %collective-permute-done.26.refs_5_ = bf16[64,1024]{1,0:T(8,128)(2,1)S(1)} collective-permute-done((bf16[64,1024]{1,0:T(8,128)(2,1)S(1)}, bf16[64,1024]{1,0:T(8,128)(2,1)S(1)}, u32[]{:S(2)}, u32[]{:S(2)}) %collective-permute-start.26) | collective-permute-done | bytes 131104 | tf_op jit(solution)/shard_map/ppermute | solution.py:329
  46.3 1.3 %collective-permute-done.33.refs_13_ = bf16[64,1024]{1,0:T(8,128)(2,1)S(1)} collective-permute-done((bf16[64,1024]{1,0:T(8,128)(2,1)S(1)}, bf16[64,1024]{1,0:T(8,128)(2,1)S(1)}, u32[]{:S(2)}, u32[]{:S(2)}) %collective-permute-start.33) | collective-permute-done | bytes 131104 | tf_op jit(solution)/shard_map/ppermute | solution.py:329
  47.7 0.5 collective-permute-start.30
  48.2 2.4 %shard_map.55 = (bf16[256,2048]{1,0:T(8,128)(2,1)S(1)}, bf16[128,256]{1,0:T(8,128)(2,1)S(1)}, bf16[128,256]{1,0:T(8,128)(2,1)S(1)}, bf16[128,256]{1,0:T(8,128)(2,1)S(1)}, bf16[128,256]{1,0:T(8,128)(2,1)S(1)}) custom-call(bf16[256,2048]{1,0:T(8,128)(2,1)S(1)} %bitcast.6, bf16[1024,256]{1,0:T(8,128)(2,1)S(1)} %get-tuple-element.31.refs_1_, ...), custom_call_target="tpu_custom_call" | custom-call | flops 1610612736 | bytes 4194304 | tf_op jit(solution)/shard_map/pallas_call | solution.py:198
  50.6 2.7 %collective-permute-start.42 = (bf16[272,256]{1,0:T(8,128)(2,1)S(1)}, bf16[272,256]{1,0:T(8,128)(2,1)S(1)}, u32[]{:S(2)}, u32[]{:S(2)}) collective-permute-start(bf16[272,256]{1,0:T(8,128)(2,1)S(1)} %get-tuple-element.51), channel_id=1, source_target_pairs={{0,2},{1,3},{2,0},{3,1},{4,6},{5,7},{6,4},{7,5},{8,10},{9,11},{10,... | collective-permute-start | bytes 417800 | tf_op jit(solution)/shard_map/ppermute | solution.py:329
  53.3 1.4 %collective-permute-start.43 = (bf16[272,256]{1,0:T(8,128)(2,1)S(1)}, bf16[272,256]{1,0:T(8,128)(2,1)S(1)}, u32[]{:S(2)}, u32[]{:S(2)}) collective-permute-start(bf16[272,256]{1,0:T(8,128)(2,1)S(1)} %get-tuple-element.52), channel_id=1, source_target_pairs={{0,3},{1,2},{2,1},{3,0},{4,7},{5,6},{6,5},{7,4},{8,11},{9,10},{10,... | collective-permute-start | bytes 417800 | tf_op jit(solution)/shard_map/ppermute | solution.py:329
  54.7 0.3 collective-permute-start.44
  55.0 2.7 %collective-permute-start.45 = (bf16[128,256]{1,0:T(8,128)(2,1)S(1)}, bf16[128,256]{1,0:T(8,128)(2,1)S(1)}, u32[]{:S(2)}, u32[]{:S(2)}) collective-permute-start(bf16[128,256]{1,0:T(8,128)(2,1)S(1)} %get-tuple-element.55), channel_id=1, source_target_pairs={{0,2},{1,3},{2,0},{3,1},{4,6},{5,7},{6,4},{7,5},{8,10},{9,11},{10,... | collective-permute-start | bytes 196616 | tf_op jit(solution)/shard_map/ppermute | solution.py:329
  57.7 1.3 %collective-permute-start.46 = (bf16[128,256]{1,0:T(8,128)(2,1)S(1)}, bf16[128,256]{1,0:T(8,128)(2,1)S(1)}, u32[]{:S(2)}, u32[]{:S(2)}) collective-permute-start(bf16[128,256]{1,0:T(8,128)(2,1)S(1)} %get-tuple-element.56), channel_id=1, source_target_pairs={{0,3},{1,2},{2,1},{3,0},{4,7},{5,6},{6,5},{7,4},{8,11},{9,10},{10,... | collective-permute-start | bytes 196616 | tf_op jit(solution)/shard_map/ppermute | solution.py:329
  59.1 1.9 %shard_map.56 = (bf16[128,256]{1,0:T(8,128)(2,1)S(1)}, bf16[128,256]{1,0:T(8,128)(2,1)S(1)}, bf16[128,256]{1,0:T(8,128)(2,1)S(1)}, bf16[128,256]{1,0:T(8,128)(2,1)S(1)}) custom-call(bf16[256,2048]{1,0:T(8,128)(2,1)S(1)} %get-tuple-element.42.refs_0_, bf16[1024,256]{1,0:T(8,128)(2,1)S(1)} %get-tuple-element.31.refs_1_, ...), custom_call_target="tpu_custom_call" | custom-call | flops 1610612736 | bytes 4194304 | tf_op jit(solution)/shard_map/pallas_call | solution.py:198
  61.0 6.0 %collective-permute-done.42.refs_6_ = bf16[272,256]{1,0:T(8,128)(2,1)S(1)} collective-permute-done((bf16[272,256]{1,0:T(8,128)(2,1)S(1)}, bf16[272,256]{1,0:T(8,128)(2,1)S(1)}, u32[]{:S(2)}, u32[]{:S(2)}) %collective-permute-start.42) | collective-permute-done | bytes 139296 | tf_op jit(solution)/shard_map/ppermute | solution.py:329
  67.2 4.9 %collective-permute-start.39 = (bf16[128,256]{1,0:T(8,128)(2,1)S(1)}, bf16[128,256]{1,0:T(8,128)(2,1)S(1)}, u32[]{:S(2)}, u32[]{:S(2)}) collective-permute-start(bf16[128,256]{1,0:T(8,128)(2,1)S(1)} %get-tuple-element.47), channel_id=1, source_target_pairs={{0,2},{1,3},{2,0},{3,1},{4,6},{5,7},{6,4},{7,5},{8,10},{9,11},{10,... | collective-permute-start | bytes 196616 | tf_op jit(solution)/shard_map/ppermute | solution.py:329
  72.1 0.8 collective-permute-start.40
  72.9 4.2 %shard_map.57.refs_8_ = f32[2048,128]{1,0:T(8,128)} custom-call(bf16[128,256]{1,0:T(8,128)(2,1)S(1)} %get-tuple-element.53.refs_0_, bf16[128,256]{1,0:T(8,128)(2,1)S(1)} %collective-permute-done.44.refs_1_, bf16[128,256]{1,0:T(8,128)(2,1)S(1)} %collective-permute-done.45.refs_2_, bf16[128,256]{1,0:T(8,128)(2,1)S(1)} %collective-permute-done.46.refs_3_, ...), custom_call_target="tpu_custom_call" | custom-call | flops 536870912 | bytes 1048576 | tf_op jit(solution)/shard_map/pallas_call | solution.py:308
  77.1 1.1 %collective-permute-done.40.refs_3_ = bf16[128,256]{1,0:T(8,128)(2,1)S(1)} collective-permute-done((bf16[128,256]{1,0:T(8,128)(2,1)S(1)}, bf16[128,256]{1,0:T(8,128)(2,1)S(1)}, u32[]{:S(2)}, u32[]{:S(2)}) %collective-permute-start.40) | collective-permute-done | bytes 65568 | tf_op jit(solution)/shard_map/ppermute | solution.py:329
  78.1 4.2 %shard_map.58 = f32[2048,128]{1,0:T(8,128)} custom-call(bf16[128,256]{1,0:T(8,128)(2,1)S(1)} %get-tuple-element.45.refs_0_, bf16[128,256]{1,0:T(8,128)(2,1)S(1)} %collective-permute-done.38.refs_1_, bf16[128,256]{1,0:T(8,128)(2,1)S(1)} %collective-permute-done.39.refs_2_, ...), custom_call_target="tpu_custom_call", output_to_operand_aliasing={{}: (8, {})} | custom-call | flops 536870912 | bytes 1048576 | tf_op jit(solution)/shard_map/pallas_call | solution.py:308
  (64 shorter events, 1.6 us)
Async XLA Ops:
  1.5 6.5 %collective-permute-start = (bf16[64,1024]{1,0:T(8,128)(2,1)S(1)}, bf16[64,1024]{1,0:T(8,128)(2,1)S(1)}, u32[]{:S(2)}, u32[]{:S(2)}) collective-permute-start(bf16[64,1024]{1,0:T(8,128)(2,1)S(1)} %get-tuple-element.33), channel_id=1, source_target_pairs={{0,8},{4,12},{8,0},{12,4},{16,24},{20,28},{24,16},{28,20},{1,9},{5... | collective-permute-start | bytes 393224 | tf_op jit(solution)/shard_map/ppermute | solution.py:329
  4.5 6.2 %collective-permute-start.1 = (bf16[64,1024]{1,0:T(8,128)(2,1)S(1)}, bf16[64,1024]{1,0:T(8,128)(2,1)S(1)}, u32[]{:S(2)}, u32[]{:S(2)}) collective-permute-start(bf16[64,1024]{1,0:T(8,128)(2,1)S(1)} %get-tuple-element.34), channel_id=1, source_target_pairs={{0,16},{4,20},{8,24},{12,28},{16,0},{20,4},{24,8},{28,12},{1,17},{... | collective-permute-start | bytes 393224 | tf_op jit(solution)/shard_map/ppermute | solution.py:329
  6.1 4.7 %collective-permute-start.4 = (bf16[64,1024]{1,0:T(8,128)(2,1)S(1)}, bf16[64,1024]{1,0:T(8,128)(2,1)S(1)}, u32[]{:S(2)}, u32[]{:S(2)}) collective-permute-start(bf16[64,1024]{1,0:T(8,128)(2,1)S(1)} %get-tuple-element.37), channel_id=1, source_target_pairs={{0,4},{4,0},{8,12},{12,8},{16,20},{20,16},{24,28},{28,24},{1,5},{5... | collective-permute-start | bytes 393224 | tf_op jit(solution)/shard_map/ppermute | solution.py:329
  6.1 5.3 %collective-permute-start.6 = (bf16[64,1024]{1,0:T(8,128)(2,1)S(1)}, bf16[64,1024]{1,0:T(8,128)(2,1)S(1)}, u32[]{:S(2)}, u32[]{:S(2)}) collective-permute-start(bf16[64,1024]{1,0:T(8,128)(2,1)S(1)} %get-tuple-element.38), channel_id=1, source_target_pairs={{0,4},{4,0},{8,12},{12,8},{16,20},{20,16},{24,28},{28,24},{1,5},{5... | collective-permute-start | bytes 393224 | tf_op jit(solution)/shard_map/ppermute | solution.py:329
  6.6 5.1 %collective-permute-start.8 = (bf16[64,1024]{1,0:T(8,128)(2,1)S(1)}, bf16[64,1024]{1,0:T(8,128)(2,1)S(1)}, u32[]{:S(2)}, u32[]{:S(2)}) collective-permute-start(bf16[64,1024]{1,0:T(8,128)(2,1)S(1)} %get-tuple-element.39), channel_id=1, source_target_pairs={{0,4},{4,0},{8,12},{12,8},{16,20},{20,16},{24,28},{28,24},{1,5},{5... | collective-permute-start | bytes 393224 | tf_op jit(solution)/shard_map/ppermute | solution.py:329
  8.0 7.4 %collective-permute-start.2 = (bf16[64,1024]{1,0:T(8,128)(2,1)S(1)}, bf16[64,1024]{1,0:T(8,128)(2,1)S(1)}, u32[]{:S(2)}, u32[]{:S(2)}) collective-permute-start(bf16[64,1024]{1,0:T(8,128)(2,1)S(1)} %get-tuple-element.35), channel_id=1, source_target_pairs={{0,24},{4,28},{8,16},{12,20},{16,8},{20,12},{24,0},{28,4},{1,25},{... | collective-permute-start | bytes 393224 | tf_op jit(solution)/shard_map/ppermute | solution.py:329
  10.7 6.4 %collective-permute-start.3 = (bf16[64,1024]{1,0:T(8,128)(2,1)S(1)}, bf16[64,1024]{1,0:T(8,128)(2,1)S(1)}, u32[]{:S(2)}, u32[]{:S(2)}) collective-permute-start(bf16[64,1024]{1,0:T(8,128)(2,1)S(1)} %get-tuple-element.36), channel_id=1, source_target_pairs={{0,4},{4,0},{8,12},{12,8},{16,20},{20,16},{24,28},{28,24},{1,5},{5... | collective-permute-start | bytes 393224 | tf_op jit(solution)/shard_map/ppermute | solution.py:329
  10.7 6.6 %collective-permute-start.5 = (bf16[64,1024]{1,0:T(8,128)(2,1)S(1)}, bf16[64,1024]{1,0:T(8,128)(2,1)S(1)}, u32[]{:S(2)}, u32[]{:S(2)}) collective-permute-start(bf16[64,1024]{1,0:T(8,128)(2,1)S(1)} %collective-permute-done.4), channel_id=1, source_target_pairs={{0,8},{4,12},{8,0},{12,4},{16,24},{20,28},{24,16},{28,20},{1,9},{5... | collective-permute-start | bytes 393224 | tf_op jit(solution)/shard_map/ppermute | solution.py:329
  11.3 8.4 %collective-permute-start.7 = (bf16[64,1024]{1,0:T(8,128)(2,1)S(1)}, bf16[64,1024]{1,0:T(8,128)(2,1)S(1)}, u32[]{:S(2)}, u32[]{:S(2)}) collective-permute-start(bf16[64,1024]{1,0:T(8,128)(2,1)S(1)} %collective-permute-done.6), channel_id=1, source_target_pairs={{0,16},{4,20},{8,24},{12,28},{16,0},{20,4},{24,8},{28,12},{1,17},{... | collective-permute-start | bytes 393224 | tf_op jit(solution)/shard_map/ppermute | solution.py:329
  11.6 8.1 %collective-permute-start.9 = (bf16[64,1024]{1,0:T(8,128)(2,1)S(1)}, bf16[64,1024]{1,0:T(8,128)(2,1)S(1)}, u32[]{:S(2)}, u32[]{:S(2)}) collective-permute-start(bf16[64,1024]{1,0:T(8,128)(2,1)S(1)} %collective-permute-done.8), channel_id=1, source_target_pairs={{0,24},{4,28},{8,16},{12,20},{16,8},{20,12},{24,0},{28,4},{1,25},{... | collective-permute-start | bytes 393224 | tf_op jit(solution)/shard_map/ppermute | solution.py:329
  14.3 33.9 %copy-start.3 = (bf16[1,256,2048]{2,1,0:T(8,128)(2,1)S(1)}, bf16[1,256,2048]{2,1,0:T(8,128)(2,1)}, u32[]{:S(2)}) copy-start(bf16[1,256,2048]{2,1,0:T(8,128)(2,1)} %param.5) | copy-start | bytes 3145732
  15.4 9.1 %collective-permute-start.41 = (bf16[272,256]{1,0:T(8,128)(2,1)S(1)}, bf16[272,256]{1,0:T(8,128)(2,1)S(1)}, u32[]{:S(2)}, u32[]{:S(2)}) collective-permute-start(bf16[272,256]{1,0:T(8,128)(2,1)S(1)} %get-tuple-element.50), channel_id=1, source_target_pairs={{0,1},{1,0},{2,3},{3,2},{4,5},{5,4},{6,7},{7,6},{8,9},{9,8},{10,11... | collective-permute-start | bytes 417800 | tf_op jit(solution)/shard_map/ppermute | solution.py:329
  21.2 4.4 %collective-permute-start.13 = (bf16[64,1024]{1,0:T(8,128)(2,1)S(1)}, bf16[64,1024]{1,0:T(8,128)(2,1)S(1)}, u32[]{:S(2)}, u32[]{:S(2)}) collective-permute-start(bf16[64,1024]{1,0:T(8,128)(2,1)S(1)} %get-tuple-element.40.refs_2_), channel_id=1, source_target_pairs={{0,4},{4,0},{8,12},{12,8},{16,20},{20,16},{24,28},{28,24},{1,5},{5... | collective-permute-start | bytes 393224 | tf_op jit(solution)/shard_map/ppermute | solution.py:329
  21.3 5.9 %collective-permute-start.11 = (bf16[64,1024]{1,0:T(8,128)(2,1)S(1)}, bf16[64,1024]{1,0:T(8,128)(2,1)S(1)}, u32[]{:S(2)}, u32[]{:S(2)}) collective-permute-start(bf16[64,1024]{1,0:T(8,128)(2,1)S(1)} %get-tuple-element.40.refs_2_), channel_id=1, source_target_pairs={{0,16},{4,20},{8,24},{12,28},{16,0},{20,4},{24,8},{28,12},{1,17},{... | collective-permute-start | bytes 393224 | tf_op jit(solution)/shard_map/ppermute | solution.py:329
  22.9 5.6 %collective-permute-start.10 = (bf16[64,1024]{1,0:T(8,128)(2,1)S(1)}, bf16[64,1024]{1,0:T(8,128)(2,1)S(1)}, u32[]{:S(2)}, u32[]{:S(2)}) collective-permute-start(bf16[64,1024]{1,0:T(8,128)(2,1)S(1)} %get-tuple-element.40.refs_2_), channel_id=1, source_target_pairs={{0,8},{4,12},{8,0},{12,4},{16,24},{20,28},{24,16},{28,20},{1,9},{5... | collective-permute-start | bytes 393224 | tf_op jit(solution)/shard_map/ppermute | solution.py:329
  24.5 5.0 %collective-permute-start.20 = (bf16[64,1024]{1,0:T(8,128)(2,1)S(1)}, bf16[64,1024]{1,0:T(8,128)(2,1)S(1)}, u32[]{:S(2)}, u32[]{:S(2)}) collective-permute-start(bf16[64,1024]{1,0:T(8,128)(2,1)S(1)} %get-tuple-element.41.refs_10_), channel_id=1, source_target_pairs={{0,4},{4,0},{8,12},{12,8},{16,20},{20,16},{24,28},{28,24},{1,5},{5... | collective-permute-start | bytes 393224 | tf_op jit(solution)/shard_map/ppermute | solution.py:329
  24.5 7.4 %collective-permute-start.18 = (bf16[64,1024]{1,0:T(8,128)(2,1)S(1)}, bf16[64,1024]{1,0:T(8,128)(2,1)S(1)}, u32[]{:S(2)}, u32[]{:S(2)}) collective-permute-start(bf16[64,1024]{1,0:T(8,128)(2,1)S(1)} %get-tuple-element.41.refs_10_), channel_id=1, source_target_pairs={{0,16},{4,20},{8,24},{12,28},{16,0},{20,4},{24,8},{28,12},{1,17},{... | collective-permute-start | bytes 393224 | tf_op jit(solution)/shard_map/ppermute | solution.py:329
  25.6 6.4 %collective-permute-start.17 = (bf16[64,1024]{1,0:T(8,128)(2,1)S(1)}, bf16[64,1024]{1,0:T(8,128)(2,1)S(1)}, u32[]{:S(2)}, u32[]{:S(2)}) collective-permute-start(bf16[64,1024]{1,0:T(8,128)(2,1)S(1)} %get-tuple-element.41.refs_10_), channel_id=1, source_target_pairs={{0,8},{4,12},{8,0},{12,4},{16,24},{20,28},{24,16},{28,20},{1,9},{5... | collective-permute-start | bytes 393224 | tf_op jit(solution)/shard_map/ppermute | solution.py:329
  27.2 5.8 %collective-permute-start.27 = (bf16[64,1024]{1,0:T(8,128)(2,1)S(1)}, bf16[64,1024]{1,0:T(8,128)(2,1)S(1)}, u32[]{:S(2)}, u32[]{:S(2)}) collective-permute-start(bf16[64,1024]{1,0:T(8,128)(2,1)S(1)} %get-tuple-element.43.refs_2_), channel_id=1, source_target_pairs={{0,4},{4,0},{8,12},{12,8},{16,20},{20,16},{24,28},{28,24},{1,5},{5... | collective-permute-start | bytes 393224 | tf_op jit(solution)/shard_map/ppermute | solution.py:329
  28.5 5.5 %collective-permute-start.25 = (bf16[64,1024]{1,0:T(8,128)(2,1)S(1)}, bf16[64,1024]{1,0:T(8,128)(2,1)S(1)}, u32[]{:S(2)}, u32[]{:S(2)}) collective-permute-start(bf16[64,1024]{1,0:T(8,128)(2,1)S(1)} %get-tuple-element.43.refs_2_), channel_id=1, source_target_pairs={{0,16},{4,20},{8,24},{12,28},{16,0},{20,4},{24,8},{28,12},{1,17},{... | collective-permute-start | bytes 393224 | tf_op jit(solution)/shard_map/ppermute | solution.py:329
  29.5 5.8 %collective-permute-start.24 = (bf16[64,1024]{1,0:T(8,128)(2,1)S(1)}, bf16[64,1024]{1,0:T(8,128)(2,1)S(1)}, u32[]{:S(2)}, u32[]{:S(2)}) collective-permute-start(bf16[64,1024]{1,0:T(8,128)(2,1)S(1)} %get-tuple-element.43.refs_2_), channel_id=1, source_target_pairs={{0,8},{4,12},{8,0},{12,4},{16,24},{20,28},{24,16},{28,20},{1,9},{5... | collective-permute-start | bytes 393224 | tf_op jit(solution)/shard_map/ppermute | solution.py:329
  32.0 3.4 %collective-permute-start.34 = (bf16[64,1024]{1,0:T(8,128)(2,1)S(1)}, bf16[64,1024]{1,0:T(8,128)(2,1)S(1)}, u32[]{:S(2)}, u32[]{:S(2)}) collective-permute-start(bf16[64,1024]{1,0:T(8,128)(2,1)S(1)} %get-tuple-element.44.refs_10_), channel_id=1, source_target_pairs={{0,4},{4,0},{8,12},{12,8},{16,20},{20,16},{24,28},{28,24},{1,5},{5... | collective-permute-start | bytes 393224 | tf_op jit(solution)/shard_map/ppermute | solution.py:329
  32.0 5.9 %collective-permute-start.32 = (bf16[64,1024]{1,0:T(8,128)(2,1)S(1)}, bf16[64,1024]{1,0:T(8,128)(2,1)S(1)}, u32[]{:S(2)}, u32[]{:S(2)}) collective-permute-start(bf16[64,1024]{1,0:T(8,128)(2,1)S(1)} %get-tuple-element.44.refs_10_), channel_id=1, source_target_pairs={{0,16},{4,20},{8,24},{12,28},{16,0},{20,4},{24,8},{28,12},{1,17},{... | collective-permute-start | bytes 393224 | tf_op jit(solution)/shard_map/ppermute | solution.py:329
  33.0 5.6 %collective-permute-start.31 = (bf16[64,1024]{1,0:T(8,128)(2,1)S(1)}, bf16[64,1024]{1,0:T(8,128)(2,1)S(1)}, u32[]{:S(2)}, u32[]{:S(2)}) collective-permute-start(bf16[64,1024]{1,0:T(8,128)(2,1)S(1)} %get-tuple-element.44.refs_10_), channel_id=1, source_target_pairs={{0,8},{4,12},{8,0},{12,4},{16,24},{20,28},{24,16},{28,20},{1,9},{5... | collective-permute-start | bytes 393224 | tf_op jit(solution)/shard_map/ppermute | solution.py:329
  34.0 5.8 %collective-permute-start.15 = (bf16[64,1024]{1,0:T(8,128)(2,1)S(1)}, bf16[64,1024]{1,0:T(8,128)(2,1)S(1)}, u32[]{:S(2)}, u32[]{:S(2)}) collective-permute-start(bf16[64,1024]{1,0:T(8,128)(2,1)S(1)} %collective-permute-done.11.refs_4_), channel_id=1, source_target_pairs={{0,4},{4,0},{8,12},{12,8},{16,20},{20,16},{24,28},{28,24},{1,5},{5... | collective-permute-start | bytes 393224 | tf_op jit(solution)/shard_map/ppermute | solution.py:329
  35.3 4.4 %collective-permute-start.14 = (bf16[64,1024]{1,0:T(8,128)(2,1)S(1)}, bf16[64,1024]{1,0:T(8,128)(2,1)S(1)}, u32[]{:S(2)}, u32[]{:S(2)}) collective-permute-start(bf16[64,1024]{1,0:T(8,128)(2,1)S(1)} %collective-permute-done.10.refs_3_), channel_id=1, source_target_pairs={{0,4},{4,0},{8,12},{12,8},{16,20},{20,16},{24,28},{28,24},{1,5},{5... | collective-permute-start | bytes 393224 | tf_op jit(solution)/shard_map/ppermute | solution.py:329
  35.3 5.9 %collective-permute-start.12 = (bf16[64,1024]{1,0:T(8,128)(2,1)S(1)}, bf16[64,1024]{1,0:T(8,128)(2,1)S(1)}, u32[]{:S(2)}, u32[]{:S(2)}) collective-permute-start(bf16[64,1024]{1,0:T(8,128)(2,1)S(1)} %collective-permute-done.10.refs_3_), channel_id=1, source_target_pairs={{0,16},{4,20},{8,24},{12,28},{16,0},{20,4},{24,8},{28,12},{1,17},{... | collective-permute-start | bytes 393224 | tf_op jit(solution)/shard_map/ppermute | solution.py:329
  37.9 4.2 %collective-permute-start.22 = (bf16[64,1024]{1,0:T(8,128)(2,1)S(1)}, bf16[64,1024]{1,0:T(8,128)(2,1)S(1)}, u32[]{:S(2)}, u32[]{:S(2)}) collective-permute-start(bf16[64,1024]{1,0:T(8,128)(2,1)S(1)} %collective-permute-done.18.refs_12_), channel_id=1, source_target_pairs={{0,4},{4,0},{8,12},{12,8},{16,20},{20,16},{24,28},{28,24},{1,5},{5... | collective-permute-start | bytes 393224 | tf_op jit(solution)/shard_map/ppermute | solution.py:329
  38.6 6.0 %collective-permute-start.19 = (bf16[64,1024]{1,0:T(8,128)(2,1)S(1)}, bf16[64,1024]{1,0:T(8,128)(2,1)S(1)}, u32[]{:S(2)}, u32[]{:S(2)}) collective-permute-start(bf16[64,1024]{1,0:T(8,128)(2,1)S(1)} %collective-permute-done.18.refs_12_), channel_id=1, source_target_pairs={{0,8},{4,12},{8,0},{12,4},{16,24},{20,28},{24,16},{28,20},{1,9},{5... | collective-permute-start | bytes 393224 | tf_op jit(solution)/shard_map/ppermute | solution.py:329
  39.8 4.9 %collective-permute-start.21 = (bf16[64,1024]{1,0:T(8,128)(2,1)S(1)}, bf16[64,1024]{1,0:T(8,128)(2,1)S(1)}, u32[]{:S(2)}, u32[]{:S(2)}) collective-permute-start(bf16[64,1024]{1,0:T(8,128)(2,1)S(1)} %collective-permute-done.17.refs_11_), channel_id=1, source_target_pairs={{0,4},{4,0},{8,12},{12,8},{16,20},{20,16},{24,28},{28,24},{1,5},{5... | collective-permute-start | bytes 393224 | tf_op jit(solution)/shard_map/ppermute | solution.py:329
  39.8 5.4 %collective-permute-start.29 = (bf16[64,1024]{1,0:T(8,128)(2,1)S(1)}, bf16[64,1024]{1,0:T(8,128)(2,1)S(1)}, u32[]{:S(2)}, u32[]{:S(2)}) collective-permute-start(bf16[64,1024]{1,0:T(8,128)(2,1)S(1)} %collective-permute-done.25.refs_4_), channel_id=1, source_target_pairs={{0,4},{4,0},{8,12},{12,8},{16,20},{20,16},{24,28},{28,24},{1,5},{5... | collective-permute-start | bytes 393224 | tf_op jit(solution)/shard_map/ppermute | solution.py:329
  41.3 5.1 %collective-permute-start.26 = (bf16[64,1024]{1,0:T(8,128)(2,1)S(1)}, bf16[64,1024]{1,0:T(8,128)(2,1)S(1)}, u32[]{:S(2)}, u32[]{:S(2)}) collective-permute-start(bf16[64,1024]{1,0:T(8,128)(2,1)S(1)} %collective-permute-done.24.refs_3_), channel_id=1, source_target_pairs={{0,16},{4,20},{8,24},{12,28},{16,0},{20,4},{24,8},{28,12},{1,17},{... | collective-permute-start | bytes 393224 | tf_op jit(solution)/shard_map/ppermute | solution.py:329
  42.1 5.5 %collective-permute-start.33 = (bf16[64,1024]{1,0:T(8,128)(2,1)S(1)}, bf16[64,1024]{1,0:T(8,128)(2,1)S(1)}, u32[]{:S(2)}, u32[]{:S(2)}) collective-permute-start(bf16[64,1024]{1,0:T(8,128)(2,1)S(1)} %collective-permute-done.32.refs_12_), channel_id=1, source_target_pairs={{0,8},{4,12},{8,0},{12,4},{16,24},{20,28},{24,16},{28,20},{1,9},{5... | collective-permute-start | bytes 393224 | tf_op jit(solution)/shard_map/ppermute | solution.py:329
  44.6 3.0 %collective-permute-start.16 = (bf16[64,1024]{1,0:T(8,128)(2,1)S(1)}, bf16[64,1024]{1,0:T(8,128)(2,1)S(1)}, u32[]{:S(2)}, u32[]{:S(2)}) collective-permute-start(bf16[64,1024]{1,0:T(8,128)(2,1)S(1)} %collective-permute-done.12.refs_5_), channel_id=1, source_target_pairs={{0,4},{4,0},{8,12},{12,8},{16,20},{20,16},{24,28},{28,24},{1,5},{5... | collective-permute-start | bytes 393224 | tf_op jit(solution)/shard_map/ppermute | solution.py:329
  44.6 3.5 %collective-permute-start.23 = (bf16[64,1024]{1,0:T(8,128)(2,1)S(1)}, bf16[64,1024]{1,0:T(8,128)(2,1)S(1)}, u32[]{:S(2)}, u32[]{:S(2)}) collective-permute-start(bf16[64,1024]{1,0:T(8,128)(2,1)S(1)} %collective-permute-done.19.refs_13_), channel_id=1, source_target_pairs={{0,4},{4,0},{8,12},{12,8},{16,20},{20,16},{24,28},{28,24},{1,5},{5... | collective-permute-start | bytes 393224 | tf_op jit(solution)/shard_map/ppermute | solution.py:329
  45.1 5.5 %collective-permute-start.28 = (bf16[64,1024]{1,0:T(8,128)(2,1)S(1)}, bf16[64,1024]{1,0:T(8,128)(2,1)S(1)}, u32[]{:S(2)}, u32[]{:S(2)}) collective-permute-start(bf16[64,1024]{1,0:T(8,128)(2,1)S(1)} %collective-permute-done.24.refs_3_), channel_id=1, source_target_pairs={{0,4},{4,0},{8,12},{12,8},{16,20},{20,16},{24,28},{28,24},{1,5},{5... | collective-permute-start | bytes 393224 | tf_op jit(solution)/shard_map/ppermute | solution.py:329
  46.3 7.0 %collective-permute-start.36 = (bf16[64,1024]{1,0:T(8,128)(2,1)S(1)}, bf16[64,1024]{1,0:T(8,128)(2,1)S(1)}, u32[]{:S(2)}, u32[]{:S(2)}) collective-permute-start(bf16[64,1024]{1,0:T(8,128)(2,1)S(1)} %collective-permute-done.32.refs_12_), channel_id=1, source_target_pairs={{0,4},{4,0},{8,12},{12,8},{16,20},{20,16},{24,28},{28,24},{1,5},{5... | collective-permute-start | bytes 393224 | tf_op jit(solution)/shard_map/ppermute | solution.py:329
  47.6 7.0 %collective-permute-start.35 = (bf16[64,1024]{1,0:T(8,128)(2,1)S(1)}, bf16[64,1024]{1,0:T(8,128)(2,1)S(1)}, u32[]{:S(2)}, u32[]{:S(2)}) collective-permute-start(bf16[64,1024]{1,0:T(8,128)(2,1)S(1)} %collective-permute-done.31.refs_11_), channel_id=1, source_target_pairs={{0,4},{4,0},{8,12},{12,8},{16,20},{20,16},{24,28},{28,24},{1,5},{5... | collective-permute-start | bytes 393224 | tf_op jit(solution)/shard_map/ppermute | solution.py:329
  47.7 7.3 %collective-permute-start.30 = (bf16[64,1024]{1,0:T(8,128)(2,1)S(1)}, bf16[64,1024]{1,0:T(8,128)(2,1)S(1)}, u32[]{:S(2)}, u32[]{:S(2)}) collective-permute-start(bf16[64,1024]{1,0:T(8,128)(2,1)S(1)} %collective-permute-done.26.refs_5_), channel_id=1, source_target_pairs={{0,4},{4,0},{8,12},{12,8},{16,20},{20,16},{24,28},{28,24},{1,5},{5... | collective-permute-start | bytes 393224 | tf_op jit(solution)/shard_map/ppermute | solution.py:329
  48.2 9.5 %collective-permute-start.37 = (bf16[64,1024]{1,0:T(8,128)(2,1)S(1)}, bf16[64,1024]{1,0:T(8,128)(2,1)S(1)}, u32[]{:S(2)}, u32[]{:S(2)}) collective-permute-start(bf16[64,1024]{1,0:T(8,128)(2,1)S(1)} %collective-permute-done.33.refs_13_), channel_id=1, source_target_pairs={{0,4},{4,0},{8,12},{12,8},{16,20},{20,16},{24,28},{28,24},{1,5},{5... | collective-permute-start | bytes 393224 | tf_op jit(solution)/shard_map/ppermute | solution.py:329
  50.6 16.3 %collective-permute-start.42 = (bf16[272,256]{1,0:T(8,128)(2,1)S(1)}, bf16[272,256]{1,0:T(8,128)(2,1)S(1)}, u32[]{:S(2)}, u32[]{:S(2)}) collective-permute-start(bf16[272,256]{1,0:T(8,128)(2,1)S(1)} %get-tuple-element.51), channel_id=1, source_target_pairs={{0,2},{1,3},{2,0},{3,1},{4,6},{5,7},{6,4},{7,5},{8,10},{9,11},{10,... | collective-permute-start | bytes 417800 | tf_op jit(solution)/shard_map/ppermute | solution.py:329
  53.3 13.9 %collective-permute-start.43 = (bf16[272,256]{1,0:T(8,128)(2,1)S(1)}, bf16[272,256]{1,0:T(8,128)(2,1)S(1)}, u32[]{:S(2)}, u32[]{:S(2)}) collective-permute-start(bf16[272,256]{1,0:T(8,128)(2,1)S(1)} %get-tuple-element.52), channel_id=1, source_target_pairs={{0,3},{1,2},{2,1},{3,0},{4,7},{5,6},{6,5},{7,4},{8,11},{9,10},{10,... | collective-permute-start | bytes 417800 | tf_op jit(solution)/shard_map/ppermute | solution.py:329
  54.7 17.4 %collective-permute-start.44 = (bf16[128,256]{1,0:T(8,128)(2,1)S(1)}, bf16[128,256]{1,0:T(8,128)(2,1)S(1)}, u32[]{:S(2)}, u32[]{:S(2)}) collective-permute-start(bf16[128,256]{1,0:T(8,128)(2,1)S(1)} %get-tuple-element.54), channel_id=1, source_target_pairs={{0,1},{1,0},{2,3},{3,2},{4,5},{5,4},{6,7},{7,6},{8,9},{9,8},{10,11... | collective-permute-start | bytes 196616 | tf_op jit(solution)/shard_map/ppermute | solution.py:329
  55.0 17.9 %collective-permute-start.45 = (bf16[128,256]{1,0:T(8,128)(2,1)S(1)}, bf16[128,256]{1,0:T(8,128)(2,1)S(1)}, u32[]{:S(2)}, u32[]{:S(2)}) collective-permute-start(bf16[128,256]{1,0:T(8,128)(2,1)S(1)} %get-tuple-element.55), channel_id=1, source_target_pairs={{0,2},{1,3},{2,0},{3,1},{4,6},{5,7},{6,4},{7,5},{8,10},{9,11},{10,... | collective-permute-start | bytes 196616 | tf_op jit(solution)/shard_map/ppermute | solution.py:329
  57.7 15.1 %collective-permute-start.46 = (bf16[128,256]{1,0:T(8,128)(2,1)S(1)}, bf16[128,256]{1,0:T(8,128)(2,1)S(1)}, u32[]{:S(2)}, u32[]{:S(2)}) collective-permute-start(bf16[128,256]{1,0:T(8,128)(2,1)S(1)} %get-tuple-element.56), channel_id=1, source_target_pairs={{0,3},{1,2},{2,1},{3,0},{4,7},{5,6},{6,5},{7,4},{8,11},{9,10},{10,... | collective-permute-start | bytes 196616 | tf_op jit(solution)/shard_map/ppermute | solution.py:329
  66.9 10.1 %collective-permute-start.38 = (bf16[128,256]{1,0:T(8,128)(2,1)S(1)}, bf16[128,256]{1,0:T(8,128)(2,1)S(1)}, u32[]{:S(2)}, u32[]{:S(2)}) collective-permute-start(bf16[128,256]{1,0:T(8,128)(2,1)S(1)} %get-tuple-element.46), channel_id=1, source_target_pairs={{0,1},{1,0},{2,3},{3,2},{4,5},{5,4},{6,7},{7,6},{8,9},{9,8},{10,11... | collective-permute-start | bytes 196616 | tf_op jit(solution)/shard_map/ppermute | solution.py:329
  67.2 9.9 %collective-permute-start.39 = (bf16[128,256]{1,0:T(8,128)(2,1)S(1)}, bf16[128,256]{1,0:T(8,128)(2,1)S(1)}, u32[]{:S(2)}, u32[]{:S(2)}) collective-permute-start(bf16[128,256]{1,0:T(8,128)(2,1)S(1)} %get-tuple-element.47), channel_id=1, source_target_pairs={{0,2},{1,3},{2,0},{3,1},{4,6},{5,7},{6,4},{7,5},{8,10},{9,11},{10,... | collective-permute-start | bytes 196616 | tf_op jit(solution)/shard_map/ppermute | solution.py:329
  72.1 6.1 %collective-permute-start.40 = (bf16[128,256]{1,0:T(8,128)(2,1)S(1)}, bf16[128,256]{1,0:T(8,128)(2,1)S(1)}, u32[]{:S(2)}, u32[]{:S(2)}) collective-permute-start(bf16[128,256]{1,0:T(8,128)(2,1)S(1)} %get-tuple-element.48), channel_id=1, source_target_pairs={{0,3},{1,2},{2,1},{3,0},{4,7},{5,6},{6,5},{7,4},{8,11},{9,10},{10,... | collective-permute-start | bytes 196616 | tf_op jit(solution)/shard_map/ppermute | solution.py:329
  (4 other events, 19.4 us)

commit v3 on v2

--- a/solution.py
+++ b/solution.py
@@ -12,7 +12,7 @@
 SWEEPS = 4
 MAP_W = 128
 SUBLANES = 8
-UNROLL = 4
+UNROLL = 8
 TILE_ROWS = 16
 GRANT = 16 * 1024 * 1024
 
@@ -31,22 +31,27 @@
     return index // 2, index % 2
 
 
+def hops(turn, chips):
+    bits = [1 << i for i in range(chips.bit_length() - 1)]
+    return bits if turn % 2 == 0 else bits[::-1]
+
+
+def distances(turn, chips):
+    found = [0]
+    for bit in hops(turn, chips):
+        found += [bit ^ k for k in found]
+    return found
+
+
 def slice_kernel(chips, block_ref, *refs):
-    keep, give, sems = refs[:chips], refs[chips : 2 * chips], refs[2 * chips]
+    keep, give = refs[:chips], refs[chips:]
     chip, core = place_of_device()
     rows, half = keep[0].shape
-    copies = []
     for k in range(chips):
         top = pl.multiple_of((chip ^ k) * rows, rows)
-        for number, (out, which) in enumerate(((give[k], 1 - core), (keep[k], core))):
+        for out, which in ((keep[k], core), (give[k], 1 - core)):
             left = pl.multiple_of(which * half, half)
-            copy = pltpu.make_async_copy(
-                block_ref.at[pl.ds(top, rows), pl.ds(left, half)], out, sems.at[2 * k + number]
-            )
-            copy.start()
-            copies.append(copy)
-    for copy in copies:
-        copy.wait()
+            out[...] = block_ref[pl.ds(top, rows), pl.ds(left, half)]
 
 
 def cut_block(block, chips):
@@ -55,9 +60,8 @@
     outs = pl.pallas_call(
         functools.partial(slice_kernel, chips),
         out_shape=[piece] * (2 * chips),
-        in_specs=[ANY],
+        in_specs=[VMEM],
         out_specs=[VMEM] * (2 * chips),
-        scratch_shapes=[pltpu.SemaphoreType.DMA((2 * chips,))],
         compiler_params=pltpu.CompilerParams(vmem_limit_bytes=GRANT),
         name="cut",
     )(block)
@@ -65,25 +69,16 @@
 
 
 def pick_kernel(chips, order_ref, *refs):
-    same, other = refs[:chips], refs[chips : 2 * chips]
-    outs, sems = refs[2 * chips : 2 * chips + TURNS], refs[2 * chips + TURNS]
+    pieces, outs = refs[: 2 * chips], refs[2 * chips :]
     chip, core = place_of_device()
     for turn in range(TURNS):
         owner = order_ref[turn]
-        distance = (owner // 2) ^ chip
-        mine = owner % 2 == core
-        for k in range(chips):
-
-            @pl.when((distance == k) & mine)
+        wanted = ((owner // 2) ^ chip) + chips * ((owner % 2) ^ core)
+        for number, piece in enumerate(pieces):
+
+            @pl.when(wanted == number)
             def _():
-                pltpu.make_async_copy(same[k], outs[turn], sems.at[turn]).start()
-
-            @pl.when((distance == k) & jnp.logical_not(mine))
-            def _():
-                pltpu.make_async_copy(other[k], outs[turn], sems.at[turn]).start()
-
-    for turn in range(TURNS):
-        pltpu.make_async_copy(same[0], outs[turn], sems.at[turn]).wait()
+                outs[turn][...] = piece[...]
 
 
 def pick_turns(owner_order, same, other):
@@ -92,9 +87,8 @@
     return pl.pallas_call(
         functools.partial(pick_kernel, chips),
         out_shape=[piece] * TURNS,
-        in_specs=[SMEM] + [ANY] * (2 * chips),
+        in_specs=[SMEM] + [VMEM] * (2 * chips),
         out_specs=[VMEM] * TURNS,
-        scratch_shapes=[pltpu.SemaphoreType.DMA((TURNS,))],
         compiler_params=pltpu.CompilerParams(vmem_limit_bytes=GRANT),
         name="pick",
     )(owner_order, *same, *other)
@@ -133,31 +127,28 @@
 
 
 def turn_kernel(turns, chips, parts, last, *refs):
-    count = len(turns)
     refs = list(refs)
     residual_ref, coefs_ref = refs.pop(0), refs.pop(0)
-    pieces = [[refs.pop(0) for _ in range(2 * chips)] for _ in turns]
+    number = 1 + len(hops(0, chips))
+    pieces = [[[refs.pop(0) for _ in range(number)] for _ in range(2)] for _ in turns]
     residual_out = None if last else refs.pop(0)
     sends = [refs.pop(0) for _ in range(parts)]
     values, held = refs
 
     chip, core = place_of_device()
     slot = lax.axis_index("point")
-    rows, half = pieces[0][0].shape
+    rows, half = pieces[0][0][0].shape
     kb = rows * chips
     local_kb = kb // parts
     sides = [pl.ds(pl.multiple_of(which * half, half), half) for which in (core, 1 - core)]
-    tops = [pl.multiple_of((chip ^ k) * rows, rows) for k in range(chips)]
+    across = lambda left, right: lax.dot_general(
+        left, right, (((1,), (1,)), ((), ())), preferred_element_type=jnp.float32
+    )
 
     source = residual_ref
     for position, turn in enumerate(turns):
-        halves = [
-            jnp.concatenate([piece[...] for piece in pieces[position][side * chips : (side + 1) * chips]], axis=0)
-            for side in range(2)
-        ]
-        across = lambda left, right: lax.dot_general(
-            left, right, (((1,), (1,)), ((), ())), preferred_element_type=jnp.float32
-        )
+        tops = [pl.multiple_of((chip ^ k) * rows, rows) for k in distances(turn, chips)]
+        halves = [jnp.concatenate([piece[...] for piece in side], axis=0) for side in pieces[position]]
         gram = across(halves[0], halves[0]) + across(halves[1], halves[1])
         step = 1.0 / jnp.sum(jnp.abs(gram), axis=1, keepdims=True)
         correlation = across(halves[0], source[:, sides[0]]) + across(halves[1], source[:, sides[1]])
@@ -169,7 +160,7 @@
         for k in range(chips):
             values[pl.ds(tops[k], rows), :] = change[k * rows : (k + 1) * rows, :]
         if turn + 1 < TURNS:
-            target = residual_out if position + 1 == count else held
+            target = residual_out if position + 1 == len(turns) else held
             for side, part in zip(sides, halves):
                 moved = lax.dot_general(
                     change, part, (((0,), (0,)), ((), ())), preferred_element_type=jnp.float32
@@ -183,16 +174,13 @@
             ]
 
 
-def run_turns(turns, residual, coefs, pieces, parts):
+def run_turns(turns, chips, residual, coefs, pieces, parts):
     count = len(turns)
     last = turns[-1] + 1 == TURNS
-    chips = len(pieces[0]) // 2
-    rows, _ = pieces[0][0].shape
     points, features = residual.shape
-    kb = rows * chips
-    local_kb = kb // parts
-    send = jax.ShapeDtypeStruct((count * local_kb, points), jnp.bfloat16)
-    flat = [piece for turn in pieces for piece in turn]
+    kb = coefs.shape[0] // TURNS
+    send = jax.ShapeDtypeStruct((count * kb // parts, points), jnp.bfloat16)
+    flat = [piece for turn in pieces for side in turn for piece in side]
     first = [] if last else [jax.ShapeDtypeStruct(residual.shape, residual.dtype)]
     flops = count * 2 * kb * features * (kb + 2 * points)
     outs = pl.pallas_call(
@@ -242,24 +230,16 @@
     return news
 
 
-def map_kernel(turns, parts, local_kb, first, *refs):
-    count = len(turns)
-    refs = list(refs)
-    changes = [refs.pop(0) for _ in range(parts)]
-    coefs = [refs.pop(0) for _ in range(parts)]
-    if not first:
-        refs.pop(0)
-    out_ref, grids, staged, sem = refs
-    rows = grids.shape[0]
-    height = count * local_kb
-    top = turns[0] * local_kb
-    before = jnp.concatenate([ref[top : top + height, :] for ref in coefs], axis=1)
-    values = jnp.concatenate([before, jnp.concatenate([ref[...] for ref in changes], axis=1)], axis=0)
-    depth, half = TURNS * local_kb, TILE_ROWS // 2
+def targets_of(coefs):
+    half = TILE_ROWS // 2
+    depth = coefs[0].shape[0] - TILE_ROWS
     where = [ref[depth:, :].astype(jnp.float32) for ref in coefs]
     row = jnp.concatenate([value[:1] for value in where], axis=1)
     lane = jnp.concatenate([value[half : half + 1] for value in where], axis=1)
-    targets = (row * MAP_W + lane).astype(jnp.int32)
+    return (row * MAP_W + lane).astype(jnp.int32)
+
+
+def place(values, targets, rows, put):
     pair = 2 if rows % 2 == 0 else 1
     pixel = lax.broadcasted_iota(jnp.int32, (pair * MAP_W, targets.shape[1]), 0)
     for r in range(0, rows, pair):
@@ -267,11 +247,56 @@
         moved = lax.dot_general(
             values, chosen, (((1,), (1,)), ((), ())), preferred_element_type=jnp.float32
         )
-        total = moved[:height] + moved[height:]
         for i in range(pair):
-            grids[r + i] = total[:, i * MAP_W : (i + 1) * MAP_W]
+            put(r + i, moved[:, i * MAP_W : (i + 1) * MAP_W])
+
+
+def place_kernel(*refs):
+    coefs, base = refs[:-1], refs[-1]
+    depth = coefs[0].shape[0] - TILE_ROWS
+    values = jnp.concatenate([ref[:depth, :] for ref in coefs], axis=1)
+
+    def put(r, value):
+        base[r] = value
+
+    place(values, targets_of(coefs), base.shape[0], put)
+
+
+def place_coefs(coefs):
+    rows = len(coefs) * coefs[0].shape[1] // MAP_W
+    depth = coefs[0].shape[0] - TILE_ROWS
+    return pl.pallas_call(
+        place_kernel,
+        out_shape=jax.ShapeDtypeStruct((rows, depth, MAP_W), jnp.float32),
+        in_specs=[VMEM] * len(coefs),
+        out_specs=VMEM,
+        cost_estimate=pl.CostEstimate(
+            flops=2 * depth * (rows * MAP_W) ** 2, bytes_accessed=8 * depth * rows * MAP_W, transcendentals=0
+        ),
+        compiler_params=pltpu.CompilerParams(vmem_limit_bytes=GRANT),
+        name="place",
+    )(*coefs)
+
+
+def map_kernel(turns, parts, local_kb, first, *refs):
+    count = len(turns)
+    refs = list(refs)
+    changes = [refs.pop(0) for _ in range(parts)]
+    coefs = [refs.pop(0) for _ in range(parts)]
+    base = refs.pop(0)
+    if not first:
+        refs.pop(0)
+    out_ref, grids, staged, sem = refs
+    rows = grids.shape[0]
+    height = count * local_kb
+    top = turns[0] * local_kb
+
+    def put(r, value):
+        grids[r] = base[r, top : top + height, :] + value
+
+    place(jnp.concatenate([ref[...] for ref in changes], axis=1), targets_of(coefs), rows, put)
     groups = height // SUBLANES
-    together = UNROLL if groups % UNROLL == 0 and rows * UNROLL <= 32 else 1
+    together = UNROLL if groups % UNROLL == 0 and rows * UNROLL <= 64 else 1
     chunk = together * SUBLANES * rows
     start = turns[0] * local_kb * rows
 
@@ -297,7 +322,7 @@
     pltpu.make_async_copy(staged, out_ref.at[pl.ds(start, height * rows)], sem).wait()
 
 
-def run_maps(turns, changes, coefs, buffer):
+def run_maps(turns, changes, coefs, base, buffer):
     parts = len(changes)
     count, points = len(turns), changes[0].shape[1]
     local_kb = changes[0].shape[0] // count
@@ -308,31 +333,25 @@
     return pl.pallas_call(
         functools.partial(map_kernel, turns, parts, local_kb, first),
         out_shape=jax.ShapeDtypeStruct((TURNS * local_kb * rows, MAP_W), jnp.float32),
-        in_specs=[VMEM] * (2 * parts) + [ANY] * len(extra),
+        in_specs=[VMEM] * (2 * parts + 1) + [ANY] * len(extra),
         out_specs=ANY,
         scratch_shapes=[
             pltpu.VMEM((rows, height, MAP_W), jnp.float32),
             pltpu.VMEM((height * rows, MAP_W), jnp.float32),
             pltpu.SemaphoreType.DMA,
         ],
-        input_output_aliases={} if first else {2 * parts: 0},
+        input_output_aliases={} if first else {2 * parts + 1: 0},
         cost_estimate=pl.CostEstimate(
-            flops=4 * height * (parts * points) ** 2,
+            flops=2 * height * (parts * points) ** 2,
             bytes_accessed=8 * height * parts * points,
             transcendentals=0,
         ),
         compiler_params=pltpu.CompilerParams(vmem_limit_bytes=GRANT),
-    )(*changes, *coefs, *extra)
+    )(*changes, *coefs, base, *extra)
 
 
 def exchange(value, axis, size, distance):
     return lax.ppermute(value, axis, [(i, i ^ distance) for i in range(size)])
-
-
-def hop(turn, k):
-    low = k & -k
-    high = 1 << (k.bit_length() - 1)
-    return high if turn % 2 == 0 else low
 
 
 def per_device(fields, parts, residual_in, coefs_in, dictionary, owner_order, pixel_of):
@@ -350,21 +369,22 @@
     other = [got[0]] + [over_chips(got[k], k) for k in range(1, chips)]
     laid, turned = lay_coefs(coefs, pixel_of.reshape(1, points), parts)
     laid = [laid[0]] + [over_points(laid[m], m) for m in range(1, parts)]
+    base = place_coefs(laid)
     chosen = pick_turns(owner_order, same, other)
 
     def gather(turn):
         held = [chosen[turn]]
-        for k in range(1, chips):
-            bit = hop(turn, k)
-            held.append(over_chips(held[k ^ bit], bit))
-        return held + [over_cores(value) for value in held]
+        for step, bit in enumerate(hops(turn, chips)):
+            whole = held[0] if step == 0 else jnp.concatenate(held, axis=0)
+            held.append(over_chips(whole, bit))
+        return [held, [over_cores(value) for value in held]]
 
     buffer = None
     for turns in GROUPS:
         pieces = [gather(turn) for turn in turns]
-        residual, sends = run_turns(turns, residual, turned, pieces, parts)
+        residual, sends = run_turns(turns, chips, residual, turned, pieces, parts)
         changes = [sends[0]] + [over_points(sends[m], m) for m in range(1, parts)]
-        buffer = run_maps(turns, changes, laid, buffer)
+        buffer = run_maps(turns, changes, laid, base, buffer)
     rows = parts * points // MAP_W
     return buffer.reshape(1, TURNS, -1, rows, MAP_W)
 

time: 82.5 us -> 78.6 us (0.953)
  starting transfers between devices: 44.4 us -> 36.9 us
  waiting for transfers between devices: 21.1 us -> 27 us
  Pallas kernels: 14.6 us -> 12.3 us
    ppermute x47 -> x39, starting transfers between devices: 44.4 us -> 36.9 us  [exchange(): return lax.ppermute(value, axis, [(i, i ^ distance) for i in range(size)])]
    ppermute x47 -> x39, waiting for transfers between devices: 21.1 us -> 27 us  [exchange(): return lax.ppermute(value, axis, [(i, i ^ distance) for i in range(size)])]
    pallas_call x2, Pallas kernels: 8.36 us -> 6.17 us  [run_maps(): pl.pallas_call(functools.partial(map_kernel, turns, parts, local_kb, firs...]
  transfers between devices with their start and end apart: 47 -> 39, of which waited for: 13 -> 14; matrix products, arithmetic and copies ran while one was open for 0% -> 0% of each run, Pallas kernels for 12% -> 11%
where the time goes in v3:
time: 78.6 us; the launch traced here: 78.4 us
  starting transfers between devices  36.9 us (47%)
  waiting for transfers between devices  27 us (34%)
  Pallas kernels  12.3 us (16%)
  local copies, waits for them, and re-layouts  2 us (3%)
    ppermute x39, starting transfers between devices, exchange(): return lax.ppermute(value, axis, [(i, i ^ distance) for i in range(size)])  36.9 us
    ppermute x39, waiting for transfers between devices, exchange(): return lax.ppermute(value, axis, [(i, i ^ distance) for i in range(size)])  27 us
    pallas_call x2, Pallas kernels, run_maps(): pl.pallas_call(functools.partial(map_kernel, turns, parts, local_kb, firs...  6.17 us
    pallas_call x2, Pallas kernels, run_turns(): pl.pallas_call(functools.partial(turn_kernel, turns, chips, parts, last),...  4.28 us
    unnamed x11, local copies, waits for them, and re-layouts  2 us
  transfers between devices with their start and end apart: 39, of which 14 were waited for; matrix products, arithmetic and copies ran while one was open for 0% of the time, Pallas kernels for 11%

profile of v3, /device:TPU:0, one launch (start us, length us, event | category | flops | bytes accessed | tf_op | source)
XLA Modules:
  0.0 78.4 jit_solution(13650700727546129953)
XLA Ops:
  0.0 1.2 %copy-done = bf16[256,2048]{1,0:T(8,128)(2,1)S(1)} copy-done((bf16[256,2048]{1,0:T(8,128)(2,1)S(1)}, bf16[256,2048]{1,0:T(8,128)(2,1)}, u32[]{:S(2)}) %copy-start) | copy-done | bytes 1048600
  1.3 3.0 %collective-permute-start = (bf16[64,1024]{1,0:T(8,128)(2,1)S(1)}, bf16[64,1024]{1,0:T(8,128)(2,1)S(1)}, u32[]{:S(2)}, u32[]{:S(2)}) collective-permute-start(bf16[64,1024]{1,0:T(8,128)(2,1)S(1)} %get-tuple-element.33), channel_id=1, source_target_pairs={{0,8},{4,12},{8,0},{12,4},{16,24},{20,28},{24,16},{28,20},{1,9},{5... | collective-permute-start | bytes 393224 | tf_op jit(solution)/shard_map/ppermute | solution.py:354
  4.3 1.5 %collective-permute-start.1 = (bf16[64,1024]{1,0:T(8,128)(2,1)S(1)}, bf16[64,1024]{1,0:T(8,128)(2,1)S(1)}, u32[]{:S(2)}, u32[]{:S(2)}) collective-permute-start(bf16[64,1024]{1,0:T(8,128)(2,1)S(1)} %get-tuple-element.34), channel_id=1, source_target_pairs={{0,16},{4,20},{8,24},{12,28},{16,0},{20,4},{24,8},{28,12},{1,17},{... | collective-permute-start | bytes 393224 | tf_op jit(solution)/shard_map/ppermute | solution.py:354
  5.9 0.5 collective-permute-start.6
  6.4 1.5 %collective-permute-done.refs_1_ = bf16[64,1024]{1,0:T(8,128)(2,1)S(1)} collective-permute-done((bf16[64,1024]{1,0:T(8,128)(2,1)S(1)}, bf16[64,1024]{1,0:T(8,128)(2,1)S(1)}, u32[]{:S(2)}, u32[]{:S(2)}) %collective-permute-start) | collective-permute-done | bytes 131104 | tf_op jit(solution)/shard_map/ppermute | solution.py:354
  7.8 2.7 %collective-permute-start.2 = (bf16[64,1024]{1,0:T(8,128)(2,1)S(1)}, bf16[64,1024]{1,0:T(8,128)(2,1)S(1)}, u32[]{:S(2)}, u32[]{:S(2)}) collective-permute-start(bf16[64,1024]{1,0:T(8,128)(2,1)S(1)} %get-tuple-element.35), channel_id=1, source_target_pairs={{0,24},{4,28},{8,16},{12,20},{16,8},{20,12},{24,0},{28,4},{1,25},{... | collective-permute-start | bytes 393224 | tf_op jit(solution)/shard_map/ppermute | solution.py:354
  10.5 0.6 collective-permute-start.5
  11.1 0.3 collective-permute-start.7
  11.4 2.7 %collective-permute-start.9 = (bf16[64,1024]{1,0:T(8,128)(2,1)S(1)}, bf16[64,1024]{1,0:T(8,128)(2,1)S(1)}, u32[]{:S(2)}, u32[]{:S(2)}) collective-permute-start(bf16[64,1024]{1,0:T(8,128)(2,1)S(1)} %collective-permute-done.8), channel_id=1, source_target_pairs={{0,24},{4,28},{8,16},{12,20},{16,8},{20,12},{24,0},{28,4},{1,25},{... | collective-permute-start | bytes 393224 | tf_op jit(solution)/shard_map/ppermute | solution.py:354
  14.1 0.2 collective-permute-done.2.refs_3_
  14.3 2.8 %collective-permute-done.5.refs_5_ = bf16[64,1024]{1,0:T(8,128)(2,1)S(1)} collective-permute-done((bf16[64,1024]{1,0:T(8,128)(2,1)S(1)}, bf16[64,1024]{1,0:T(8,128)(2,1)S(1)}, u32[]{:S(2)}, u32[]{:S(2)}) %collective-permute-start.5) | collective-permute-done | bytes 131104 | tf_op jit(solution)/shard_map/ppermute | solution.py:354
  17.2 2.3 %collective-permute-done.7.refs_6_ = bf16[64,1024]{1,0:T(8,128)(2,1)S(1)} collective-permute-done((bf16[64,1024]{1,0:T(8,128)(2,1)S(1)}, bf16[64,1024]{1,0:T(8,128)(2,1)S(1)}, u32[]{:S(2)}, u32[]{:S(2)}) %collective-permute-start.7) | collective-permute-done | bytes 131104 | tf_op jit(solution)/shard_map/ppermute | solution.py:354
  19.5 0.8 pick.1
  20.3 2.3 %collective-permute-start.10 = (bf16[64,1024]{1,0:T(8,128)(2,1)S(1)}, bf16[64,1024]{1,0:T(8,128)(2,1)S(1)}, u32[]{:S(2)}, u32[]{:S(2)}) collective-permute-start(bf16[64,1024]{1,0:T(8,128)(2,1)S(1)} %get-tuple-element.40.refs_2_), channel_id=1, source_target_pairs={{0,8},{4,12},{8,0},{12,4},{16,24},{20,28},{24,16},{28,20},{1,9},{5... | collective-permute-start | bytes 393224 | tf_op jit(solution)/shard_map/ppermute | solution.py:354
  22.6 1.0 %collective-permute-start.15 = (bf16[64,1024]{1,0:T(8,128)(2,1)S(1)}, bf16[64,1024]{1,0:T(8,128)(2,1)S(1)}, u32[]{:S(2)}, u32[]{:S(2)}) collective-permute-start(bf16[64,1024]{1,0:T(8,128)(2,1)S(1)} %get-tuple-element.41.refs_8_), channel_id=1, source_target_pairs={{0,16},{4,20},{8,24},{12,28},{16,0},{20,4},{24,8},{28,12},{1,17},{... | collective-permute-start | bytes 393224 | tf_op jit(solution)/shard_map/ppermute | solution.py:354
  23.7 0.7 copy-done.1
  24.3 0.3 lay.1
  24.6 1.7 %collective-permute-start.33 = (bf16[272,256]{1,0:T(8,128)(2,1)S(1)}, bf16[272,256]{1,0:T(8,128)(2,1)S(1)}, u32[]{:S(2)}, u32[]{:S(2)}) collective-permute-start(bf16[272,256]{1,0:T(8,128)(2,1)S(1)} %get-tuple-element.50), channel_id=1, source_target_pairs={{0,1},{1,0},{2,3},{3,2},{4,5},{5,4},{6,7},{7,6},{8,9},{9,8},{10,11... | collective-permute-start | bytes 417800 | tf_op jit(solution)/shard_map/ppermute | solution.py:354
  26.3 0.5 collective-permute-start.17
  26.8 0.9 %collective-permute-start.20 = (bf16[64,1024]{1,0:T(8,128)(2,1)S(1)}, bf16[64,1024]{1,0:T(8,128)(2,1)S(1)}, u32[]{:S(2)}, u32[]{:S(2)}) collective-permute-start(bf16[64,1024]{1,0:T(8,128)(2,1)S(1)} %get-tuple-element.43.refs_2_), channel_id=1, source_target_pairs={{0,8},{4,12},{8,0},{12,4},{16,24},{20,28},{24,16},{28,20},{1,9},{5... | collective-permute-start | bytes 393224 | tf_op jit(solution)/shard_map/ppermute | solution.py:354
  27.7 0.9 %collective-permute-start.25 = (bf16[64,1024]{1,0:T(8,128)(2,1)S(1)}, bf16[64,1024]{1,0:T(8,128)(2,1)S(1)}, u32[]{:S(2)}, u32[]{:S(2)}) collective-permute-start(bf16[64,1024]{1,0:T(8,128)(2,1)S(1)} %get-tuple-element.44.refs_8_), channel_id=1, source_target_pairs={{0,16},{4,20},{8,24},{12,28},{16,0},{20,4},{24,8},{28,12},{1,17},{... | collective-permute-start | bytes 393224 | tf_op jit(solution)/shard_map/ppermute | solution.py:354
  28.6 1.1 %collective-permute-done.33.refs_1_.refs_5_ = bf16[272,256]{1,0:T(8,128)(2,1)S(1)} collective-permute-done((bf16[272,256]{1,0:T(8,128)(2,1)S(1)}, bf16[272,256]{1,0:T(8,128)(2,1)S(1)}, u32[]{:S(2)}, u32[]{:S(2)}) %collective-permute-start.33) | collective-permute-done | bytes 139296 | tf_op jit(solution)/shard_map/ppermute | solution.py:354
  29.7 1.1 %collective-permute-start.11 = (bf16[128,1024]{1,0:T(8,128)(2,1)S(1)}, bf16[128,1024]{1,0:T(8,128)(2,1)S(1)}, u32[]{:S(2)}, u32[]{:S(2)}) collective-permute-start(bf16[128,1024]{1,0:T(8,128)(2,1)S(1)} %pad_maximum_fusion), channel_id=1, source_target_pairs={{0,16},{4,20},{8,24},{12,28},{16,0},{20,4},{24,8},{28,12},{1,17},{... | collective-permute-start | bytes 786440 | tf_op jit(solution)/shard_map/ppermute | solution.py:354
  30.8 1.5 %collective-permute-done.20.refs_3_ = bf16[64,1024]{1,0:T(8,128)(2,1)S(1)} collective-permute-done((bf16[64,1024]{1,0:T(8,128)(2,1)S(1)}, bf16[64,1024]{1,0:T(8,128)(2,1)S(1)}, u32[]{:S(2)}, u32[]{:S(2)}) %collective-permute-start.20) | collective-permute-done | bytes 131104 | tf_op jit(solution)/shard_map/ppermute | solution.py:354
  32.2 0.4 collective-permute-start.16
  32.8 1.4 %collective-permute-done.25.refs_9_ = bf16[64,1024]{1,0:T(8,128)(2,1)S(1)} collective-permute-done((bf16[64,1024]{1,0:T(8,128)(2,1)S(1)}, bf16[64,1024]{1,0:T(8,128)(2,1)S(1)}, u32[]{:S(2)}, u32[]{:S(2)}) %collective-permute-start.25) | collective-permute-done | bytes 131104 | tf_op jit(solution)/shard_map/ppermute | solution.py:354
  34.2 0.8 %collective-permute-start.21 = (bf16[128,1024]{1,0:T(8,128)(2,1)S(1)}, bf16[128,1024]{1,0:T(8,128)(2,1)S(1)}, u32[]{:S(2)}, u32[]{:S(2)}) collective-permute-start(bf16[128,1024]{1,0:T(8,128)(2,1)S(1)} %pad_maximum_fusion.2), channel_id=1, source_target_pairs={{0,16},{4,20},{8,24},{12,28},{16,0},{20,4},{24,8},{28,12},{1,17},{... | collective-permute-start | bytes 786440 | tf_op jit(solution)/shard_map/ppermute | solution.py:354
  35.0 1.3 %collective-permute-start.26 = (bf16[128,1024]{1,0:T(8,128)(2,1)S(1)}, bf16[128,1024]{1,0:T(8,128)(2,1)S(1)}, u32[]{:S(2)}, u32[]{:S(2)}) collective-permute-start(bf16[128,1024]{1,0:T(8,128)(2,1)S(1)} %pad_maximum_fusion.3), channel_id=1, source_target_pairs={{0,8},{4,12},{8,0},{12,4},{16,24},{20,28},{24,16},{28,20},{1,9},{5... | collective-permute-start | bytes 786440 | tf_op jit(solution)/shard_map/ppermute | solution.py:354
  36.4 3.4 %collective-permute-done.11.refs_4_ = bf16[128,1024]{1,0:T(8,128)(2,1)S(1)} collective-permute-done((bf16[128,1024]{1,0:T(8,128)(2,1)S(1)}, bf16[128,1024]{1,0:T(8,128)(2,1)S(1)}, u32[]{:S(2)}, u32[]{:S(2)}) %collective-permute-start.11) | collective-permute-done | bytes 262176 | tf_op jit(solution)/shard_map/ppermute | solution.py:354
  39.8 1.6 %collective-permute-done.16.refs_10_ = bf16[128,1024]{1,0:T(8,128)(2,1)S(1)} collective-permute-done((bf16[128,1024]{1,0:T(8,128)(2,1)S(1)}, bf16[128,1024]{1,0:T(8,128)(2,1)S(1)}, u32[]{:S(2)}, u32[]{:S(2)}) %collective-permute-start.16) | collective-permute-done | bytes 262176 | tf_op jit(solution)/shard_map/ppermute | solution.py:354
  41.4 0.5 collective-permute-start.18
  41.9 1.8 %collective-permute-done.21.refs_4_ = bf16[128,1024]{1,0:T(8,128)(2,1)S(1)} collective-permute-done((bf16[128,1024]{1,0:T(8,128)(2,1)S(1)}, bf16[128,1024]{1,0:T(8,128)(2,1)S(1)}, u32[]{:S(2)}, u32[]{:S(2)}) %collective-permute-start.21) | collective-permute-done | bytes 262176 | tf_op jit(solution)/shard_map/ppermute | solution.py:354
  43.7 1.6 %collective-permute-done.26.refs_10_ = bf16[128,1024]{1,0:T(8,128)(2,1)S(1)} collective-permute-done((bf16[128,1024]{1,0:T(8,128)(2,1)S(1)}, bf16[128,1024]{1,0:T(8,128)(2,1)S(1)}, u32[]{:S(2)}, u32[]{:S(2)}) %collective-permute-start.26) | collective-permute-done | bytes 262176 | tf_op jit(solution)/shard_map/ppermute | solution.py:354
  45.3 0.5 collective-permute-start.27
  45.9 0.4 collective-permute-start.28
  46.3 2.4 %shard_map.55 = (bf16[256,2048]{1,0:T(8,128)(2,1)S(1)}, bf16[128,256]{1,0:T(8,128)(2,1)S(1)}, bf16[128,256]{1,0:T(8,128)(2,1)S(1)}, bf16[128,256]{1,0:T(8,128)(2,1)S(1)}, bf16[128,256]{1,0:T(8,128)(2,1)S(1)}) custom-call(bf16[256,2048]{1,0:T(8,128)(2,1)S(1)} %bitcast.6, bf16[1024,256]{1,0:T(8,128)(2,1)S(1)} %get-tuple-element.31.refs_1_, ...), custom_call_target="tpu_custom_call" | custom-call | flops 1610612736 | bytes 4194304 | tf_op jit(solution)/shard_map/pallas_call | solution.py:186
  48.7 2.7 %collective-permute-start.34 = (bf16[272,256]{1,0:T(8,128)(2,1)S(1)}, bf16[272,256]{1,0:T(8,128)(2,1)S(1)}, u32[]{:S(2)}, u32[]{:S(2)}) collective-permute-start(bf16[272,256]{1,0:T(8,128)(2,1)S(1)} %get-tuple-element.51), channel_id=1, source_target_pairs={{0,2},{1,3},{2,0},{3,1},{4,6},{5,7},{6,4},{7,5},{8,10},{9,11},{10,... | collective-permute-start | bytes 417800 | tf_op jit(solution)/shard_map/ppermute | solution.py:354
  51.4 0.9 %collective-permute-start.36 = (bf16[128,256]{1,0:T(8,128)(2,1)S(1)}, bf16[128,256]{1,0:T(8,128)(2,1)S(1)}, u32[]{:S(2)}, u32[]{:S(2)}) collective-permute-start(bf16[128,256]{1,0:T(8,128)(2,1)S(1)} %get-tuple-element.54), channel_id=1, source_target_pairs={{0,1},{1,0},{2,3},{3,2},{4,5},{5,4},{6,7},{7,6},{8,9},{9,8},{10,11... | collective-permute-start | bytes 196616 | tf_op jit(solution)/shard_map/ppermute | solution.py:354
  52.3 3.5 %collective-permute-start.37 = (bf16[128,256]{1,0:T(8,128)(2,1)S(1)}, bf16[128,256]{1,0:T(8,128)(2,1)S(1)}, u32[]{:S(2)}, u32[]{:S(2)}) collective-permute-start(bf16[128,256]{1,0:T(8,128)(2,1)S(1)} %get-tuple-element.55), channel_id=1, source_target_pairs={{0,2},{1,3},{2,0},{3,1},{4,6},{5,7},{6,4},{7,5},{8,10},{9,11},{10,... | collective-permute-start | bytes 196616 | tf_op jit(solution)/shard_map/ppermute | solution.py:354
  55.8 1.9 %shard_map.56 = (bf16[128,256]{1,0:T(8,128)(2,1)S(1)}, bf16[128,256]{1,0:T(8,128)(2,1)S(1)}, bf16[128,256]{1,0:T(8,128)(2,1)S(1)}, bf16[128,256]{1,0:T(8,128)(2,1)S(1)}) custom-call(bf16[256,2048]{1,0:T(8,128)(2,1)S(1)} %get-tuple-element.42.refs_0_, bf16[1024,256]{1,0:T(8,128)(2,1)S(1)} %get-tuple-element.31.refs_1_, ...), custom_call_target="tpu_custom_call" | custom-call | flops 1610612736 | bytes 4194304 | tf_op jit(solution)/shard_map/pallas_call | solution.py:186
  57.8 6.1 %collective-permute-done.34.refs_2_.refs_6_ = bf16[272,256]{1,0:T(8,128)(2,1)S(1)} collective-permute-done((bf16[272,256]{1,0:T(8,128)(2,1)S(1)}, bf16[272,256]{1,0:T(8,128)(2,1)S(1)}, u32[]{:S(2)}, u32[]{:S(2)}) %collective-permute-start.34) | collective-permute-done | bytes 139296 | tf_op jit(solution)/shard_map/ppermute | solution.py:354
  63.8 0.6 collective-permute-start.30
  64.4 4.9 %collective-permute-start.31 = (bf16[128,256]{1,0:T(8,128)(2,1)S(1)}, bf16[128,256]{1,0:T(8,128)(2,1)S(1)}, u32[]{:S(2)}, u32[]{:S(2)}) collective-permute-start(bf16[128,256]{1,0:T(8,128)(2,1)S(1)} %get-tuple-element.47), channel_id=1, source_target_pairs={{0,2},{1,3},{2,0},{3,1},{4,6},{5,7},{6,4},{7,5},{8,10},{9,11},{10,... | collective-permute-start | bytes 196616 | tf_op jit(solution)/shard_map/ppermute | solution.py:354
  69.3 0.4 collective-permute-start.32
  69.7 0.8 place.1.refs_8_
  70.5 3.1 %shard_map.57.refs_9_ = f32[2048,128]{1,0:T(8,128)} custom-call(bf16[128,256]{1,0:T(8,128)(2,1)S(1)} %get-tuple-element.53.refs_0_, bf16[128,256]{1,0:T(8,128)(2,1)S(1)} %collective-permute-done.36.refs_1_, bf16[128,256]{1,0:T(8,128)(2,1)S(1)} %collective-permute-done.37.refs_2_, bf16[128,256]{1,0:T(8,128)(2,1)S(1)} %collective-permute-done.38.refs_3_, ...), custom_call_target="tpu_custom_call" | custom-call | flops 268435456 | bytes 1048576 | tf_op jit(solution)/shard_map/pallas_call | solution.py:333
  73.8 1.6 %collective-permute-done.32.refs_3_ = bf16[128,256]{1,0:T(8,128)(2,1)S(1)} collective-permute-done((bf16[128,256]{1,0:T(8,128)(2,1)S(1)}, bf16[128,256]{1,0:T(8,128)(2,1)S(1)}, u32[]{:S(2)}, u32[]{:S(2)}) %collective-permute-start.32) | collective-permute-done | bytes 65568 | tf_op jit(solution)/shard_map/ppermute | solution.py:354
  75.4 3.1 %shard_map.58 = f32[2048,128]{1,0:T(8,128)} custom-call(bf16[128,256]{1,0:T(8,128)(2,1)S(1)} %get-tuple-element.45.refs_0_, bf16[128,256]{1,0:T(8,128)(2,1)S(1)} %collective-permute-done.30.refs_1_, bf16[128,256]{1,0:T(8,128)(2,1)S(1)} %collective-permute-done.31.refs_2_, ...), custom_call_target="tpu_custom_call", output_to_operand_aliasing={{}: (9, {})} | custom-call | flops 268435456 | bytes 1048576 | tf_op jit(solution)/shard_map/pallas_call | solution.py:333
  (53 shorter events, 0.7 us)
Async XLA Ops:
  0.0 1.2 %copy-start = (bf16[256,2048]{1,0:T(8,128)(2,1)S(1)}, bf16[256,2048]{1,0:T(8,128)(2,1)}, u32[]{:S(2)}) copy-start(bf16[256,2048]{1,0:T(8,128)(2,1)} %block_ref.1) | copy-start | bytes 3145732
  1.3 6.5 %collective-permute-start = (bf16[64,1024]{1,0:T(8,128)(2,1)S(1)}, bf16[64,1024]{1,0:T(8,128)(2,1)S(1)}, u32[]{:S(2)}, u32[]{:S(2)}) collective-permute-start(bf16[64,1024]{1,0:T(8,128)(2,1)S(1)} %get-tuple-element.33), channel_id=1, source_target_pairs={{0,8},{4,12},{8,0},{12,4},{16,24},{20,28},{24,16},{28,20},{1,9},{5... | collective-permute-start | bytes 393224 | tf_op jit(solution)/shard_map/ppermute | solution.py:354
  4.3 6.2 %collective-permute-start.1 = (bf16[64,1024]{1,0:T(8,128)(2,1)S(1)}, bf16[64,1024]{1,0:T(8,128)(2,1)S(1)}, u32[]{:S(2)}, u32[]{:S(2)}) collective-permute-start(bf16[64,1024]{1,0:T(8,128)(2,1)S(1)} %get-tuple-element.34), channel_id=1, source_target_pairs={{0,16},{4,20},{8,24},{12,28},{16,0},{20,4},{24,8},{28,12},{1,17},{... | collective-permute-start | bytes 393224 | tf_op jit(solution)/shard_map/ppermute | solution.py:354
  5.8 4.7 %collective-permute-start.4 = (bf16[64,1024]{1,0:T(8,128)(2,1)S(1)}, bf16[64,1024]{1,0:T(8,128)(2,1)S(1)}, u32[]{:S(2)}, u32[]{:S(2)}) collective-permute-start(bf16[64,1024]{1,0:T(8,128)(2,1)S(1)} %get-tuple-element.37), channel_id=1, source_target_pairs={{0,4},{4,0},{8,12},{12,8},{16,20},{20,16},{24,28},{28,24},{1,5},{5... | collective-permute-start | bytes 393224 | tf_op jit(solution)/shard_map/ppermute | solution.py:354
  5.9 5.3 %collective-permute-start.6 = (bf16[64,1024]{1,0:T(8,128)(2,1)S(1)}, bf16[64,1024]{1,0:T(8,128)(2,1)S(1)}, u32[]{:S(2)}, u32[]{:S(2)}) collective-permute-start(bf16[64,1024]{1,0:T(8,128)(2,1)S(1)} %get-tuple-element.38), channel_id=1, source_target_pairs={{0,4},{4,0},{8,12},{12,8},{16,20},{20,16},{24,28},{28,24},{1,5},{5... | collective-permute-start | bytes 393224 | tf_op jit(solution)/shard_map/ppermute | solution.py:354
  6.4 5.1 %collective-permute-start.8 = (bf16[64,1024]{1,0:T(8,128)(2,1)S(1)}, bf16[64,1024]{1,0:T(8,128)(2,1)S(1)}, u32[]{:S(2)}, u32[]{:S(2)}) collective-permute-start(bf16[64,1024]{1,0:T(8,128)(2,1)S(1)} %get-tuple-element.39), channel_id=1, source_target_pairs={{0,4},{4,0},{8,12},{12,8},{16,20},{20,16},{24,28},{28,24},{1,5},{5... | collective-permute-start | bytes 393224 | tf_op jit(solution)/shard_map/ppermute | solution.py:354
  7.8 6.5 %collective-permute-start.2 = (bf16[64,1024]{1,0:T(8,128)(2,1)S(1)}, bf16[64,1024]{1,0:T(8,128)(2,1)S(1)}, u32[]{:S(2)}, u32[]{:S(2)}) collective-permute-start(bf16[64,1024]{1,0:T(8,128)(2,1)S(1)} %get-tuple-element.35), channel_id=1, source_target_pairs={{0,24},{4,28},{8,16},{12,20},{16,8},{20,12},{24,0},{28,4},{1,25},{... | collective-permute-start | bytes 393224 | tf_op jit(solution)/shard_map/ppermute | solution.py:354
  10.5 9.0 %copy-start.2 = (s32[8]{0:T(128)S(1)}, s32[8]{0:T(128)}, u32[]{:S(2)}) copy-start(s32[8]{0:T(128)} %order_ref.1) | copy-start | bytes 100
  10.5 3.8 %collective-permute-start.3 = (bf16[64,1024]{1,0:T(8,128)(2,1)S(1)}, bf16[64,1024]{1,0:T(8,128)(2,1)S(1)}, u32[]{:S(2)}, u32[]{:S(2)}) collective-permute-start(bf16[64,1024]{1,0:T(8,128)(2,1)S(1)} %get-tuple-element.36), channel_id=1, source_target_pairs={{0,4},{4,0},{8,12},{12,8},{16,20},{20,16},{24,28},{28,24},{1,5},{5... | collective-permute-start | bytes 393224 | tf_op jit(solution)/shard_map/ppermute | solution.py:354
  10.5 6.6 %collective-permute-start.5 = (bf16[64,1024]{1,0:T(8,128)(2,1)S(1)}, bf16[64,1024]{1,0:T(8,128)(2,1)S(1)}, u32[]{:S(2)}, u32[]{:S(2)}) collective-permute-start(bf16[64,1024]{1,0:T(8,128)(2,1)S(1)} %collective-permute-done.4), channel_id=1, source_target_pairs={{0,8},{4,12},{8,0},{12,4},{16,24},{20,28},{24,16},{28,20},{1,9},{5... | collective-permute-start | bytes 393224 | tf_op jit(solution)/shard_map/ppermute | solution.py:354
  11.1 8.4 %collective-permute-start.7 = (bf16[64,1024]{1,0:T(8,128)(2,1)S(1)}, bf16[64,1024]{1,0:T(8,128)(2,1)S(1)}, u32[]{:S(2)}, u32[]{:S(2)}) collective-permute-start(bf16[64,1024]{1,0:T(8,128)(2,1)S(1)} %collective-permute-done.6), channel_id=1, source_target_pairs={{0,16},{4,20},{8,24},{12,28},{16,0},{20,4},{24,8},{28,12},{1,17},{... | collective-permute-start | bytes 393224 | tf_op jit(solution)/shard_map/ppermute | solution.py:354
  11.4 8.1 %collective-permute-start.9 = (bf16[64,1024]{1,0:T(8,128)(2,1)S(1)}, bf16[64,1024]{1,0:T(8,128)(2,1)S(1)}, u32[]{:S(2)}, u32[]{:S(2)}) collective-permute-start(bf16[64,1024]{1,0:T(8,128)(2,1)S(1)} %collective-permute-done.8), channel_id=1, source_target_pairs={{0,24},{4,28},{8,16},{12,20},{16,8},{20,12},{24,0},{28,4},{1,25},{... | collective-permute-start | bytes 393224 | tf_op jit(solution)/shard_map/ppermute | solution.py:354
  19.5 4.0 %copy-start.4 = (bf16[1,256,4,256]{3,2,1,0:T(4,128)(2,1)S(1)}, bf16[1,256,4,256]{3,2,1,0:T(4,128)(2,1)}, u32[]{:S(2)}) copy-start(bf16[1,256,4,256]{3,2,1,0:T(4,128)(2,1)} %param.6) | copy-start | bytes 1572868
  20.3 6.5 %collective-permute-start.10 = (bf16[64,1024]{1,0:T(8,128)(2,1)S(1)}, bf16[64,1024]{1,0:T(8,128)(2,1)S(1)}, u32[]{:S(2)}, u32[]{:S(2)}) collective-permute-start(bf16[64,1024]{1,0:T(8,128)(2,1)S(1)} %get-tuple-element.40.refs_2_), channel_id=1, source_target_pairs={{0,8},{4,12},{8,0},{12,4},{16,24},{20,28},{24,16},{28,20},{1,9},{5... | collective-permute-start | bytes 393224 | tf_op jit(solution)/shard_map/ppermute | solution.py:354
  22.6 5.1 %collective-permute-start.15 = (bf16[64,1024]{1,0:T(8,128)(2,1)S(1)}, bf16[64,1024]{1,0:T(8,128)(2,1)S(1)}, u32[]{:S(2)}, u32[]{:S(2)}) collective-permute-start(bf16[64,1024]{1,0:T(8,128)(2,1)S(1)} %get-tuple-element.41.refs_8_), channel_id=1, source_target_pairs={{0,16},{4,20},{8,24},{12,28},{16,0},{20,4},{24,8},{28,12},{1,17},{... | collective-permute-start | bytes 393224 | tf_op jit(solution)/shard_map/ppermute | solution.py:354
  23.7 0.7 copy-start.1
  24.6 5.1 %collective-permute-start.33 = (bf16[272,256]{1,0:T(8,128)(2,1)S(1)}, bf16[272,256]{1,0:T(8,128)(2,1)S(1)}, u32[]{:S(2)}, u32[]{:S(2)}) collective-permute-start(bf16[272,256]{1,0:T(8,128)(2,1)S(1)} %get-tuple-element.50), channel_id=1, source_target_pairs={{0,1},{1,0},{2,3},{3,2},{4,5},{5,4},{6,7},{7,6},{8,9},{9,8},{10,11... | collective-permute-start | bytes 417800 | tf_op jit(solution)/shard_map/ppermute | solution.py:354
  26.2 6.4 %collective-permute-start.12 = (bf16[64,1024]{1,0:T(8,128)(2,1)S(1)}, bf16[64,1024]{1,0:T(8,128)(2,1)S(1)}, u32[]{:S(2)}, u32[]{:S(2)}) collective-permute-start(bf16[64,1024]{1,0:T(8,128)(2,1)S(1)} %get-tuple-element.40.refs_2_), channel_id=1, source_target_pairs={{0,4},{4,0},{8,12},{12,8},{16,20},{20,16},{24,28},{28,24},{1,5},{5... | collective-permute-start | bytes 393224 | tf_op jit(solution)/shard_map/ppermute | solution.py:354
  26.3 8.8 %collective-permute-start.17 = (bf16[64,1024]{1,0:T(8,128)(2,1)S(1)}, bf16[64,1024]{1,0:T(8,128)(2,1)S(1)}, u32[]{:S(2)}, u32[]{:S(2)}) collective-permute-start(bf16[64,1024]{1,0:T(8,128)(2,1)S(1)} %get-tuple-element.41.refs_8_), channel_id=1, source_target_pairs={{0,4},{4,0},{8,12},{12,8},{16,20},{20,16},{24,28},{28,24},{1,5},{5... | collective-permute-start | bytes 393224 | tf_op jit(solution)/shard_map/ppermute | solution.py:354
  26.8 19.6 %copy-start.3 = (bf16[1,256,2048]{2,1,0:T(8,128)(2,1)S(1)}, bf16[1,256,2048]{2,1,0:T(8,128)(2,1)}, u32[]{:S(2)}) copy-start(bf16[1,256,2048]{2,1,0:T(8,128)(2,1)} %param.5) | copy-start | bytes 3145732
  26.8 5.5 %collective-permute-start.20 = (bf16[64,1024]{1,0:T(8,128)(2,1)S(1)}, bf16[64,1024]{1,0:T(8,128)(2,1)S(1)}, u32[]{:S(2)}, u32[]{:S(2)}) collective-permute-start(bf16[64,1024]{1,0:T(8,128)(2,1)S(1)} %get-tuple-element.43.refs_2_), channel_id=1, source_target_pairs={{0,8},{4,12},{8,0},{12,4},{16,24},{20,28},{24,16},{28,20},{1,9},{5... | collective-permute-start | bytes 393224 | tf_op jit(solution)/shard_map/ppermute | solution.py:354
  27.7 6.4 %collective-permute-start.25 = (bf16[64,1024]{1,0:T(8,128)(2,1)S(1)}, bf16[64,1024]{1,0:T(8,128)(2,1)S(1)}, u32[]{:S(2)}, u32[]{:S(2)}) collective-permute-start(bf16[64,1024]{1,0:T(8,128)(2,1)S(1)} %get-tuple-element.44.refs_8_), channel_id=1, source_target_pairs={{0,16},{4,20},{8,24},{12,28},{16,0},{20,4},{24,8},{28,12},{1,17},{... | collective-permute-start | bytes 393224 | tf_op jit(solution)/shard_map/ppermute | solution.py:354
  29.7 10.1 %collective-permute-start.11 = (bf16[128,1024]{1,0:T(8,128)(2,1)S(1)}, bf16[128,1024]{1,0:T(8,128)(2,1)S(1)}, u32[]{:S(2)}, u32[]{:S(2)}) collective-permute-start(bf16[128,1024]{1,0:T(8,128)(2,1)S(1)} %pad_maximum_fusion), channel_id=1, source_target_pairs={{0,16},{4,20},{8,24},{12,28},{16,0},{20,4},{24,8},{28,12},{1,17},{... | collective-permute-start | bytes 786440 | tf_op jit(solution)/shard_map/ppermute | solution.py:354
  32.2 9.2 %collective-permute-start.16 = (bf16[128,1024]{1,0:T(8,128)(2,1)S(1)}, bf16[128,1024]{1,0:T(8,128)(2,1)S(1)}, u32[]{:S(2)}, u32[]{:S(2)}) collective-permute-start(bf16[128,1024]{1,0:T(8,128)(2,1)S(1)} %pad_maximum_fusion.1), channel_id=1, source_target_pairs={{0,8},{4,12},{8,0},{12,4},{16,24},{20,28},{24,16},{28,20},{1,9},{5... | collective-permute-start | bytes 786440 | tf_op jit(solution)/shard_map/ppermute | solution.py:354
  32.7 3.7 %collective-permute-start.22 = (bf16[64,1024]{1,0:T(8,128)(2,1)S(1)}, bf16[64,1024]{1,0:T(8,128)(2,1)S(1)}, u32[]{:S(2)}, u32[]{:S(2)}) collective-permute-start(bf16[64,1024]{1,0:T(8,128)(2,1)S(1)} %get-tuple-element.43.refs_2_), channel_id=1, source_target_pairs={{0,4},{4,0},{8,12},{12,8},{16,20},{20,16},{24,28},{28,24},{1,5},{5... | collective-permute-start | bytes 393224 | tf_op jit(solution)/shard_map/ppermute | solution.py:354
  34.2 9.5 %collective-permute-start.21 = (bf16[128,1024]{1,0:T(8,128)(2,1)S(1)}, bf16[128,1024]{1,0:T(8,128)(2,1)S(1)}, u32[]{:S(2)}, u32[]{:S(2)}) collective-permute-start(bf16[128,1024]{1,0:T(8,128)(2,1)S(1)} %pad_maximum_fusion.2), channel_id=1, source_target_pairs={{0,16},{4,20},{8,24},{12,28},{16,0},{20,4},{24,8},{28,12},{1,17},{... | collective-permute-start | bytes 786440 | tf_op jit(solution)/shard_map/ppermute | solution.py:354
  35.0 10.3 %collective-permute-start.26 = (bf16[128,1024]{1,0:T(8,128)(2,1)S(1)}, bf16[128,1024]{1,0:T(8,128)(2,1)S(1)}, u32[]{:S(2)}, u32[]{:S(2)}) collective-permute-start(bf16[128,1024]{1,0:T(8,128)(2,1)S(1)} %pad_maximum_fusion.3), channel_id=1, source_target_pairs={{0,8},{4,12},{8,0},{12,4},{16,24},{20,28},{24,16},{28,20},{1,9},{5... | collective-permute-start | bytes 786440 | tf_op jit(solution)/shard_map/ppermute | solution.py:354
  36.4 5.0 %collective-permute-start.13 = (bf16[64,1024]{1,0:T(8,128)(2,1)S(1)}, bf16[64,1024]{1,0:T(8,128)(2,1)S(1)}, u32[]{:S(2)}, u32[]{:S(2)}) collective-permute-start(bf16[64,1024]{1,0:T(8,128)(2,1)S(1)} %collective-permute-done.10.refs_3_), channel_id=1, source_target_pairs={{0,4},{4,0},{8,12},{12,8},{16,20},{20,16},{24,28},{28,24},{1,5},{5... | collective-permute-start | bytes 393224 | tf_op jit(solution)/shard_map/ppermute | solution.py:354
  39.8 6.0 %collective-permute-start.14 = (bf16[128,1024]{1,0:T(8,128)(2,1)S(1)}, bf16[128,1024]{1,0:T(8,128)(2,1)S(1)}, u32[]{:S(2)}, u32[]{:S(2)}) collective-permute-start(bf16[128,1024]{1,0:T(8,128)(2,1)S(1)} %collective-permute-done.11.refs_4_), channel_id=1, source_target_pairs={{0,4},{4,0},{8,12},{12,8},{16,20},{20,16},{24,28},{28,24},{1,5},{5... | collective-permute-start | bytes 786440 | tf_op jit(solution)/shard_map/ppermute | solution.py:354
  41.4 4.5 %collective-permute-start.19 = (bf16[128,1024]{1,0:T(8,128)(2,1)S(1)}, bf16[128,1024]{1,0:T(8,128)(2,1)S(1)}, u32[]{:S(2)}, u32[]{:S(2)}) collective-permute-start(bf16[128,1024]{1,0:T(8,128)(2,1)S(1)} %collective-permute-done.16.refs_10_), channel_id=1, source_target_pairs={{0,4},{4,0},{8,12},{12,8},{16,20},{20,16},{24,28},{28,24},{1,5},{5... | collective-permute-start | bytes 786440 | tf_op jit(solution)/shard_map/ppermute | solution.py:354
  41.4 3.9 %collective-permute-start.18 = (bf16[64,1024]{1,0:T(8,128)(2,1)S(1)}, bf16[64,1024]{1,0:T(8,128)(2,1)S(1)}, u32[]{:S(2)}, u32[]{:S(2)}) collective-permute-start(bf16[64,1024]{1,0:T(8,128)(2,1)S(1)} %collective-permute-done.15.refs_9_), channel_id=1, source_target_pairs={{0,4},{4,0},{8,12},{12,8},{16,20},{20,16},{24,28},{28,24},{1,5},{5... | collective-permute-start | bytes 393224 | tf_op jit(solution)/shard_map/ppermute | solution.py:354
  43.7 8.6 %collective-permute-start.24 = (bf16[128,1024]{1,0:T(8,128)(2,1)S(1)}, bf16[128,1024]{1,0:T(8,128)(2,1)S(1)}, u32[]{:S(2)}, u32[]{:S(2)}) collective-permute-start(bf16[128,1024]{1,0:T(8,128)(2,1)S(1)} %collective-permute-done.21.refs_4_), channel_id=1, source_target_pairs={{0,4},{4,0},{8,12},{12,8},{16,20},{20,16},{24,28},{28,24},{1,5},{5... | collective-permute-start | bytes 786440 | tf_op jit(solution)/shard_map/ppermute | solution.py:354
  45.3 10.5 %collective-permute-start.29 = (bf16[128,1024]{1,0:T(8,128)(2,1)S(1)}, bf16[128,1024]{1,0:T(8,128)(2,1)S(1)}, u32[]{:S(2)}, u32[]{:S(2)}) collective-permute-start(bf16[128,1024]{1,0:T(8,128)(2,1)S(1)} %collective-permute-done.26.refs_10_), channel_id=1, source_target_pairs={{0,4},{4,0},{8,12},{12,8},{16,20},{20,16},{24,28},{28,24},{1,5},{5... | collective-permute-start | bytes 786440 | tf_op jit(solution)/shard_map/ppermute | solution.py:354
  45.3 3.4 %collective-permute-start.27 = (bf16[64,1024]{1,0:T(8,128)(2,1)S(1)}, bf16[64,1024]{1,0:T(8,128)(2,1)S(1)}, u32[]{:S(2)}, u32[]{:S(2)}) collective-permute-start(bf16[64,1024]{1,0:T(8,128)(2,1)S(1)} %get-tuple-element.44.refs_8_), channel_id=1, source_target_pairs={{0,4},{4,0},{8,12},{12,8},{16,20},{20,16},{24,28},{28,24},{1,5},{5... | collective-permute-start | bytes 393224 | tf_op jit(solution)/shard_map/ppermute | solution.py:354
  45.8 5.6 %collective-permute-start.23 = (bf16[64,1024]{1,0:T(8,128)(2,1)S(1)}, bf16[64,1024]{1,0:T(8,128)(2,1)S(1)}, u32[]{:S(2)}, u32[]{:S(2)}) collective-permute-start(bf16[64,1024]{1,0:T(8,128)(2,1)S(1)} %collective-permute-done.20.refs_3_), channel_id=1, source_target_pairs={{0,4},{4,0},{8,12},{12,8},{16,20},{20,16},{24,28},{28,24},{1,5},{5... | collective-permute-start | bytes 393224 | tf_op jit(solution)/shard_map/ppermute | solution.py:354
  45.9 5.5 %collective-permute-start.28 = (bf16[64,1024]{1,0:T(8,128)(2,1)S(1)}, bf16[64,1024]{1,0:T(8,128)(2,1)S(1)}, u32[]{:S(2)}, u32[]{:S(2)}) collective-permute-start(bf16[64,1024]{1,0:T(8,128)(2,1)S(1)} %collective-permute-done.25.refs_9_), channel_id=1, source_target_pairs={{0,4},{4,0},{8,12},{12,8},{16,20},{20,16},{24,28},{28,24},{1,5},{5... | collective-permute-start | bytes 393224 | tf_op jit(solution)/shard_map/ppermute | solution.py:354
  48.7 15.1 %collective-permute-start.34 = (bf16[272,256]{1,0:T(8,128)(2,1)S(1)}, bf16[272,256]{1,0:T(8,128)(2,1)S(1)}, u32[]{:S(2)}, u32[]{:S(2)}) collective-permute-start(bf16[272,256]{1,0:T(8,128)(2,1)S(1)} %get-tuple-element.51), channel_id=1, source_target_pairs={{0,2},{1,3},{2,0},{3,1},{4,6},{5,7},{6,4},{7,5},{8,10},{9,11},{10,... | collective-permute-start | bytes 417800 | tf_op jit(solution)/shard_map/ppermute | solution.py:354
  51.4 13.0 %collective-permute-start.35 = (bf16[272,256]{1,0:T(8,128)(2,1)S(1)}, bf16[272,256]{1,0:T(8,128)(2,1)S(1)}, u32[]{:S(2)}, u32[]{:S(2)}) collective-permute-start(bf16[272,256]{1,0:T(8,128)(2,1)S(1)} %get-tuple-element.52), channel_id=1, source_target_pairs={{0,3},{1,2},{2,1},{3,0},{4,7},{5,6},{6,5},{7,4},{8,11},{9,10},{10,... | collective-permute-start | bytes 417800 | tf_op jit(solution)/shard_map/ppermute | solution.py:354
  51.4 17.9 %collective-permute-start.36 = (bf16[128,256]{1,0:T(8,128)(2,1)S(1)}, bf16[128,256]{1,0:T(8,128)(2,1)S(1)}, u32[]{:S(2)}, u32[]{:S(2)}) collective-permute-start(bf16[128,256]{1,0:T(8,128)(2,1)S(1)} %get-tuple-element.54), channel_id=1, source_target_pairs={{0,1},{1,0},{2,3},{3,2},{4,5},{5,4},{6,7},{7,6},{8,9},{9,8},{10,11... | collective-permute-start | bytes 196616 | tf_op jit(solution)/shard_map/ppermute | solution.py:354
  52.3 18.3 %collective-permute-start.37 = (bf16[128,256]{1,0:T(8,128)(2,1)S(1)}, bf16[128,256]{1,0:T(8,128)(2,1)S(1)}, u32[]{:S(2)}, u32[]{:S(2)}) collective-permute-start(bf16[128,256]{1,0:T(8,128)(2,1)S(1)} %get-tuple-element.55), channel_id=1, source_target_pairs={{0,2},{1,3},{2,0},{3,1},{4,6},{5,7},{6,4},{7,5},{8,10},{9,11},{10,... | collective-permute-start | bytes 196616 | tf_op jit(solution)/shard_map/ppermute | solution.py:354
  55.8 14.8 %collective-permute-start.38 = (bf16[128,256]{1,0:T(8,128)(2,1)S(1)}, bf16[128,256]{1,0:T(8,128)(2,1)S(1)}, u32[]{:S(2)}, u32[]{:S(2)}) collective-permute-start(bf16[128,256]{1,0:T(8,128)(2,1)S(1)} %get-tuple-element.56), channel_id=1, source_target_pairs={{0,3},{1,2},{2,1},{3,0},{4,7},{5,6},{6,5},{7,4},{8,11},{9,10},{10,... | collective-permute-start | bytes 196616 | tf_op jit(solution)/shard_map/ppermute | solution.py:354
  63.8 9.8 %collective-permute-start.30 = (bf16[128,256]{1,0:T(8,128)(2,1)S(1)}, bf16[128,256]{1,0:T(8,128)(2,1)S(1)}, u32[]{:S(2)}, u32[]{:S(2)}) collective-permute-start(bf16[128,256]{1,0:T(8,128)(2,1)S(1)} %get-tuple-element.46), channel_id=1, source_target_pairs={{0,1},{1,0},{2,3},{3,2},{4,5},{5,4},{6,7},{7,6},{8,9},{9,8},{10,11... | collective-permute-start | bytes 196616 | tf_op jit(solution)/shard_map/ppermute | solution.py:354
  64.4 9.4 %collective-permute-start.31 = (bf16[128,256]{1,0:T(8,128)(2,1)S(1)}, bf16[128,256]{1,0:T(8,128)(2,1)S(1)}, u32[]{:S(2)}, u32[]{:S(2)}) collective-permute-start(bf16[128,256]{1,0:T(8,128)(2,1)S(1)} %get-tuple-element.47), channel_id=1, source_target_pairs={{0,2},{1,3},{2,0},{3,1},{4,6},{5,7},{6,4},{7,5},{8,10},{9,11},{10,... | collective-permute-start | bytes 196616 | tf_op jit(solution)/shard_map/ppermute | solution.py:354
  69.3 6.1 %collective-permute-start.32 = (bf16[128,256]{1,0:T(8,128)(2,1)S(1)}, bf16[128,256]{1,0:T(8,128)(2,1)S(1)}, u32[]{:S(2)}, u32[]{:S(2)}) collective-permute-start(bf16[128,256]{1,0:T(8,128)(2,1)S(1)} %get-tuple-element.48), channel_id=1, source_target_pairs={{0,3},{1,2},{2,1},{3,0},{4,7},{5,6},{6,5},{7,4},{8,11},{9,10},{10,... | collective-permute-start | bytes 196616 | tf_op jit(solution)/shard_map/ppermute | solution.py:354

commit v4 on v3

--- a/solution.py
+++ b/solution.py
@@ -14,6 +14,7 @@
 SUBLANES = 8
 UNROLL = 8
 TILE_ROWS = 16
+SHARED_ROWS = 32
 GRANT = 16 * 1024 * 1024
 
 
@@ -43,23 +44,31 @@
     return found
 
 
+def spans(chips, rows):
+    return [rows // 2 if k & (k - 1) and rows >= SHARED_ROWS else rows for k in range(chips)]
+
+
 def slice_kernel(chips, block_ref, *refs):
     keep, give = refs[:chips], refs[chips:]
     chip, core = place_of_device()
-    rows, half = keep[0].shape
+    parity = lax.axis_index("point") % 2
+    rows, half = give[0].shape
     for k in range(chips):
-        top = pl.multiple_of((chip ^ k) * rows, rows)
         for out, which in ((keep[k], core), (give[k], 1 - core)):
+            span = out.shape[0]
+            top = (chip ^ k) * rows + (0 if span == rows else parity * span)
             left = pl.multiple_of(which * half, half)
-            out[...] = block_ref[pl.ds(top, rows), pl.ds(left, half)]
+            out[...] = block_ref[pl.ds(pl.multiple_of(top, span), span), pl.ds(left, half)]
 
 
 def cut_block(block, chips):
     kb, features = block.shape
-    piece = jax.ShapeDtypeStruct((kb // chips, features // 2), block.dtype)
+    rows = kb // chips
     outs = pl.pallas_call(
         functools.partial(slice_kernel, chips),
-        out_shape=[piece] * (2 * chips),
+        out_shape=[
+            jax.ShapeDtypeStruct((span, features // 2), block.dtype) for span in spans(chips, rows) + [rows] * chips
+        ],
         in_specs=[VMEM],
         out_specs=[VMEM] * (2 * chips),
         compiler_params=pltpu.CompilerParams(vmem_limit_bytes=GRANT),
@@ -68,30 +77,37 @@
     return outs[:chips], outs[chips:]
 
 
-def pick_kernel(chips, order_ref, *refs):
-    pieces, outs = refs[: 2 * chips], refs[2 * chips :]
+def pick_kernel(turns, counts, order_ref, *refs):
+    refs = list(refs)
+    pieces = [[refs.pop(0) for _ in range(count)] for count in counts]
+    chips = len(pieces) // 2
     chip, core = place_of_device()
-    for turn in range(TURNS):
+    parity = lax.axis_index("point") % 2
+    for position, turn in enumerate(turns):
         owner = order_ref[turn]
         wanted = ((owner // 2) ^ chip) + chips * ((owner % 2) ^ core)
         for number, piece in enumerate(pieces):
 
             @pl.when(wanted == number)
             def _():
-                outs[turn][...] = piece[...]
-
-
-def pick_turns(owner_order, same, other):
-    chips = len(same)
-    piece = jax.ShapeDtypeStruct(same[0].shape, same[0].dtype)
+                if len(piece) == 1:
+                    refs[position][...] = piece[0][...]
+                else:
+                    span = piece[0].shape[0]
+                    for part, which in zip(piece, (parity, 1 - parity)):
+                        refs[position][pl.ds(pl.multiple_of(which * span, span), span), :] = part[...]
+
+
+def pick_turns(turns, owner_order, pieces):
+    flat = [part for piece in pieces for part in piece]
+    piece = jax.ShapeDtypeStruct(pieces[0][0].shape, flat[0].dtype)
     return pl.pallas_call(
-        functools.partial(pick_kernel, chips),
-        out_shape=[piece] * TURNS,
-        in_specs=[SMEM] + [VMEM] * (2 * chips),
-        out_specs=[VMEM] * TURNS,
-        compiler_params=pltpu.CompilerParams(vmem_limit_bytes=GRANT),
-        name="pick",
-    )(owner_order, *same, *other)
+        functools.partial(pick_kernel, turns, [len(piece) for piece in pieces]),
+        out_shape=[piece] * len(turns),
+        in_specs=[SMEM] + [VMEM] * len(flat),
+        out_specs=[VMEM] * len(turns),
+        compiler_params=pltpu.CompilerParams(vmem_limit_bytes=GRANT),
+    )(owner_order, *flat)
 
 
 def lay_kernel(parts, coefs_ref, pixel_ref, *refs):
@@ -149,9 +165,9 @@
     for position, turn in enumerate(turns):
         tops = [pl.multiple_of((chip ^ k) * rows, rows) for k in distances(turn, chips)]
         halves = [jnp.concatenate([piece[...] for piece in side], axis=0) for side in pieces[position]]
+        correlation = across(halves[0], source[:, sides[0]]) + across(halves[1], source[:, sides[1]])
         gram = across(halves[0], halves[0]) + across(halves[1], halves[1])
         step = 1.0 / jnp.sum(jnp.abs(gram), axis=1, keepdims=True)
-        correlation = across(halves[0], source[:, sides[0]]) + across(halves[1], source[:, sides[1]])
         before = jnp.concatenate(
             [coefs_ref[pl.ds(pl.multiple_of(turn * kb + top, rows), rows), :] for top in tops], axis=0
         ).astype(jnp.float32)
@@ -318,7 +334,7 @@
         ).start()
         return carry
 
-    lax.fori_loop(0, groups // together, one, 0)
+    lax.fori_loop(0, groups // together, one, 0, unroll=groups // together <= 2)
     pltpu.make_async_copy(staged, out_ref.at[pl.ds(start, height * rows)], sem).wait()
 
 
@@ -365,12 +381,15 @@
 
     keep, give = cut_block(dictionary, chips)
     got = [over_cores(give[k]) for k in range(chips)]
-    same = [keep[0]] + [over_chips(keep[k], k) for k in range(1, chips)]
-    other = [got[0]] + [over_chips(got[k], k) for k in range(1, chips)]
+    same = [[keep[0]]] + [[over_chips(keep[k], k)] for k in range(1, chips)]
+    for k, piece in enumerate(same):
+        if keep[k].shape != keep[0].shape:
+            piece.append(over_points(piece[0], 1))
+    other = [[got[0]]] + [[over_chips(got[k], k)] for k in range(1, chips)]
     laid, turned = lay_coefs(coefs, pixel_of.reshape(1, points), parts)
     laid = [laid[0]] + [over_points(laid[m], m) for m in range(1, parts)]
     base = place_coefs(laid)
-    chosen = pick_turns(owner_order, same, other)
+    chosen = [piece for turns in GROUPS for piece in pick_turns(turns, owner_order, same + other)]
 
     def gather(turn):
         held = [chosen[turn]]

time: 78.6 us -> 79.1 us (level)
  waiting for transfers between devices: 27 us -> 27.8 us
    pallas_call x2, Pallas kernels: 6.17 us -> 5.18 us  [run_maps(): pl.pallas_call(functools.partial(map_kernel, turns, parts, local_kb, firs...]
    ppermute x39 -> x40, waiting for transfers between devices: 27 us -> 27.8 us  [exchange(): return lax.ppermute(value, axis, [(i, i ^ distance) for i in range(size)])]
    ppermute x39 -> x40, starting transfers between devices: 36.9 us -> 36.9 us  [exchange(): return lax.ppermute(value, axis, [(i, i ^ distance) for i in range(size)])]
  transfers between devices with their start and end apart: 39 -> 40, of which waited for: 14 -> 13; matrix products, arithmetic and copies ran while one was open for 0% -> 0% of each run, Pallas kernels for 11% -> 11%
where the time goes in v4:
time: 79.1 us; the launch traced here: 78.9 us
  starting transfers between devices  36.9 us (47%)
  waiting for transfers between devices  27.8 us (35%)
  Pallas kernels  11.9 us (15%)
  local copies, waits for them, and re-layouts  2 us (3%)
    ppermute x40, starting transfers between devices, exchange(): return lax.ppermute(value, axis, [(i, i ^ distance) for i in range(size)])  36.9 us
    ppermute x40, waiting for transfers between devices, exchange(): return lax.ppermute(value, axis, [(i, i ^ distance) for i in range(size)])  27.8 us
    pallas_call x2, Pallas kernels, run_maps(): pl.pallas_call(functools.partial(map_kernel, turns, parts, local_kb, firs...  5.18 us
    pallas_call x2, Pallas kernels, run_turns(): pl.pallas_call(functools.partial(turn_kernel, turns, chips, parts, last),...  4.28 us
    unnamed x11, local copies, waits for them, and re-layouts  2 us
  transfers between devices with their start and end apart: 40, of which 13 were waited for; matrix products, arithmetic and copies ran while one was open for 0% of the time, Pallas kernels for 11%

profile of v4, /device:TPU:0, one launch (start us, length us, event | category | flops | bytes accessed | tf_op | source)
XLA Modules:
  0.0 78.9 jit_solution(17828407573818980871)
XLA Ops:
  0.0 1.2 %copy-done = bf16[256,2048]{1,0:T(8,128)(2,1)S(1)} copy-done((bf16[256,2048]{1,0:T(8,128)(2,1)S(1)}, bf16[256,2048]{1,0:T(8,128)(2,1)}, u32[]{:S(2)}) %copy-start) | copy-done | bytes 1048600
  1.3 3.0 %collective-permute-start = (bf16[64,1024]{1,0:T(8,128)(2,1)S(1)}, bf16[64,1024]{1,0:T(8,128)(2,1)S(1)}, u32[]{:S(2)}, u32[]{:S(2)}) collective-permute-start(bf16[64,1024]{1,0:T(8,128)(2,1)S(1)} %get-tuple-element.33), channel_id=1, source_target_pairs={{0,8},{4,12},{8,0},{12,4},{16,24},{20,28},{24,16},{28,20},{1,9},{5... | collective-permute-start | bytes 393224 | tf_op jit(solution)/shard_map/ppermute | solution.py:370
  4.3 1.5 %collective-permute-start.2 = (bf16[32,1024]{1,0:T(8,128)(2,1)S(1)}, bf16[32,1024]{1,0:T(8,128)(2,1)S(1)}, u32[]{:S(2)}, u32[]{:S(2)}) collective-permute-start(bf16[32,1024]{1,0:T(8,128)(2,1)S(1)} %get-tuple-element.35), channel_id=1, source_target_pairs={{0,24},{4,28},{8,16},{12,20},{16,8},{20,12},{24,0},{28,4},{1,25},{... | collective-permute-start | bytes 196616 | tf_op jit(solution)/shard_map/ppermute | solution.py:370
  5.8 0.5 collective-permute-start.7
  6.3 4.1 %collective-permute-done.2.refs_3_ = bf16[32,1024]{1,0:T(8,128)(2,1)S(1)} collective-permute-done((bf16[32,1024]{1,0:T(8,128)(2,1)S(1)}, bf16[32,1024]{1,0:T(8,128)(2,1)S(1)}, u32[]{:S(2)}, u32[]{:S(2)}) %collective-permute-start.2) | collective-permute-done | bytes 65568 | tf_op jit(solution)/shard_map/ppermute | solution.py:370
  10.4 0.6 collective-permute-start.1
  11.0 1.5 %collective-permute-start.6 = (bf16[64,1024]{1,0:T(8,128)(2,1)S(1)}, bf16[64,1024]{1,0:T(8,128)(2,1)S(1)}, u32[]{:S(2)}, u32[]{:S(2)}) collective-permute-start(bf16[64,1024]{1,0:T(8,128)(2,1)S(1)} %collective-permute-done.5), channel_id=1, source_target_pairs={{0,8},{4,12},{8,0},{12,4},{16,24},{20,28},{24,16},{28,20},{1,9},{5... | collective-permute-start | bytes 393224 | tf_op jit(solution)/shard_map/ppermute | solution.py:370
  12.5 1.5 %collective-permute-start.8 = (bf16[64,1024]{1,0:T(8,128)(2,1)S(1)}, bf16[64,1024]{1,0:T(8,128)(2,1)S(1)}, u32[]{:S(2)}, u32[]{:S(2)}) collective-permute-start(bf16[64,1024]{1,0:T(8,128)(2,1)S(1)} %collective-permute-done.7), channel_id=1, source_target_pairs={{0,16},{4,20},{8,24},{12,28},{16,0},{20,4},{24,8},{28,12},{1,17},{... | collective-permute-start | bytes 393224 | tf_op jit(solution)/shard_map/ppermute | solution.py:370
  14.0 0.5 collective-permute-start.10
  14.6 0.9 %collective-permute-done.1.refs_2_ = bf16[64,1024]{1,0:T(8,128)(2,1)S(1)} collective-permute-done((bf16[64,1024]{1,0:T(8,128)(2,1)S(1)}, bf16[64,1024]{1,0:T(8,128)(2,1)S(1)}, u32[]{:S(2)}, u32[]{:S(2)}) %collective-permute-start.1) | collective-permute-done | bytes 131104 | tf_op jit(solution)/shard_map/ppermute | solution.py:370
  15.5 1.6 %collective-permute-start.3 = (bf16[32,1024]{1,0:T(8,128)(2,1)S(1)}, bf16[32,1024]{1,0:T(8,128)(2,1)S(1)}, u32[]{:S(2)}, u32[]{:S(2)}) collective-permute-start(bf16[32,1024]{1,0:T(8,128)(2,1)S(1)} %collective-permute-done.2.refs_3_), channel_id=1, source_target_pairs={{0,1},{1,0},{2,3},{3,2},{4,5},{5,4},{6,7},{7,6},{8,9},{9,8},{10,11... | collective-permute-start | bytes 196616 | tf_op jit(solution)/shard_map/ppermute | solution.py:370
  17.1 2.7 %collective-permute-done.3.refs_4_ = bf16[32,1024]{1,0:T(8,128)(2,1)S(1)} collective-permute-done((bf16[32,1024]{1,0:T(8,128)(2,1)S(1)}, bf16[32,1024]{1,0:T(8,128)(2,1)S(1)}, u32[]{:S(2)}, u32[]{:S(2)}) %collective-permute-start.3) | collective-permute-done | bytes 65568 | tf_op jit(solution)/shard_map/ppermute | solution.py:370
  19.8 1.2 %collective-permute-done.8.refs_7_ = bf16[64,1024]{1,0:T(8,128)(2,1)S(1)} collective-permute-done((bf16[64,1024]{1,0:T(8,128)(2,1)S(1)}, bf16[64,1024]{1,0:T(8,128)(2,1)S(1)}, u32[]{:S(2)}, u32[]{:S(2)}) %collective-permute-start.8) | collective-permute-done | bytes 131104 | tf_op jit(solution)/shard_map/ppermute | solution.py:370
  21.0 0.7 shard_map.55
  21.7 1.6 %collective-permute-start.11 = (bf16[64,1024]{1,0:T(8,128)(2,1)S(1)}, bf16[64,1024]{1,0:T(8,128)(2,1)S(1)}, u32[]{:S(2)}, u32[]{:S(2)}) collective-permute-start(bf16[64,1024]{1,0:T(8,128)(2,1)S(1)} %get-tuple-element.40.refs_2_), channel_id=1, source_target_pairs={{0,8},{4,12},{8,0},{12,4},{16,24},{20,28},{24,16},{28,20},{1,9},{5... | collective-permute-start | bytes 393224 | tf_op jit(solution)/shard_map/ppermute | solution.py:370
  23.3 0.5 collective-permute-start.16
  23.9 0.7 copy-done.2
  24.8 1.7 %collective-permute-start.34 = (bf16[272,256]{1,0:T(8,128)(2,1)S(1)}, bf16[272,256]{1,0:T(8,128)(2,1)S(1)}, u32[]{:S(2)}, u32[]{:S(2)}) collective-permute-start(bf16[272,256]{1,0:T(8,128)(2,1)S(1)} %get-tuple-element.50), channel_id=1, source_target_pairs={{0,1},{1,0},{2,3},{3,2},{4,5},{5,4},{6,7},{7,6},{8,9},{9,8},{10,11... | collective-permute-start | bytes 417800 | tf_op jit(solution)/shard_map/ppermute | solution.py:370
  26.5 0.5 collective-permute-start.18
  27.0 0.7 shard_map.57
  27.7 1.5 %collective-permute-start.21 = (bf16[64,1024]{1,0:T(8,128)(2,1)S(1)}, bf16[64,1024]{1,0:T(8,128)(2,1)S(1)}, u32[]{:S(2)}, u32[]{:S(2)}) collective-permute-start(bf16[64,1024]{1,0:T(8,128)(2,1)S(1)} %get-tuple-element.43.refs_2_), channel_id=1, source_target_pairs={{0,8},{4,12},{8,0},{12,4},{16,24},{20,28},{24,16},{28,20},{1,9},{5... | collective-permute-start | bytes 393224 | tf_op jit(solution)/shard_map/ppermute | solution.py:370
  29.2 0.7 collective-permute-start.26
  29.9 1.5 %collective-permute-start.12 = (bf16[128,1024]{1,0:T(8,128)(2,1)S(1)}, bf16[128,1024]{1,0:T(8,128)(2,1)S(1)}, u32[]{:S(2)}, u32[]{:S(2)}) collective-permute-start(bf16[128,1024]{1,0:T(8,128)(2,1)S(1)} %pad_maximum_fusion), channel_id=1, source_target_pairs={{0,16},{4,20},{8,24},{12,28},{16,0},{20,4},{24,8},{28,12},{1,17},{... | collective-permute-start | bytes 786440 | tf_op jit(solution)/shard_map/ppermute | solution.py:370
  31.5 1.7 %collective-permute-done.21.refs_3_ = bf16[64,1024]{1,0:T(8,128)(2,1)S(1)} collective-permute-done((bf16[64,1024]{1,0:T(8,128)(2,1)S(1)}, bf16[64,1024]{1,0:T(8,128)(2,1)S(1)}, u32[]{:S(2)}, u32[]{:S(2)}) %collective-permute-start.21) | collective-permute-done | bytes 131104 | tf_op jit(solution)/shard_map/ppermute | solution.py:370
  33.1 1.4 %collective-permute-start.17 = (bf16[128,1024]{1,0:T(8,128)(2,1)S(1)}, bf16[128,1024]{1,0:T(8,128)(2,1)S(1)}, u32[]{:S(2)}, u32[]{:S(2)}) collective-permute-start(bf16[128,1024]{1,0:T(8,128)(2,1)S(1)} %pad_maximum_fusion.1), channel_id=1, source_target_pairs={{0,8},{4,12},{8,0},{12,4},{16,24},{20,28},{24,16},{28,20},{1,9},{5... | collective-permute-start | bytes 786440 | tf_op jit(solution)/shard_map/ppermute | solution.py:370
  34.7 0.9 %collective-permute-done.26.refs_9_ = bf16[64,1024]{1,0:T(8,128)(2,1)S(1)} collective-permute-done((bf16[64,1024]{1,0:T(8,128)(2,1)S(1)}, bf16[64,1024]{1,0:T(8,128)(2,1)S(1)}, u32[]{:S(2)}, u32[]{:S(2)}) %collective-permute-start.26) | collective-permute-done | bytes 131104 | tf_op jit(solution)/shard_map/ppermute | solution.py:370
  35.6 0.6 collective-permute-start.22
  36.3 1.6 %collective-permute-start.27 = (bf16[128,1024]{1,0:T(8,128)(2,1)S(1)}, bf16[128,1024]{1,0:T(8,128)(2,1)S(1)}, u32[]{:S(2)}, u32[]{:S(2)}) collective-permute-start(bf16[128,1024]{1,0:T(8,128)(2,1)S(1)} %pad_maximum_fusion.3), channel_id=1, source_target_pairs={{0,8},{4,12},{8,0},{12,4},{16,24},{20,28},{24,16},{28,20},{1,9},{5... | collective-permute-start | bytes 786440 | tf_op jit(solution)/shard_map/ppermute | solution.py:370
  37.8 3.4 %collective-permute-done.12.refs_4_ = bf16[128,1024]{1,0:T(8,128)(2,1)S(1)} collective-permute-done((bf16[128,1024]{1,0:T(8,128)(2,1)S(1)}, bf16[128,1024]{1,0:T(8,128)(2,1)S(1)}, u32[]{:S(2)}, u32[]{:S(2)}) %collective-permute-start.12) | collective-permute-done | bytes 262176 | tf_op jit(solution)/shard_map/ppermute | solution.py:370
  41.2 1.1 %collective-permute-done.17.refs_10_ = bf16[128,1024]{1,0:T(8,128)(2,1)S(1)} collective-permute-done((bf16[128,1024]{1,0:T(8,128)(2,1)S(1)}, bf16[128,1024]{1,0:T(8,128)(2,1)S(1)}, u32[]{:S(2)}, u32[]{:S(2)}) %collective-permute-start.17) | collective-permute-done | bytes 262176 | tf_op jit(solution)/shard_map/ppermute | solution.py:370
  42.3 0.5 collective-permute-start.19
  42.8 2.8 %collective-permute-done.22.refs_4_ = bf16[128,1024]{1,0:T(8,128)(2,1)S(1)} collective-permute-done((bf16[128,1024]{1,0:T(8,128)(2,1)S(1)}, bf16[128,1024]{1,0:T(8,128)(2,1)S(1)}, u32[]{:S(2)}, u32[]{:S(2)}) %collective-permute-start.22) | collective-permute-done | bytes 262176 | tf_op jit(solution)/shard_map/ppermute | solution.py:370
  45.6 0.5 collective-permute-done.27.refs_10_
  46.1 0.5 collective-permute-start.28
  47.1 2.4 %shard_map.56 = (bf16[256,2048]{1,0:T(8,128)(2,1)S(1)}, bf16[128,256]{1,0:T(8,128)(2,1)S(1)}, bf16[128,256]{1,0:T(8,128)(2,1)S(1)}, bf16[128,256]{1,0:T(8,128)(2,1)S(1)}, bf16[128,256]{1,0:T(8,128)(2,1)S(1)}) custom-call(bf16[256,2048]{1,0:T(8,128)(2,1)S(1)} %bitcast.6, bf16[1024,256]{1,0:T(8,128)(2,1)S(1)} %get-tuple-element.31.refs_1_, ...), custom_call_target="tpu_custom_call" | custom-call | flops 1610612736 | bytes 4194304 | tf_op jit(solution)/shard_map/pallas_call | solution.py:202
  49.5 2.7 %collective-permute-start.35 = (bf16[272,256]{1,0:T(8,128)(2,1)S(1)}, bf16[272,256]{1,0:T(8,128)(2,1)S(1)}, u32[]{:S(2)}, u32[]{:S(2)}) collective-permute-start(bf16[272,256]{1,0:T(8,128)(2,1)S(1)} %get-tuple-element.51), channel_id=1, source_target_pairs={{0,2},{1,3},{2,0},{3,1},{4,6},{5,7},{6,4},{7,5},{8,10},{9,11},{10,... | collective-permute-start | bytes 417800 | tf_op jit(solution)/shard_map/ppermute | solution.py:370
  52.2 0.8 %collective-permute-start.37 = (bf16[128,256]{1,0:T(8,128)(2,1)S(1)}, bf16[128,256]{1,0:T(8,128)(2,1)S(1)}, u32[]{:S(2)}, u32[]{:S(2)}) collective-permute-start(bf16[128,256]{1,0:T(8,128)(2,1)S(1)} %get-tuple-element.54), channel_id=1, source_target_pairs={{0,1},{1,0},{2,3},{3,2},{4,5},{5,4},{6,7},{7,6},{8,9},{9,8},{10,11... | collective-permute-start | bytes 196616 | tf_op jit(solution)/shard_map/ppermute | solution.py:370
  53.1 3.5 %collective-permute-start.38 = (bf16[128,256]{1,0:T(8,128)(2,1)S(1)}, bf16[128,256]{1,0:T(8,128)(2,1)S(1)}, u32[]{:S(2)}, u32[]{:S(2)}) collective-permute-start(bf16[128,256]{1,0:T(8,128)(2,1)S(1)} %get-tuple-element.55), channel_id=1, source_target_pairs={{0,2},{1,3},{2,0},{3,1},{4,6},{5,7},{6,4},{7,5},{8,10},{9,11},{10,... | collective-permute-start | bytes 196616 | tf_op jit(solution)/shard_map/ppermute | solution.py:370
  56.6 1.9 %shard_map.58 = (bf16[128,256]{1,0:T(8,128)(2,1)S(1)}, bf16[128,256]{1,0:T(8,128)(2,1)S(1)}, bf16[128,256]{1,0:T(8,128)(2,1)S(1)}, bf16[128,256]{1,0:T(8,128)(2,1)S(1)}) custom-call(bf16[256,2048]{1,0:T(8,128)(2,1)S(1)} %get-tuple-element.42.refs_0_, bf16[1024,256]{1,0:T(8,128)(2,1)S(1)} %get-tuple-element.31.refs_1_, ...), custom_call_target="tpu_custom_call" | custom-call | flops 1610612736 | bytes 4194304 | tf_op jit(solution)/shard_map/pallas_call | solution.py:202
  58.6 6.3 %collective-permute-done.35.refs_2_.refs_6_ = bf16[272,256]{1,0:T(8,128)(2,1)S(1)} collective-permute-done((bf16[272,256]{1,0:T(8,128)(2,1)S(1)}, bf16[272,256]{1,0:T(8,128)(2,1)S(1)}, u32[]{:S(2)}, u32[]{:S(2)}) %collective-permute-start.35) | collective-permute-done | bytes 139296 | tf_op jit(solution)/shard_map/ppermute | solution.py:370
  64.9 0.5 collective-permute-start.31
  65.4 4.9 %collective-permute-start.32 = (bf16[128,256]{1,0:T(8,128)(2,1)S(1)}, bf16[128,256]{1,0:T(8,128)(2,1)S(1)}, u32[]{:S(2)}, u32[]{:S(2)}) collective-permute-start(bf16[128,256]{1,0:T(8,128)(2,1)S(1)} %get-tuple-element.47), channel_id=1, source_target_pairs={{0,2},{1,3},{2,0},{3,1},{4,6},{5,7},{6,4},{7,5},{8,10},{9,11},{10,... | collective-permute-start | bytes 196616 | tf_op jit(solution)/shard_map/ppermute | solution.py:370
  70.3 0.5 collective-permute-start.33
  70.8 0.8 place.1.refs_8_
  71.5 2.6 %shard_map.59.refs_9_ = f32[2048,128]{1,0:T(8,128)} custom-call(bf16[128,256]{1,0:T(8,128)(2,1)S(1)} %get-tuple-element.53.refs_0_, bf16[128,256]{1,0:T(8,128)(2,1)S(1)} %collective-permute-done.37.refs_1_, bf16[128,256]{1,0:T(8,128)(2,1)S(1)} %collective-permute-done.38.refs_2_, bf16[128,256]{1,0:T(8,128)(2,1)S(1)} %collective-permute-done.39.refs_3_, ...), custom_call_target="tpu_custom_call" | custom-call | flops 268435456 | bytes 1048576 | tf_op jit(solution)/shard_map/pallas_call | solution.py:349
  74.2 0.7 collective-permute-done.32.refs_2_
  74.8 1.5 %collective-permute-done.33.refs_3_ = bf16[128,256]{1,0:T(8,128)(2,1)S(1)} collective-permute-done((bf16[128,256]{1,0:T(8,128)(2,1)S(1)}, bf16[128,256]{1,0:T(8,128)(2,1)S(1)}, u32[]{:S(2)}, u32[]{:S(2)}) %collective-permute-start.33) | collective-permute-done | bytes 65568 | tf_op jit(solution)/shard_map/ppermute | solution.py:370
  76.3 2.6 %shard_map.60 = f32[2048,128]{1,0:T(8,128)} custom-call(bf16[128,256]{1,0:T(8,128)(2,1)S(1)} %get-tuple-element.45.refs_0_, bf16[128,256]{1,0:T(8,128)(2,1)S(1)} %collective-permute-done.31.refs_1_, bf16[128,256]{1,0:T(8,128)(2,1)S(1)} %collective-permute-done.32.refs_2_, ...), custom_call_target="tpu_custom_call", output_to_operand_aliasing={{}: (9, {})} | custom-call | flops 268435456 | bytes 1048576 | tf_op jit(solution)/shard_map/pallas_call | solution.py:349
  (56 shorter events, 1.4 us)
Async XLA Ops:
  0.0 1.2 %copy-start = (bf16[256,2048]{1,0:T(8,128)(2,1)S(1)}, bf16[256,2048]{1,0:T(8,128)(2,1)}, u32[]{:S(2)}) copy-start(bf16[256,2048]{1,0:T(8,128)(2,1)} %block_ref.1) | copy-start | bytes 3145732
  1.3 9.7 %collective-permute-start = (bf16[64,1024]{1,0:T(8,128)(2,1)S(1)}, bf16[64,1024]{1,0:T(8,128)(2,1)S(1)}, u32[]{:S(2)}, u32[]{:S(2)}) collective-permute-start(bf16[64,1024]{1,0:T(8,128)(2,1)S(1)} %get-tuple-element.33), channel_id=1, source_target_pairs={{0,8},{4,12},{8,0},{12,4},{16,24},{20,28},{24,16},{28,20},{1,9},{5... | collective-permute-start | bytes 393224 | tf_op jit(solution)/shard_map/ppermute | solution.py:370
  4.3 6.1 %collective-permute-start.2 = (bf16[32,1024]{1,0:T(8,128)(2,1)S(1)}, bf16[32,1024]{1,0:T(8,128)(2,1)S(1)}, u32[]{:S(2)}, u32[]{:S(2)}) collective-permute-start(bf16[32,1024]{1,0:T(8,128)(2,1)S(1)} %get-tuple-element.35), channel_id=1, source_target_pairs={{0,24},{4,28},{8,16},{12,20},{16,8},{20,12},{24,0},{28,4},{1,25},{... | collective-permute-start | bytes 196616 | tf_op jit(solution)/shard_map/ppermute | solution.py:370
  5.8 5.2 %collective-permute-start.5 = (bf16[64,1024]{1,0:T(8,128)(2,1)S(1)}, bf16[64,1024]{1,0:T(8,128)(2,1)S(1)}, u32[]{:S(2)}, u32[]{:S(2)}) collective-permute-start(bf16[64,1024]{1,0:T(8,128)(2,1)S(1)} %get-tuple-element.37), channel_id=1, source_target_pairs={{0,4},{4,0},{8,12},{12,8},{16,20},{20,16},{24,28},{28,24},{1,5},{5... | collective-permute-start | bytes 393224 | tf_op jit(solution)/shard_map/ppermute | solution.py:370
  5.8 6.7 %collective-permute-start.7 = (bf16[64,1024]{1,0:T(8,128)(2,1)S(1)}, bf16[64,1024]{1,0:T(8,128)(2,1)S(1)}, u32[]{:S(2)}, u32[]{:S(2)}) collective-permute-start(bf16[64,1024]{1,0:T(8,128)(2,1)S(1)} %get-tuple-element.38), channel_id=1, source_target_pairs={{0,4},{4,0},{8,12},{12,8},{16,20},{20,16},{24,28},{28,24},{1,5},{5... | collective-permute-start | bytes 393224 | tf_op jit(solution)/shard_map/ppermute | solution.py:370
  6.3 7.7 %collective-permute-start.9 = (bf16[64,1024]{1,0:T(8,128)(2,1)S(1)}, bf16[64,1024]{1,0:T(8,128)(2,1)S(1)}, u32[]{:S(2)}, u32[]{:S(2)}) collective-permute-start(bf16[64,1024]{1,0:T(8,128)(2,1)S(1)} %get-tuple-element.39), channel_id=1, source_target_pairs={{0,4},{4,0},{8,12},{12,8},{16,20},{20,16},{24,28},{28,24},{1,5},{5... | collective-permute-start | bytes 393224 | tf_op jit(solution)/shard_map/ppermute | solution.py:370
  10.4 5.1 %collective-permute-start.1 = (bf16[64,1024]{1,0:T(8,128)(2,1)S(1)}, bf16[64,1024]{1,0:T(8,128)(2,1)S(1)}, u32[]{:S(2)}, u32[]{:S(2)}) collective-permute-start(bf16[64,1024]{1,0:T(8,128)(2,1)S(1)} %get-tuple-element.34), channel_id=1, source_target_pairs={{0,16},{4,20},{8,24},{12,28},{16,0},{20,4},{24,8},{28,12},{1,17},{... | collective-permute-start | bytes 393224 | tf_op jit(solution)/shard_map/ppermute | solution.py:370
  11.0 10.0 %copy-start.1 = (s32[8]{0:T(128)S(1)}, s32[8]{0:T(128)}, u32[]{:S(2)}) copy-start(s32[8]{0:T(128)} %order_ref.3) | copy-start | bytes 100
  11.0 8.8 %collective-permute-start.4 = (bf16[64,1024]{1,0:T(8,128)(2,1)S(1)}, bf16[64,1024]{1,0:T(8,128)(2,1)S(1)}, u32[]{:S(2)}, u32[]{:S(2)}) collective-permute-start(bf16[64,1024]{1,0:T(8,128)(2,1)S(1)} %get-tuple-element.36), channel_id=1, source_target_pairs={{0,4},{4,0},{8,12},{12,8},{16,20},{20,16},{24,28},{28,24},{1,5},{5... | collective-permute-start | bytes 393224 | tf_op jit(solution)/shard_map/ppermute | solution.py:370
  11.0 8.8 %collective-permute-start.6 = (bf16[64,1024]{1,0:T(8,128)(2,1)S(1)}, bf16[64,1024]{1,0:T(8,128)(2,1)S(1)}, u32[]{:S(2)}, u32[]{:S(2)}) collective-permute-start(bf16[64,1024]{1,0:T(8,128)(2,1)S(1)} %collective-permute-done.5), channel_id=1, source_target_pairs={{0,8},{4,12},{8,0},{12,4},{16,24},{20,28},{24,16},{28,20},{1,9},{5... | collective-permute-start | bytes 393224 | tf_op jit(solution)/shard_map/ppermute | solution.py:370
  12.5 8.5 %collective-permute-start.8 = (bf16[64,1024]{1,0:T(8,128)(2,1)S(1)}, bf16[64,1024]{1,0:T(8,128)(2,1)S(1)}, u32[]{:S(2)}, u32[]{:S(2)}) collective-permute-start(bf16[64,1024]{1,0:T(8,128)(2,1)S(1)} %collective-permute-done.7), channel_id=1, source_target_pairs={{0,16},{4,20},{8,24},{12,28},{16,0},{20,4},{24,8},{28,12},{1,17},{... | collective-permute-start | bytes 393224 | tf_op jit(solution)/shard_map/ppermute | solution.py:370
  14.0 7.0 %collective-permute-start.10 = (bf16[64,1024]{1,0:T(8,128)(2,1)S(1)}, bf16[64,1024]{1,0:T(8,128)(2,1)S(1)}, u32[]{:S(2)}, u32[]{:S(2)}) collective-permute-start(bf16[64,1024]{1,0:T(8,128)(2,1)S(1)} %collective-permute-done.9), channel_id=1, source_target_pairs={{0,24},{4,28},{8,16},{12,20},{16,8},{20,12},{24,0},{28,4},{1,25},{... | collective-permute-start | bytes 393224 | tf_op jit(solution)/shard_map/ppermute | solution.py:370
  15.5 4.3 %collective-permute-start.3 = (bf16[32,1024]{1,0:T(8,128)(2,1)S(1)}, bf16[32,1024]{1,0:T(8,128)(2,1)S(1)}, u32[]{:S(2)}, u32[]{:S(2)}) collective-permute-start(bf16[32,1024]{1,0:T(8,128)(2,1)S(1)} %collective-permute-done.2.refs_3_), channel_id=1, source_target_pairs={{0,1},{1,0},{2,3},{3,2},{4,5},{5,4},{6,7},{7,6},{8,9},{9,8},{10,11... | collective-permute-start | bytes 196616 | tf_op jit(solution)/shard_map/ppermute | solution.py:370
  21.0 2.7 %copy-start.4 = (bf16[1,256,4,256]{3,2,1,0:T(4,128)(2,1)S(1)}, bf16[1,256,4,256]{3,2,1,0:T(4,128)(2,1)}, u32[]{:S(2)}) copy-start(bf16[1,256,4,256]{3,2,1,0:T(4,128)(2,1)} %param.6) | copy-start | bytes 1572868
  21.7 5.9 %collective-permute-start.11 = (bf16[64,1024]{1,0:T(8,128)(2,1)S(1)}, bf16[64,1024]{1,0:T(8,128)(2,1)S(1)}, u32[]{:S(2)}, u32[]{:S(2)}) collective-permute-start(bf16[64,1024]{1,0:T(8,128)(2,1)S(1)} %get-tuple-element.40.refs_2_), channel_id=1, source_target_pairs={{0,8},{4,12},{8,0},{12,4},{16,24},{20,28},{24,16},{28,20},{1,9},{5... | collective-permute-start | bytes 393224 | tf_op jit(solution)/shard_map/ppermute | solution.py:370
  23.3 5.9 %collective-permute-start.16 = (bf16[64,1024]{1,0:T(8,128)(2,1)S(1)}, bf16[64,1024]{1,0:T(8,128)(2,1)S(1)}, u32[]{:S(2)}, u32[]{:S(2)}) collective-permute-start(bf16[64,1024]{1,0:T(8,128)(2,1)S(1)} %get-tuple-element.41.refs_8_), channel_id=1, source_target_pairs={{0,16},{4,20},{8,24},{12,28},{16,0},{20,4},{24,8},{28,12},{1,17},{... | collective-permute-start | bytes 393224 | tf_op jit(solution)/shard_map/ppermute | solution.py:370
  23.9 0.7 copy-start.2
  24.8 5.1 %collective-permute-start.34 = (bf16[272,256]{1,0:T(8,128)(2,1)S(1)}, bf16[272,256]{1,0:T(8,128)(2,1)S(1)}, u32[]{:S(2)}, u32[]{:S(2)}) collective-permute-start(bf16[272,256]{1,0:T(8,128)(2,1)S(1)} %get-tuple-element.50), channel_id=1, source_target_pairs={{0,1},{1,0},{2,3},{3,2},{4,5},{5,4},{6,7},{7,6},{8,9},{9,8},{10,11... | collective-permute-start | bytes 417800 | tf_op jit(solution)/shard_map/ppermute | solution.py:370
  26.5 8.1 %collective-permute-start.13 = (bf16[64,1024]{1,0:T(8,128)(2,1)S(1)}, bf16[64,1024]{1,0:T(8,128)(2,1)S(1)}, u32[]{:S(2)}, u32[]{:S(2)}) collective-permute-start(bf16[64,1024]{1,0:T(8,128)(2,1)S(1)} %get-tuple-element.40.refs_2_), channel_id=1, source_target_pairs={{0,4},{4,0},{8,12},{12,8},{16,20},{20,16},{24,28},{28,24},{1,5},{5... | collective-permute-start | bytes 393224 | tf_op jit(solution)/shard_map/ppermute | solution.py:370
  26.5 9.8 %collective-permute-start.18 = (bf16[64,1024]{1,0:T(8,128)(2,1)S(1)}, bf16[64,1024]{1,0:T(8,128)(2,1)S(1)}, u32[]{:S(2)}, u32[]{:S(2)}) collective-permute-start(bf16[64,1024]{1,0:T(8,128)(2,1)S(1)} %get-tuple-element.41.refs_8_), channel_id=1, source_target_pairs={{0,4},{4,0},{8,12},{12,8},{16,20},{20,16},{24,28},{28,24},{1,5},{5... | collective-permute-start | bytes 393224 | tf_op jit(solution)/shard_map/ppermute | solution.py:370
  27.7 19.5 %copy-start.3 = (bf16[1,256,2048]{2,1,0:T(8,128)(2,1)S(1)}, bf16[1,256,2048]{2,1,0:T(8,128)(2,1)}, u32[]{:S(2)}) copy-start(bf16[1,256,2048]{2,1,0:T(8,128)(2,1)} %param.5) | copy-start | bytes 3145732
  27.7 5.5 %collective-permute-start.21 = (bf16[64,1024]{1,0:T(8,128)(2,1)S(1)}, bf16[64,1024]{1,0:T(8,128)(2,1)S(1)}, u32[]{:S(2)}, u32[]{:S(2)}) collective-permute-start(bf16[64,1024]{1,0:T(8,128)(2,1)S(1)} %get-tuple-element.43.refs_2_), channel_id=1, source_target_pairs={{0,8},{4,12},{8,0},{12,4},{16,24},{20,28},{24,16},{28,20},{1,9},{5... | collective-permute-start | bytes 393224 | tf_op jit(solution)/shard_map/ppermute | solution.py:370
  29.2 6.4 %collective-permute-start.26 = (bf16[64,1024]{1,0:T(8,128)(2,1)S(1)}, bf16[64,1024]{1,0:T(8,128)(2,1)S(1)}, u32[]{:S(2)}, u32[]{:S(2)}) collective-permute-start(bf16[64,1024]{1,0:T(8,128)(2,1)S(1)} %get-tuple-element.44.refs_8_), channel_id=1, source_target_pairs={{0,16},{4,20},{8,24},{12,28},{16,0},{20,4},{24,8},{28,12},{1,17},{... | collective-permute-start | bytes 393224 | tf_op jit(solution)/shard_map/ppermute | solution.py:370
  29.9 11.3 %collective-permute-start.12 = (bf16[128,1024]{1,0:T(8,128)(2,1)S(1)}, bf16[128,1024]{1,0:T(8,128)(2,1)S(1)}, u32[]{:S(2)}, u32[]{:S(2)}) collective-permute-start(bf16[128,1024]{1,0:T(8,128)(2,1)S(1)} %pad_maximum_fusion), channel_id=1, source_target_pairs={{0,16},{4,20},{8,24},{12,28},{16,0},{20,4},{24,8},{28,12},{1,17},{... | collective-permute-start | bytes 786440 | tf_op jit(solution)/shard_map/ppermute | solution.py:370
  33.1 9.2 %collective-permute-start.17 = (bf16[128,1024]{1,0:T(8,128)(2,1)S(1)}, bf16[128,1024]{1,0:T(8,128)(2,1)S(1)}, u32[]{:S(2)}, u32[]{:S(2)}) collective-permute-start(bf16[128,1024]{1,0:T(8,128)(2,1)S(1)} %pad_maximum_fusion.1), channel_id=1, source_target_pairs={{0,8},{4,12},{8,0},{12,4},{16,24},{20,28},{24,16},{28,20},{1,9},{5... | collective-permute-start | bytes 786440 | tf_op jit(solution)/shard_map/ppermute | solution.py:370
  34.6 3.3 %collective-permute-start.23 = (bf16[64,1024]{1,0:T(8,128)(2,1)S(1)}, bf16[64,1024]{1,0:T(8,128)(2,1)S(1)}, u32[]{:S(2)}, u32[]{:S(2)}) collective-permute-start(bf16[64,1024]{1,0:T(8,128)(2,1)S(1)} %get-tuple-element.43.refs_2_), channel_id=1, source_target_pairs={{0,4},{4,0},{8,12},{12,8},{16,20},{20,16},{24,28},{28,24},{1,5},{5... | collective-permute-start | bytes 393224 | tf_op jit(solution)/shard_map/ppermute | solution.py:370
  35.6 10.0 %collective-permute-start.22 = (bf16[128,1024]{1,0:T(8,128)(2,1)S(1)}, bf16[128,1024]{1,0:T(8,128)(2,1)S(1)}, u32[]{:S(2)}, u32[]{:S(2)}) collective-permute-start(bf16[128,1024]{1,0:T(8,128)(2,1)S(1)} %pad_maximum_fusion.2), channel_id=1, source_target_pairs={{0,16},{4,20},{8,24},{12,28},{16,0},{20,4},{24,8},{28,12},{1,17},{... | collective-permute-start | bytes 786440 | tf_op jit(solution)/shard_map/ppermute | solution.py:370
  36.3 9.8 %collective-permute-start.27 = (bf16[128,1024]{1,0:T(8,128)(2,1)S(1)}, bf16[128,1024]{1,0:T(8,128)(2,1)S(1)}, u32[]{:S(2)}, u32[]{:S(2)}) collective-permute-start(bf16[128,1024]{1,0:T(8,128)(2,1)S(1)} %pad_maximum_fusion.3), channel_id=1, source_target_pairs={{0,8},{4,12},{8,0},{12,4},{16,24},{20,28},{24,16},{28,20},{1,9},{5... | collective-permute-start | bytes 786440 | tf_op jit(solution)/shard_map/ppermute | solution.py:370
  37.8 4.5 %collective-permute-start.14 = (bf16[64,1024]{1,0:T(8,128)(2,1)S(1)}, bf16[64,1024]{1,0:T(8,128)(2,1)S(1)}, u32[]{:S(2)}, u32[]{:S(2)}) collective-permute-start(bf16[64,1024]{1,0:T(8,128)(2,1)S(1)} %collective-permute-done.11.refs_3_), channel_id=1, source_target_pairs={{0,4},{4,0},{8,12},{12,8},{16,20},{20,16},{24,28},{28,24},{1,5},{5... | collective-permute-start | bytes 393224 | tf_op jit(solution)/shard_map/ppermute | solution.py:370
  41.2 5.4 %collective-permute-start.15 = (bf16[128,1024]{1,0:T(8,128)(2,1)S(1)}, bf16[128,1024]{1,0:T(8,128)(2,1)S(1)}, u32[]{:S(2)}, u32[]{:S(2)}) collective-permute-start(bf16[128,1024]{1,0:T(8,128)(2,1)S(1)} %collective-permute-done.12.refs_4_), channel_id=1, source_target_pairs={{0,4},{4,0},{8,12},{12,8},{16,20},{20,16},{24,28},{28,24},{1,5},{5... | collective-permute-start | bytes 786440 | tf_op jit(solution)/shard_map/ppermute | solution.py:370
  42.3 4.4 %collective-permute-start.20 = (bf16[128,1024]{1,0:T(8,128)(2,1)S(1)}, bf16[128,1024]{1,0:T(8,128)(2,1)S(1)}, u32[]{:S(2)}, u32[]{:S(2)}) collective-permute-start(bf16[128,1024]{1,0:T(8,128)(2,1)S(1)} %collective-permute-done.17.refs_10_), channel_id=1, source_target_pairs={{0,4},{4,0},{8,12},{12,8},{16,20},{20,16},{24,28},{28,24},{1,5},{5... | collective-permute-start | bytes 786440 | tf_op jit(solution)/shard_map/ppermute | solution.py:370
  42.3 3.8 %collective-permute-start.19 = (bf16[64,1024]{1,0:T(8,128)(2,1)S(1)}, bf16[64,1024]{1,0:T(8,128)(2,1)S(1)}, u32[]{:S(2)}, u32[]{:S(2)}) collective-permute-start(bf16[64,1024]{1,0:T(8,128)(2,1)S(1)} %collective-permute-done.16.refs_9_), channel_id=1, source_target_pairs={{0,4},{4,0},{8,12},{12,8},{16,20},{20,16},{24,28},{28,24},{1,5},{5... | collective-permute-start | bytes 393224 | tf_op jit(solution)/shard_map/ppermute | solution.py:370
  45.6 7.5 %collective-permute-start.25 = (bf16[128,1024]{1,0:T(8,128)(2,1)S(1)}, bf16[128,1024]{1,0:T(8,128)(2,1)S(1)}, u32[]{:S(2)}, u32[]{:S(2)}) collective-permute-start(bf16[128,1024]{1,0:T(8,128)(2,1)S(1)} %collective-permute-done.22.refs_4_), channel_id=1, source_target_pairs={{0,4},{4,0},{8,12},{12,8},{16,20},{20,16},{24,28},{28,24},{1,5},{5... | collective-permute-start | bytes 786440 | tf_op jit(solution)/shard_map/ppermute | solution.py:370
  46.1 10.5 %collective-permute-start.30 = (bf16[128,1024]{1,0:T(8,128)(2,1)S(1)}, bf16[128,1024]{1,0:T(8,128)(2,1)S(1)}, u32[]{:S(2)}, u32[]{:S(2)}) collective-permute-start(bf16[128,1024]{1,0:T(8,128)(2,1)S(1)} %collective-permute-done.27.refs_10_), channel_id=1, source_target_pairs={{0,4},{4,0},{8,12},{12,8},{16,20},{20,16},{24,28},{28,24},{1,5},{5... | collective-permute-start | bytes 786440 | tf_op jit(solution)/shard_map/ppermute | solution.py:370
  46.1 3.4 %collective-permute-start.28 = (bf16[64,1024]{1,0:T(8,128)(2,1)S(1)}, bf16[64,1024]{1,0:T(8,128)(2,1)S(1)}, u32[]{:S(2)}, u32[]{:S(2)}) collective-permute-start(bf16[64,1024]{1,0:T(8,128)(2,1)S(1)} %get-tuple-element.44.refs_8_), channel_id=1, source_target_pairs={{0,4},{4,0},{8,12},{12,8},{16,20},{20,16},{24,28},{28,24},{1,5},{5... | collective-permute-start | bytes 393224 | tf_op jit(solution)/shard_map/ppermute | solution.py:370
  46.6 5.6 %collective-permute-start.24 = (bf16[64,1024]{1,0:T(8,128)(2,1)S(1)}, bf16[64,1024]{1,0:T(8,128)(2,1)S(1)}, u32[]{:S(2)}, u32[]{:S(2)}) collective-permute-start(bf16[64,1024]{1,0:T(8,128)(2,1)S(1)} %collective-permute-done.21.refs_3_), channel_id=1, source_target_pairs={{0,4},{4,0},{8,12},{12,8},{16,20},{20,16},{24,28},{28,24},{1,5},{5... | collective-permute-start | bytes 393224 | tf_op jit(solution)/shard_map/ppermute | solution.py:370
  46.7 5.5 %collective-permute-start.29 = (bf16[64,1024]{1,0:T(8,128)(2,1)S(1)}, bf16[64,1024]{1,0:T(8,128)(2,1)S(1)}, u32[]{:S(2)}, u32[]{:S(2)}) collective-permute-start(bf16[64,1024]{1,0:T(8,128)(2,1)S(1)} %collective-permute-done.26.refs_9_), channel_id=1, source_target_pairs={{0,4},{4,0},{8,12},{12,8},{16,20},{20,16},{24,28},{28,24},{1,5},{5... | collective-permute-start | bytes 393224 | tf_op jit(solution)/shard_map/ppermute | solution.py:370
  49.5 15.3 %collective-permute-start.35 = (bf16[272,256]{1,0:T(8,128)(2,1)S(1)}, bf16[272,256]{1,0:T(8,128)(2,1)S(1)}, u32[]{:S(2)}, u32[]{:S(2)}) collective-permute-start(bf16[272,256]{1,0:T(8,128)(2,1)S(1)} %get-tuple-element.51), channel_id=1, source_target_pairs={{0,2},{1,3},{2,0},{3,1},{4,6},{5,7},{6,4},{7,5},{8,10},{9,11},{10,... | collective-permute-start | bytes 417800 | tf_op jit(solution)/shard_map/ppermute | solution.py:370
  52.2 13.2 %collective-permute-start.36 = (bf16[272,256]{1,0:T(8,128)(2,1)S(1)}, bf16[272,256]{1,0:T(8,128)(2,1)S(1)}, u32[]{:S(2)}, u32[]{:S(2)}) collective-permute-start(bf16[272,256]{1,0:T(8,128)(2,1)S(1)} %get-tuple-element.52), channel_id=1, source_target_pairs={{0,3},{1,2},{2,1},{3,0},{4,7},{5,6},{6,5},{7,4},{8,11},{9,10},{10,... | collective-permute-start | bytes 417800 | tf_op jit(solution)/shard_map/ppermute | solution.py:370
  52.2 18.0 %collective-permute-start.37 = (bf16[128,256]{1,0:T(8,128)(2,1)S(1)}, bf16[128,256]{1,0:T(8,128)(2,1)S(1)}, u32[]{:S(2)}, u32[]{:S(2)}) collective-permute-start(bf16[128,256]{1,0:T(8,128)(2,1)S(1)} %get-tuple-element.54), channel_id=1, source_target_pairs={{0,1},{1,0},{2,3},{3,2},{4,5},{5,4},{6,7},{7,6},{8,9},{9,8},{10,11... | collective-permute-start | bytes 196616 | tf_op jit(solution)/shard_map/ppermute | solution.py:370
  53.1 18.4 %collective-permute-start.38 = (bf16[128,256]{1,0:T(8,128)(2,1)S(1)}, bf16[128,256]{1,0:T(8,128)(2,1)S(1)}, u32[]{:S(2)}, u32[]{:S(2)}) collective-permute-start(bf16[128,256]{1,0:T(8,128)(2,1)S(1)} %get-tuple-element.55), channel_id=1, source_target_pairs={{0,2},{1,3},{2,0},{3,1},{4,6},{5,7},{6,4},{7,5},{8,10},{9,11},{10,... | collective-permute-start | bytes 196616 | tf_op jit(solution)/shard_map/ppermute | solution.py:370
  56.6 15.0 %collective-permute-start.39 = (bf16[128,256]{1,0:T(8,128)(2,1)S(1)}, bf16[128,256]{1,0:T(8,128)(2,1)S(1)}, u32[]{:S(2)}, u32[]{:S(2)}) collective-permute-start(bf16[128,256]{1,0:T(8,128)(2,1)S(1)} %get-tuple-element.56), channel_id=1, source_target_pairs={{0,3},{1,2},{2,1},{3,0},{4,7},{5,6},{6,5},{7,4},{8,11},{9,10},{10,... | collective-permute-start | bytes 196616 | tf_op jit(solution)/shard_map/ppermute | solution.py:370
  64.9 9.3 %collective-permute-start.31 = (bf16[128,256]{1,0:T(8,128)(2,1)S(1)}, bf16[128,256]{1,0:T(8,128)(2,1)S(1)}, u32[]{:S(2)}, u32[]{:S(2)}) collective-permute-start(bf16[128,256]{1,0:T(8,128)(2,1)S(1)} %get-tuple-element.46), channel_id=1, source_target_pairs={{0,1},{1,0},{2,3},{3,2},{4,5},{5,4},{6,7},{7,6},{8,9},{9,8},{10,11... | collective-permute-start | bytes 196616 | tf_op jit(solution)/shard_map/ppermute | solution.py:370
  65.4 9.5 %collective-permute-start.32 = (bf16[128,256]{1,0:T(8,128)(2,1)S(1)}, bf16[128,256]{1,0:T(8,128)(2,1)S(1)}, u32[]{:S(2)}, u32[]{:S(2)}) collective-permute-start(bf16[128,256]{1,0:T(8,128)(2,1)S(1)} %get-tuple-element.47), channel_id=1, source_target_pairs={{0,2},{1,3},{2,0},{3,1},{4,6},{5,7},{6,4},{7,5},{8,10},{9,11},{10,... | collective-permute-start | bytes 196616 | tf_op jit(solution)/shard_map/ppermute | solution.py:370
  70.3 6.1 %collective-permute-start.33 = (bf16[128,256]{1,0:T(8,128)(2,1)S(1)}, bf16[128,256]{1,0:T(8,128)(2,1)S(1)}, u32[]{:S(2)}, u32[]{:S(2)}) collective-permute-start(bf16[128,256]{1,0:T(8,128)(2,1)S(1)} %get-tuple-element.48), channel_id=1, source_target_pairs={{0,3},{1,2},{2,1},{3,0},{4,7},{5,6},{6,5},{7,4},{8,11},{9,10},{10,... | collective-permute-start | bytes 196616 | tf_op jit(solution)/shard_map/ppermute | solution.py:370

commit v5 on v3

--- a/solution.py
+++ b/solution.py
@@ -12,7 +12,7 @@
 SWEEPS = 4
 MAP_W = 128
 SUBLANES = 8
-UNROLL = 8
+UNROLL = 16
 TILE_ROWS = 16
 GRANT = 16 * 1024 * 1024
 
@@ -68,29 +68,28 @@
     return outs[:chips], outs[chips:]
 
 
-def pick_kernel(chips, order_ref, *refs):
+def pick_kernel(turns, chips, order_ref, *refs):
     pieces, outs = refs[: 2 * chips], refs[2 * chips :]
     chip, core = place_of_device()
-    for turn in range(TURNS):
+    for position, turn in enumerate(turns):
         owner = order_ref[turn]
         wanted = ((owner // 2) ^ chip) + chips * ((owner % 2) ^ core)
         for number, piece in enumerate(pieces):
 
             @pl.when(wanted == number)
             def _():
-                outs[turn][...] = piece[...]
-
-
-def pick_turns(owner_order, same, other):
+                outs[position][...] = piece[...]
+
+
+def pick_turns(turns, owner_order, same, other):
     chips = len(same)
     piece = jax.ShapeDtypeStruct(same[0].shape, same[0].dtype)
     return pl.pallas_call(
-        functools.partial(pick_kernel, chips),
-        out_shape=[piece] * TURNS,
+        functools.partial(pick_kernel, turns, chips),
+        out_shape=[piece] * len(turns),
         in_specs=[SMEM] + [VMEM] * (2 * chips),
-        out_specs=[VMEM] * TURNS,
-        compiler_params=pltpu.CompilerParams(vmem_limit_bytes=GRANT),
-        name="pick",
+        out_specs=[VMEM] * len(turns),
+        compiler_params=pltpu.CompilerParams(vmem_limit_bytes=GRANT),
     )(owner_order, *same, *other)
 
 
@@ -149,9 +148,9 @@
     for position, turn in enumerate(turns):
         tops = [pl.multiple_of((chip ^ k) * rows, rows) for k in distances(turn, chips)]
         halves = [jnp.concatenate([piece[...] for piece in side], axis=0) for side in pieces[position]]
+        correlation = across(halves[0], source[:, sides[0]]) + across(halves[1], source[:, sides[1]])
         gram = across(halves[0], halves[0]) + across(halves[1], halves[1])
         step = 1.0 / jnp.sum(jnp.abs(gram), axis=1, keepdims=True)
-        correlation = across(halves[0], source[:, sides[0]]) + across(halves[1], source[:, sides[1]])
         before = jnp.concatenate(
             [coefs_ref[pl.ds(pl.multiple_of(turn * kb + top, rows), rows), :] for top in tops], axis=0
         ).astype(jnp.float32)
@@ -296,7 +295,7 @@
 
     place(jnp.concatenate([ref[...] for ref in changes], axis=1), targets_of(coefs), rows, put)
     groups = height // SUBLANES
-    together = UNROLL if groups % UNROLL == 0 and rows * UNROLL <= 64 else 1
+    together = UNROLL if groups % UNROLL == 0 and rows * UNROLL <= 128 else 1
     chunk = together * SUBLANES * rows
     start = turns[0] * local_kb * rows
 
@@ -370,7 +369,7 @@
     laid, turned = lay_coefs(coefs, pixel_of.reshape(1, points), parts)
     laid = [laid[0]] + [over_points(laid[m], m) for m in range(1, parts)]
     base = place_coefs(laid)
-    chosen = pick_turns(owner_order, same, other)
+    chosen = [piece for turns in GROUPS for piece in pick_turns(turns, owner_order, same, other)]
 
     def gather(turn):
         held = [chosen[turn]]

time: 78.6 us -> 79 us (level)
    pallas_call x2, Pallas kernels: 6.17 us -> 5.3 us  [run_maps(): pl.pallas_call(functools.partial(map_kernel, turns, parts, local_kb, firs...]
where the time goes in v5:
time: 79 us; the launch traced here: 78.8 us
  starting transfers between devices  36.9 us (47%)
  waiting for transfers between devices  27.6 us (35%)
  Pallas kernels  12 us (15%)
  local copies, waits for them, and re-layouts  2 us (3%)
    ppermute x39, starting transfers between devices, exchange(): return lax.ppermute(value, axis, [(i, i ^ distance) for i in range(size)])  36.9 us
    ppermute x39, waiting for transfers between devices, exchange(): return lax.ppermute(value, axis, [(i, i ^ distance) for i in range(size)])  27.6 us
    pallas_call x2, Pallas kernels, run_maps(): pl.pallas_call(functools.partial(map_kernel, turns, parts, local_kb, firs...  5.3 us
    pallas_call x2, Pallas kernels, run_turns(): pl.pallas_call(functools.partial(turn_kernel, turns, chips, parts, last),...  4.28 us
    unnamed x11, local copies, waits for them, and re-layouts  2 us
  transfers between devices with their start and end apart: 39, of which 14 were waited for; matrix products, arithmetic and copies ran while one was open for 0% of the time, Pallas kernels for 11%

profile of v5, /device:TPU:0, one launch (start us, length us, event | category | flops | bytes accessed | tf_op | source)
XLA Modules:
  0.0 78.8 jit_solution(14619953035296724380)
XLA Ops:
  0.0 1.2 %copy-done = bf16[256,2048]{1,0:T(8,128)(2,1)S(1)} copy-done((bf16[256,2048]{1,0:T(8,128)(2,1)S(1)}, bf16[256,2048]{1,0:T(8,128)(2,1)}, u32[]{:S(2)}) %copy-start) | copy-done | bytes 1048600
  1.3 3.0 %collective-permute-start = (bf16[64,1024]{1,0:T(8,128)(2,1)S(1)}, bf16[64,1024]{1,0:T(8,128)(2,1)S(1)}, u32[]{:S(2)}, u32[]{:S(2)}) collective-permute-start(bf16[64,1024]{1,0:T(8,128)(2,1)S(1)} %get-tuple-element.33), channel_id=1, source_target_pairs={{0,8},{4,12},{8,0},{12,4},{16,24},{20,28},{24,16},{28,20},{1,9},{5... | collective-permute-start | bytes 393224 | tf_op jit(solution)/shard_map/ppermute | solution.py:353
  4.3 1.5 %collective-permute-start.1 = (bf16[64,1024]{1,0:T(8,128)(2,1)S(1)}, bf16[64,1024]{1,0:T(8,128)(2,1)S(1)}, u32[]{:S(2)}, u32[]{:S(2)}) collective-permute-start(bf16[64,1024]{1,0:T(8,128)(2,1)S(1)} %get-tuple-element.34), channel_id=1, source_target_pairs={{0,16},{4,20},{8,24},{12,28},{16,0},{20,4},{24,8},{28,12},{1,17},{... | collective-permute-start | bytes 393224 | tf_op jit(solution)/shard_map/ppermute | solution.py:353
  5.9 0.5 collective-permute-start.6
  6.4 1.5 %collective-permute-done.refs_1_ = bf16[64,1024]{1,0:T(8,128)(2,1)S(1)} collective-permute-done((bf16[64,1024]{1,0:T(8,128)(2,1)S(1)}, bf16[64,1024]{1,0:T(8,128)(2,1)S(1)}, u32[]{:S(2)}, u32[]{:S(2)}) %collective-permute-start) | collective-permute-done | bytes 131104 | tf_op jit(solution)/shard_map/ppermute | solution.py:353
  7.8 2.7 %collective-permute-start.2 = (bf16[64,1024]{1,0:T(8,128)(2,1)S(1)}, bf16[64,1024]{1,0:T(8,128)(2,1)S(1)}, u32[]{:S(2)}, u32[]{:S(2)}) collective-permute-start(bf16[64,1024]{1,0:T(8,128)(2,1)S(1)} %get-tuple-element.35), channel_id=1, source_target_pairs={{0,24},{4,28},{8,16},{12,20},{16,8},{20,12},{24,0},{28,4},{1,25},{... | collective-permute-start | bytes 393224 | tf_op jit(solution)/shard_map/ppermute | solution.py:353
  10.5 0.6 collective-permute-start.5
  11.1 0.3 collective-permute-start.7
  11.4 2.7 %collective-permute-start.9 = (bf16[64,1024]{1,0:T(8,128)(2,1)S(1)}, bf16[64,1024]{1,0:T(8,128)(2,1)S(1)}, u32[]{:S(2)}, u32[]{:S(2)}) collective-permute-start(bf16[64,1024]{1,0:T(8,128)(2,1)S(1)} %collective-permute-done.8), channel_id=1, source_target_pairs={{0,24},{4,28},{8,16},{12,20},{16,8},{20,12},{24,0},{28,4},{1,25},{... | collective-permute-start | bytes 393224 | tf_op jit(solution)/shard_map/ppermute | solution.py:353
  14.3 2.8 %collective-permute-done.5.refs_5_ = bf16[64,1024]{1,0:T(8,128)(2,1)S(1)} collective-permute-done((bf16[64,1024]{1,0:T(8,128)(2,1)S(1)}, bf16[64,1024]{1,0:T(8,128)(2,1)S(1)}, u32[]{:S(2)}, u32[]{:S(2)}) %collective-permute-start.5) | collective-permute-done | bytes 131104 | tf_op jit(solution)/shard_map/ppermute | solution.py:353
  17.2 2.3 %collective-permute-done.7.refs_6_ = bf16[64,1024]{1,0:T(8,128)(2,1)S(1)} collective-permute-done((bf16[64,1024]{1,0:T(8,128)(2,1)S(1)}, bf16[64,1024]{1,0:T(8,128)(2,1)S(1)}, u32[]{:S(2)}, u32[]{:S(2)}) %collective-permute-start.7) | collective-permute-done | bytes 131104 | tf_op jit(solution)/shard_map/ppermute | solution.py:353
  19.5 0.7 shard_map.55
  20.2 2.3 %collective-permute-start.10 = (bf16[64,1024]{1,0:T(8,128)(2,1)S(1)}, bf16[64,1024]{1,0:T(8,128)(2,1)S(1)}, u32[]{:S(2)}, u32[]{:S(2)}) collective-permute-start(bf16[64,1024]{1,0:T(8,128)(2,1)S(1)} %get-tuple-element.40.refs_2_), channel_id=1, source_target_pairs={{0,8},{4,12},{8,0},{12,4},{16,24},{20,28},{24,16},{28,20},{1,9},{5... | collective-permute-start | bytes 393224 | tf_op jit(solution)/shard_map/ppermute | solution.py:353
  22.5 1.0 %collective-permute-start.15 = (bf16[64,1024]{1,0:T(8,128)(2,1)S(1)}, bf16[64,1024]{1,0:T(8,128)(2,1)S(1)}, u32[]{:S(2)}, u32[]{:S(2)}) collective-permute-start(bf16[64,1024]{1,0:T(8,128)(2,1)S(1)} %get-tuple-element.41.refs_8_), channel_id=1, source_target_pairs={{0,16},{4,20},{8,24},{12,28},{16,0},{20,4},{24,8},{28,12},{1,17},{... | collective-permute-start | bytes 393224 | tf_op jit(solution)/shard_map/ppermute | solution.py:353
  23.6 0.7 copy-done.2
  24.5 1.7 %collective-permute-start.33 = (bf16[272,256]{1,0:T(8,128)(2,1)S(1)}, bf16[272,256]{1,0:T(8,128)(2,1)S(1)}, u32[]{:S(2)}, u32[]{:S(2)}) collective-permute-start(bf16[272,256]{1,0:T(8,128)(2,1)S(1)} %get-tuple-element.50), channel_id=1, source_target_pairs={{0,1},{1,0},{2,3},{3,2},{4,5},{5,4},{6,7},{7,6},{8,9},{9,8},{10,11... | collective-permute-start | bytes 417800 | tf_op jit(solution)/shard_map/ppermute | solution.py:353
  26.1 0.5 collective-permute-start.17
  26.7 0.7 shard_map.57
  27.3 0.5 collective-permute-start.20
  27.8 0.8 collective-permute-start.25
  28.6 1.0 %collective-permute-done.33.refs_1_.refs_5_ = bf16[272,256]{1,0:T(8,128)(2,1)S(1)} collective-permute-done((bf16[272,256]{1,0:T(8,128)(2,1)S(1)}, bf16[272,256]{1,0:T(8,128)(2,1)S(1)}, u32[]{:S(2)}, u32[]{:S(2)}) %collective-permute-start.33) | collective-permute-done | bytes 139296 | tf_op jit(solution)/shard_map/ppermute | solution.py:353
  29.6 1.1 %collective-permute-start.11 = (bf16[128,1024]{1,0:T(8,128)(2,1)S(1)}, bf16[128,1024]{1,0:T(8,128)(2,1)S(1)}, u32[]{:S(2)}, u32[]{:S(2)}) collective-permute-start(bf16[128,1024]{1,0:T(8,128)(2,1)S(1)} %pad_maximum_fusion), channel_id=1, source_target_pairs={{0,16},{4,20},{8,24},{12,28},{16,0},{20,4},{24,8},{28,12},{1,17},{... | collective-permute-start | bytes 786440 | tf_op jit(solution)/shard_map/ppermute | solution.py:353
  30.7 2.1 %collective-permute-done.20.refs_3_ = bf16[64,1024]{1,0:T(8,128)(2,1)S(1)} collective-permute-done((bf16[64,1024]{1,0:T(8,128)(2,1)S(1)}, bf16[64,1024]{1,0:T(8,128)(2,1)S(1)}, u32[]{:S(2)}, u32[]{:S(2)}) %collective-permute-start.20) | collective-permute-done | bytes 131104 | tf_op jit(solution)/shard_map/ppermute | solution.py:353
  32.8 0.4 collective-permute-start.16
  33.3 1.0 %collective-permute-done.25.refs_9_ = bf16[64,1024]{1,0:T(8,128)(2,1)S(1)} collective-permute-done((bf16[64,1024]{1,0:T(8,128)(2,1)S(1)}, bf16[64,1024]{1,0:T(8,128)(2,1)S(1)}, u32[]{:S(2)}, u32[]{:S(2)}) %collective-permute-start.25) | collective-permute-done | bytes 131104 | tf_op jit(solution)/shard_map/ppermute | solution.py:353
  34.3 0.7 collective-permute-start.21
  35.0 2.0 %collective-permute-start.26 = (bf16[128,1024]{1,0:T(8,128)(2,1)S(1)}, bf16[128,1024]{1,0:T(8,128)(2,1)S(1)}, u32[]{:S(2)}, u32[]{:S(2)}) collective-permute-start(bf16[128,1024]{1,0:T(8,128)(2,1)S(1)} %pad_maximum_fusion.3), channel_id=1, source_target_pairs={{0,8},{4,12},{8,0},{12,4},{16,24},{20,28},{24,16},{28,20},{1,9},{5... | collective-permute-start | bytes 786440 | tf_op jit(solution)/shard_map/ppermute | solution.py:353
  37.0 2.9 %collective-permute-done.11.refs_4_ = bf16[128,1024]{1,0:T(8,128)(2,1)S(1)} collective-permute-done((bf16[128,1024]{1,0:T(8,128)(2,1)S(1)}, bf16[128,1024]{1,0:T(8,128)(2,1)S(1)}, u32[]{:S(2)}, u32[]{:S(2)}) %collective-permute-start.11) | collective-permute-done | bytes 262176 | tf_op jit(solution)/shard_map/ppermute | solution.py:353
  39.9 2.1 %collective-permute-done.16.refs_10_ = bf16[128,1024]{1,0:T(8,128)(2,1)S(1)} collective-permute-done((bf16[128,1024]{1,0:T(8,128)(2,1)S(1)}, bf16[128,1024]{1,0:T(8,128)(2,1)S(1)}, u32[]{:S(2)}, u32[]{:S(2)}) %collective-permute-start.16) | collective-permute-done | bytes 262176 | tf_op jit(solution)/shard_map/ppermute | solution.py:353
  42.0 0.5 collective-permute-start.18
  42.5 1.8 %collective-permute-done.21.refs_4_ = bf16[128,1024]{1,0:T(8,128)(2,1)S(1)} collective-permute-done((bf16[128,1024]{1,0:T(8,128)(2,1)S(1)}, bf16[128,1024]{1,0:T(8,128)(2,1)S(1)}, u32[]{:S(2)}, u32[]{:S(2)}) %collective-permute-start.21) | collective-permute-done | bytes 262176 | tf_op jit(solution)/shard_map/ppermute | solution.py:353
  44.3 1.5 %collective-permute-done.26.refs_10_ = bf16[128,1024]{1,0:T(8,128)(2,1)S(1)} collective-permute-done((bf16[128,1024]{1,0:T(8,128)(2,1)S(1)}, bf16[128,1024]{1,0:T(8,128)(2,1)S(1)}, u32[]{:S(2)}, u32[]{:S(2)}) %collective-permute-start.26) | collective-permute-done | bytes 262176 | tf_op jit(solution)/shard_map/ppermute | solution.py:353
  45.8 0.5 collective-permute-start.27
  46.4 0.4 collective-permute-start.28
  46.8 2.4 %shard_map.56 = (bf16[256,2048]{1,0:T(8,128)(2,1)S(1)}, bf16[128,256]{1,0:T(8,128)(2,1)S(1)}, bf16[128,256]{1,0:T(8,128)(2,1)S(1)}, bf16[128,256]{1,0:T(8,128)(2,1)S(1)}, bf16[128,256]{1,0:T(8,128)(2,1)S(1)}) custom-call(bf16[256,2048]{1,0:T(8,128)(2,1)S(1)} %bitcast.6, bf16[1024,256]{1,0:T(8,128)(2,1)S(1)} %get-tuple-element.31.refs_1_, ...), custom_call_target="tpu_custom_call" | custom-call | flops 1610612736 | bytes 4194304 | tf_op jit(solution)/shard_map/pallas_call | solution.py:185
  49.2 2.7 %collective-permute-start.34 = (bf16[272,256]{1,0:T(8,128)(2,1)S(1)}, bf16[272,256]{1,0:T(8,128)(2,1)S(1)}, u32[]{:S(2)}, u32[]{:S(2)}) collective-permute-start(bf16[272,256]{1,0:T(8,128)(2,1)S(1)} %get-tuple-element.51), channel_id=1, source_target_pairs={{0,2},{1,3},{2,0},{3,1},{4,6},{5,7},{6,4},{7,5},{8,10},{9,11},{10,... | collective-permute-start | bytes 417800 | tf_op jit(solution)/shard_map/ppermute | solution.py:353
  52.1 0.7 collective-permute-start.36
  52.8 3.5 %collective-permute-start.37 = (bf16[128,256]{1,0:T(8,128)(2,1)S(1)}, bf16[128,256]{1,0:T(8,128)(2,1)S(1)}, u32[]{:S(2)}, u32[]{:S(2)}) collective-permute-start(bf16[128,256]{1,0:T(8,128)(2,1)S(1)} %get-tuple-element.55), channel_id=1, source_target_pairs={{0,2},{1,3},{2,0},{3,1},{4,6},{5,7},{6,4},{7,5},{8,10},{9,11},{10,... | collective-permute-start | bytes 196616 | tf_op jit(solution)/shard_map/ppermute | solution.py:353
  56.5 1.9 %shard_map.58 = (bf16[128,256]{1,0:T(8,128)(2,1)S(1)}, bf16[128,256]{1,0:T(8,128)(2,1)S(1)}, bf16[128,256]{1,0:T(8,128)(2,1)S(1)}, bf16[128,256]{1,0:T(8,128)(2,1)S(1)}) custom-call(bf16[256,2048]{1,0:T(8,128)(2,1)S(1)} %get-tuple-element.42.refs_0_, bf16[1024,256]{1,0:T(8,128)(2,1)S(1)} %get-tuple-element.31.refs_1_, ...), custom_call_target="tpu_custom_call" | custom-call | flops 1610612736 | bytes 4194304 | tf_op jit(solution)/shard_map/pallas_call | solution.py:185
  58.4 6.2 %collective-permute-done.34.refs_2_.refs_6_ = bf16[272,256]{1,0:T(8,128)(2,1)S(1)} collective-permute-done((bf16[272,256]{1,0:T(8,128)(2,1)S(1)}, bf16[272,256]{1,0:T(8,128)(2,1)S(1)}, u32[]{:S(2)}, u32[]{:S(2)}) %collective-permute-start.34) | collective-permute-done | bytes 139296 | tf_op jit(solution)/shard_map/ppermute | solution.py:353
  64.6 0.6 collective-permute-start.30
  65.2 4.9 %collective-permute-start.31 = (bf16[128,256]{1,0:T(8,128)(2,1)S(1)}, bf16[128,256]{1,0:T(8,128)(2,1)S(1)}, u32[]{:S(2)}, u32[]{:S(2)}) collective-permute-start(bf16[128,256]{1,0:T(8,128)(2,1)S(1)} %get-tuple-element.47), channel_id=1, source_target_pairs={{0,2},{1,3},{2,0},{3,1},{4,6},{5,7},{6,4},{7,5},{8,10},{9,11},{10,... | collective-permute-start | bytes 196616 | tf_op jit(solution)/shard_map/ppermute | solution.py:353
  70.1 0.4 collective-permute-start.32
  70.5 0.8 place.1.refs_8_
  71.3 2.7 %shard_map.59.refs_9_ = f32[2048,128]{1,0:T(8,128)} custom-call(bf16[128,256]{1,0:T(8,128)(2,1)S(1)} %get-tuple-element.53.refs_0_, bf16[128,256]{1,0:T(8,128)(2,1)S(1)} %collective-permute-done.36.refs_1_, bf16[128,256]{1,0:T(8,128)(2,1)S(1)} %collective-permute-done.37.refs_2_, bf16[128,256]{1,0:T(8,128)(2,1)S(1)} %collective-permute-done.38.refs_3_, ...), custom_call_target="tpu_custom_call" | custom-call | flops 268435456 | bytes 1048576 | tf_op jit(solution)/shard_map/pallas_call | solution.py:332
  74.0 0.6 collective-permute-done.31.refs_2_
  74.6 1.6 %collective-permute-done.32.refs_3_ = bf16[128,256]{1,0:T(8,128)(2,1)S(1)} collective-permute-done((bf16[128,256]{1,0:T(8,128)(2,1)S(1)}, bf16[128,256]{1,0:T(8,128)(2,1)S(1)}, u32[]{:S(2)}, u32[]{:S(2)}) %collective-permute-start.32) | collective-permute-done | bytes 65568 | tf_op jit(solution)/shard_map/ppermute | solution.py:353
  76.1 2.6 %shard_map.60 = f32[2048,128]{1,0:T(8,128)} custom-call(bf16[128,256]{1,0:T(8,128)(2,1)S(1)} %get-tuple-element.45.refs_0_, bf16[128,256]{1,0:T(8,128)(2,1)S(1)} %collective-permute-done.30.refs_1_, bf16[128,256]{1,0:T(8,128)(2,1)S(1)} %collective-permute-done.31.refs_2_, ...), custom_call_target="tpu_custom_call", output_to_operand_aliasing={{}: (9, {})} | custom-call | flops 268435456 | bytes 1048576 | tf_op jit(solution)/shard_map/pallas_call | solution.py:332
  (54 shorter events, 1.4 us)
Async XLA Ops:
  0.0 1.2 %copy-start = (bf16[256,2048]{1,0:T(8,128)(2,1)S(1)}, bf16[256,2048]{1,0:T(8,128)(2,1)}, u32[]{:S(2)}) copy-start(bf16[256,2048]{1,0:T(8,128)(2,1)} %block_ref.1) | copy-start | bytes 3145732
  1.3 6.5 %collective-permute-start = (bf16[64,1024]{1,0:T(8,128)(2,1)S(1)}, bf16[64,1024]{1,0:T(8,128)(2,1)S(1)}, u32[]{:S(2)}, u32[]{:S(2)}) collective-permute-start(bf16[64,1024]{1,0:T(8,128)(2,1)S(1)} %get-tuple-element.33), channel_id=1, source_target_pairs={{0,8},{4,12},{8,0},{12,4},{16,24},{20,28},{24,16},{28,20},{1,9},{5... | collective-permute-start | bytes 393224 | tf_op jit(solution)/shard_map/ppermute | solution.py:353
  4.3 6.2 %collective-permute-start.1 = (bf16[64,1024]{1,0:T(8,128)(2,1)S(1)}, bf16[64,1024]{1,0:T(8,128)(2,1)S(1)}, u32[]{:S(2)}, u32[]{:S(2)}) collective-permute-start(bf16[64,1024]{1,0:T(8,128)(2,1)S(1)} %get-tuple-element.34), channel_id=1, source_target_pairs={{0,16},{4,20},{8,24},{12,28},{16,0},{20,4},{24,8},{28,12},{1,17},{... | collective-permute-start | bytes 393224 | tf_op jit(solution)/shard_map/ppermute | solution.py:353
  5.8 4.7 %collective-permute-start.4 = (bf16[64,1024]{1,0:T(8,128)(2,1)S(1)}, bf16[64,1024]{1,0:T(8,128)(2,1)S(1)}, u32[]{:S(2)}, u32[]{:S(2)}) collective-permute-start(bf16[64,1024]{1,0:T(8,128)(2,1)S(1)} %get-tuple-element.37), channel_id=1, source_target_pairs={{0,4},{4,0},{8,12},{12,8},{16,20},{20,16},{24,28},{28,24},{1,5},{5... | collective-permute-start | bytes 393224 | tf_op jit(solution)/shard_map/ppermute | solution.py:353
  5.9 5.3 %collective-permute-start.6 = (bf16[64,1024]{1,0:T(8,128)(2,1)S(1)}, bf16[64,1024]{1,0:T(8,128)(2,1)S(1)}, u32[]{:S(2)}, u32[]{:S(2)}) collective-permute-start(bf16[64,1024]{1,0:T(8,128)(2,1)S(1)} %get-tuple-element.38), channel_id=1, source_target_pairs={{0,4},{4,0},{8,12},{12,8},{16,20},{20,16},{24,28},{28,24},{1,5},{5... | collective-permute-start | bytes 393224 | tf_op jit(solution)/shard_map/ppermute | solution.py:353
  6.4 5.1 %collective-permute-start.8 = (bf16[64,1024]{1,0:T(8,128)(2,1)S(1)}, bf16[64,1024]{1,0:T(8,128)(2,1)S(1)}, u32[]{:S(2)}, u32[]{:S(2)}) collective-permute-start(bf16[64,1024]{1,0:T(8,128)(2,1)S(1)} %get-tuple-element.39), channel_id=1, source_target_pairs={{0,4},{4,0},{8,12},{12,8},{16,20},{20,16},{24,28},{28,24},{1,5},{5... | collective-permute-start | bytes 393224 | tf_op jit(solution)/shard_map/ppermute | solution.py:353
  7.8 6.5 %collective-permute-start.2 = (bf16[64,1024]{1,0:T(8,128)(2,1)S(1)}, bf16[64,1024]{1,0:T(8,128)(2,1)S(1)}, u32[]{:S(2)}, u32[]{:S(2)}) collective-permute-start(bf16[64,1024]{1,0:T(8,128)(2,1)S(1)} %get-tuple-element.35), channel_id=1, source_target_pairs={{0,24},{4,28},{8,16},{12,20},{16,8},{20,12},{24,0},{28,4},{1,25},{... | collective-permute-start | bytes 393224 | tf_op jit(solution)/shard_map/ppermute | solution.py:353
  10.5 9.0 %copy-start.1 = (s32[8]{0:T(128)S(1)}, s32[8]{0:T(128)}, u32[]{:S(2)}) copy-start(s32[8]{0:T(128)} %order_ref.3) | copy-start | bytes 100
  10.5 3.8 %collective-permute-start.3 = (bf16[64,1024]{1,0:T(8,128)(2,1)S(1)}, bf16[64,1024]{1,0:T(8,128)(2,1)S(1)}, u32[]{:S(2)}, u32[]{:S(2)}) collective-permute-start(bf16[64,1024]{1,0:T(8,128)(2,1)S(1)} %get-tuple-element.36), channel_id=1, source_target_pairs={{0,4},{4,0},{8,12},{12,8},{16,20},{20,16},{24,28},{28,24},{1,5},{5... | collective-permute-start | bytes 393224 | tf_op jit(solution)/shard_map/ppermute | solution.py:353
  10.5 6.6 %collective-permute-start.5 = (bf16[64,1024]{1,0:T(8,128)(2,1)S(1)}, bf16[64,1024]{1,0:T(8,128)(2,1)S(1)}, u32[]{:S(2)}, u32[]{:S(2)}) collective-permute-start(bf16[64,1024]{1,0:T(8,128)(2,1)S(1)} %collective-permute-done.4), channel_id=1, source_target_pairs={{0,8},{4,12},{8,0},{12,4},{16,24},{20,28},{24,16},{28,20},{1,9},{5... | collective-permute-start | bytes 393224 | tf_op jit(solution)/shard_map/ppermute | solution.py:353
  11.1 8.4 %collective-permute-start.7 = (bf16[64,1024]{1,0:T(8,128)(2,1)S(1)}, bf16[64,1024]{1,0:T(8,128)(2,1)S(1)}, u32[]{:S(2)}, u32[]{:S(2)}) collective-permute-start(bf16[64,1024]{1,0:T(8,128)(2,1)S(1)} %collective-permute-done.6), channel_id=1, source_target_pairs={{0,16},{4,20},{8,24},{12,28},{16,0},{20,4},{24,8},{28,12},{1,17},{... | collective-permute-start | bytes 393224 | tf_op jit(solution)/shard_map/ppermute | solution.py:353
  11.4 8.1 %collective-permute-start.9 = (bf16[64,1024]{1,0:T(8,128)(2,1)S(1)}, bf16[64,1024]{1,0:T(8,128)(2,1)S(1)}, u32[]{:S(2)}, u32[]{:S(2)}) collective-permute-start(bf16[64,1024]{1,0:T(8,128)(2,1)S(1)} %collective-permute-done.8), channel_id=1, source_target_pairs={{0,24},{4,28},{8,16},{12,20},{16,8},{20,12},{24,0},{28,4},{1,25},{... | collective-permute-start | bytes 393224 | tf_op jit(solution)/shard_map/ppermute | solution.py:353
  19.5 3.9 %copy-start.4 = (bf16[1,256,4,256]{3,2,1,0:T(4,128)(2,1)S(1)}, bf16[1,256,4,256]{3,2,1,0:T(4,128)(2,1)}, u32[]{:S(2)}) copy-start(bf16[1,256,4,256]{3,2,1,0:T(4,128)(2,1)} %param.6) | copy-start | bytes 1572868
  20.2 7.1 %collective-permute-start.10 = (bf16[64,1024]{1,0:T(8,128)(2,1)S(1)}, bf16[64,1024]{1,0:T(8,128)(2,1)S(1)}, u32[]{:S(2)}, u32[]{:S(2)}) collective-permute-start(bf16[64,1024]{1,0:T(8,128)(2,1)S(1)} %get-tuple-element.40.refs_2_), channel_id=1, source_target_pairs={{0,8},{4,12},{8,0},{12,4},{16,24},{20,28},{24,16},{28,20},{1,9},{5... | collective-permute-start | bytes 393224 | tf_op jit(solution)/shard_map/ppermute | solution.py:353
  22.5 5.4 %collective-permute-start.15 = (bf16[64,1024]{1,0:T(8,128)(2,1)S(1)}, bf16[64,1024]{1,0:T(8,128)(2,1)S(1)}, u32[]{:S(2)}, u32[]{:S(2)}) collective-permute-start(bf16[64,1024]{1,0:T(8,128)(2,1)S(1)} %get-tuple-element.41.refs_8_), channel_id=1, source_target_pairs={{0,16},{4,20},{8,24},{12,28},{16,0},{20,4},{24,8},{28,12},{1,17},{... | collective-permute-start | bytes 393224 | tf_op jit(solution)/shard_map/ppermute | solution.py:353
  23.5 0.7 copy-start.2
  24.5 5.1 %collective-permute-start.33 = (bf16[272,256]{1,0:T(8,128)(2,1)S(1)}, bf16[272,256]{1,0:T(8,128)(2,1)S(1)}, u32[]{:S(2)}, u32[]{:S(2)}) collective-permute-start(bf16[272,256]{1,0:T(8,128)(2,1)S(1)} %get-tuple-element.50), channel_id=1, source_target_pairs={{0,1},{1,0},{2,3},{3,2},{4,5},{5,4},{6,7},{7,6},{8,9},{9,8},{10,11... | collective-permute-start | bytes 417800 | tf_op jit(solution)/shard_map/ppermute | solution.py:353
  26.1 7.1 %collective-permute-start.12 = (bf16[64,1024]{1,0:T(8,128)(2,1)S(1)}, bf16[64,1024]{1,0:T(8,128)(2,1)S(1)}, u32[]{:S(2)}, u32[]{:S(2)}) collective-permute-start(bf16[64,1024]{1,0:T(8,128)(2,1)S(1)} %get-tuple-element.40.refs_2_), channel_id=1, source_target_pairs={{0,4},{4,0},{8,12},{12,8},{16,20},{20,16},{24,28},{28,24},{1,5},{5... | collective-permute-start | bytes 393224 | tf_op jit(solution)/shard_map/ppermute | solution.py:353
  26.1 8.8 %collective-permute-start.17 = (bf16[64,1024]{1,0:T(8,128)(2,1)S(1)}, bf16[64,1024]{1,0:T(8,128)(2,1)S(1)}, u32[]{:S(2)}, u32[]{:S(2)}) collective-permute-start(bf16[64,1024]{1,0:T(8,128)(2,1)S(1)} %get-tuple-element.41.refs_8_), channel_id=1, source_target_pairs={{0,4},{4,0},{8,12},{12,8},{16,20},{20,16},{24,28},{28,24},{1,5},{5... | collective-permute-start | bytes 393224 | tf_op jit(solution)/shard_map/ppermute | solution.py:353
  27.3 19.5 %copy-start.3 = (bf16[1,256,2048]{2,1,0:T(8,128)(2,1)S(1)}, bf16[1,256,2048]{2,1,0:T(8,128)(2,1)}, u32[]{:S(2)}) copy-start(bf16[1,256,2048]{2,1,0:T(8,128)(2,1)} %param.5) | copy-start | bytes 3145732
  27.3 5.5 %collective-permute-start.20 = (bf16[64,1024]{1,0:T(8,128)(2,1)S(1)}, bf16[64,1024]{1,0:T(8,128)(2,1)S(1)}, u32[]{:S(2)}, u32[]{:S(2)}) collective-permute-start(bf16[64,1024]{1,0:T(8,128)(2,1)S(1)} %get-tuple-element.43.refs_2_), channel_id=1, source_target_pairs={{0,8},{4,12},{8,0},{12,4},{16,24},{20,28},{24,16},{28,20},{1,9},{5... | collective-permute-start | bytes 393224 | tf_op jit(solution)/shard_map/ppermute | solution.py:353
  27.8 6.4 %collective-permute-start.25 = (bf16[64,1024]{1,0:T(8,128)(2,1)S(1)}, bf16[64,1024]{1,0:T(8,128)(2,1)S(1)}, u32[]{:S(2)}, u32[]{:S(2)}) collective-permute-start(bf16[64,1024]{1,0:T(8,128)(2,1)S(1)} %get-tuple-element.44.refs_8_), channel_id=1, source_target_pairs={{0,16},{4,20},{8,24},{12,28},{16,0},{20,4},{24,8},{28,12},{1,17},{... | collective-permute-start | bytes 393224 | tf_op jit(solution)/shard_map/ppermute | solution.py:353
  29.6 10.3 %collective-permute-start.11 = (bf16[128,1024]{1,0:T(8,128)(2,1)S(1)}, bf16[128,1024]{1,0:T(8,128)(2,1)S(1)}, u32[]{:S(2)}, u32[]{:S(2)}) collective-permute-start(bf16[128,1024]{1,0:T(8,128)(2,1)S(1)} %pad_maximum_fusion), channel_id=1, source_target_pairs={{0,16},{4,20},{8,24},{12,28},{16,0},{20,4},{24,8},{28,12},{1,17},{... | collective-permute-start | bytes 786440 | tf_op jit(solution)/shard_map/ppermute | solution.py:353
  32.8 9.2 %collective-permute-start.16 = (bf16[128,1024]{1,0:T(8,128)(2,1)S(1)}, bf16[128,1024]{1,0:T(8,128)(2,1)S(1)}, u32[]{:S(2)}, u32[]{:S(2)}) collective-permute-start(bf16[128,1024]{1,0:T(8,128)(2,1)S(1)} %pad_maximum_fusion.1), channel_id=1, source_target_pairs={{0,8},{4,12},{8,0},{12,4},{16,24},{20,28},{24,16},{28,20},{1,9},{5... | collective-permute-start | bytes 786440 | tf_op jit(solution)/shard_map/ppermute | solution.py:353
  33.2 3.8 %collective-permute-start.22 = (bf16[64,1024]{1,0:T(8,128)(2,1)S(1)}, bf16[64,1024]{1,0:T(8,128)(2,1)S(1)}, u32[]{:S(2)}, u32[]{:S(2)}) collective-permute-start(bf16[64,1024]{1,0:T(8,128)(2,1)S(1)} %get-tuple-element.43.refs_2_), channel_id=1, source_target_pairs={{0,4},{4,0},{8,12},{12,8},{16,20},{20,16},{24,28},{28,24},{1,5},{5... | collective-permute-start | bytes 393224 | tf_op jit(solution)/shard_map/ppermute | solution.py:353
  34.3 10.0 %collective-permute-start.21 = (bf16[128,1024]{1,0:T(8,128)(2,1)S(1)}, bf16[128,1024]{1,0:T(8,128)(2,1)S(1)}, u32[]{:S(2)}, u32[]{:S(2)}) collective-permute-start(bf16[128,1024]{1,0:T(8,128)(2,1)S(1)} %pad_maximum_fusion.2), channel_id=1, source_target_pairs={{0,16},{4,20},{8,24},{12,28},{16,0},{20,4},{24,8},{28,12},{1,17},{... | collective-permute-start | bytes 786440 | tf_op jit(solution)/shard_map/ppermute | solution.py:353
  35.0 10.8 %collective-permute-start.26 = (bf16[128,1024]{1,0:T(8,128)(2,1)S(1)}, bf16[128,1024]{1,0:T(8,128)(2,1)S(1)}, u32[]{:S(2)}, u32[]{:S(2)}) collective-permute-start(bf16[128,1024]{1,0:T(8,128)(2,1)S(1)} %pad_maximum_fusion.3), channel_id=1, source_target_pairs={{0,8},{4,12},{8,0},{12,4},{16,24},{20,28},{24,16},{28,20},{1,9},{5... | collective-permute-start | bytes 786440 | tf_op jit(solution)/shard_map/ppermute | solution.py:353
  37.0 5.0 %collective-permute-start.13 = (bf16[64,1024]{1,0:T(8,128)(2,1)S(1)}, bf16[64,1024]{1,0:T(8,128)(2,1)S(1)}, u32[]{:S(2)}, u32[]{:S(2)}) collective-permute-start(bf16[64,1024]{1,0:T(8,128)(2,1)S(1)} %collective-permute-done.10.refs_3_), channel_id=1, source_target_pairs={{0,4},{4,0},{8,12},{12,8},{16,20},{20,16},{24,28},{28,24},{1,5},{5... | collective-permute-start | bytes 393224 | tf_op jit(solution)/shard_map/ppermute | solution.py:353
  39.9 6.4 %collective-permute-start.14 = (bf16[128,1024]{1,0:T(8,128)(2,1)S(1)}, bf16[128,1024]{1,0:T(8,128)(2,1)S(1)}, u32[]{:S(2)}, u32[]{:S(2)}) collective-permute-start(bf16[128,1024]{1,0:T(8,128)(2,1)S(1)} %collective-permute-done.11.refs_4_), channel_id=1, source_target_pairs={{0,4},{4,0},{8,12},{12,8},{16,20},{20,16},{24,28},{28,24},{1,5},{5... | collective-permute-start | bytes 786440 | tf_op jit(solution)/shard_map/ppermute | solution.py:353
  42.0 4.4 %collective-permute-start.19 = (bf16[128,1024]{1,0:T(8,128)(2,1)S(1)}, bf16[128,1024]{1,0:T(8,128)(2,1)S(1)}, u32[]{:S(2)}, u32[]{:S(2)}) collective-permute-start(bf16[128,1024]{1,0:T(8,128)(2,1)S(1)} %collective-permute-done.16.refs_10_), channel_id=1, source_target_pairs={{0,4},{4,0},{8,12},{12,8},{16,20},{20,16},{24,28},{28,24},{1,5},{5... | collective-permute-start | bytes 786440 | tf_op jit(solution)/shard_map/ppermute | solution.py:353
  42.0 3.8 %collective-permute-start.18 = (bf16[64,1024]{1,0:T(8,128)(2,1)S(1)}, bf16[64,1024]{1,0:T(8,128)(2,1)S(1)}, u32[]{:S(2)}, u32[]{:S(2)}) collective-permute-start(bf16[64,1024]{1,0:T(8,128)(2,1)S(1)} %collective-permute-done.15.refs_9_), channel_id=1, source_target_pairs={{0,4},{4,0},{8,12},{12,8},{16,20},{20,16},{24,28},{28,24},{1,5},{5... | collective-permute-start | bytes 393224 | tf_op jit(solution)/shard_map/ppermute | solution.py:353
  44.3 8.5 %collective-permute-start.24 = (bf16[128,1024]{1,0:T(8,128)(2,1)S(1)}, bf16[128,1024]{1,0:T(8,128)(2,1)S(1)}, u32[]{:S(2)}, u32[]{:S(2)}) collective-permute-start(bf16[128,1024]{1,0:T(8,128)(2,1)S(1)} %collective-permute-done.21.refs_4_), channel_id=1, source_target_pairs={{0,4},{4,0},{8,12},{12,8},{16,20},{20,16},{24,28},{28,24},{1,5},{5... | collective-permute-start | bytes 786440 | tf_op jit(solution)/shard_map/ppermute | solution.py:353
  45.8 10.5 %collective-permute-start.29 = (bf16[128,1024]{1,0:T(8,128)(2,1)S(1)}, bf16[128,1024]{1,0:T(8,128)(2,1)S(1)}, u32[]{:S(2)}, u32[]{:S(2)}) collective-permute-start(bf16[128,1024]{1,0:T(8,128)(2,1)S(1)} %collective-permute-done.26.refs_10_), channel_id=1, source_target_pairs={{0,4},{4,0},{8,12},{12,8},{16,20},{20,16},{24,28},{28,24},{1,5},{5... | collective-permute-start | bytes 786440 | tf_op jit(solution)/shard_map/ppermute | solution.py:353
  45.8 3.4 %collective-permute-start.27 = (bf16[64,1024]{1,0:T(8,128)(2,1)S(1)}, bf16[64,1024]{1,0:T(8,128)(2,1)S(1)}, u32[]{:S(2)}, u32[]{:S(2)}) collective-permute-start(bf16[64,1024]{1,0:T(8,128)(2,1)S(1)} %get-tuple-element.44.refs_8_), channel_id=1, source_target_pairs={{0,4},{4,0},{8,12},{12,8},{16,20},{20,16},{24,28},{28,24},{1,5},{5... | collective-permute-start | bytes 393224 | tf_op jit(solution)/shard_map/ppermute | solution.py:353
  46.3 5.5 %collective-permute-start.23 = (bf16[64,1024]{1,0:T(8,128)(2,1)S(1)}, bf16[64,1024]{1,0:T(8,128)(2,1)S(1)}, u32[]{:S(2)}, u32[]{:S(2)}) collective-permute-start(bf16[64,1024]{1,0:T(8,128)(2,1)S(1)} %collective-permute-done.20.refs_3_), channel_id=1, source_target_pairs={{0,4},{4,0},{8,12},{12,8},{16,20},{20,16},{24,28},{28,24},{1,5},{5... | collective-permute-start | bytes 393224 | tf_op jit(solution)/shard_map/ppermute | solution.py:353
  46.4 5.7 %collective-permute-start.28 = (bf16[64,1024]{1,0:T(8,128)(2,1)S(1)}, bf16[64,1024]{1,0:T(8,128)(2,1)S(1)}, u32[]{:S(2)}, u32[]{:S(2)}) collective-permute-start(bf16[64,1024]{1,0:T(8,128)(2,1)S(1)} %collective-permute-done.25.refs_9_), channel_id=1, source_target_pairs={{0,4},{4,0},{8,12},{12,8},{16,20},{20,16},{24,28},{28,24},{1,5},{5... | collective-permute-start | bytes 393224 | tf_op jit(solution)/shard_map/ppermute | solution.py:353
  49.2 15.4 %collective-permute-start.34 = (bf16[272,256]{1,0:T(8,128)(2,1)S(1)}, bf16[272,256]{1,0:T(8,128)(2,1)S(1)}, u32[]{:S(2)}, u32[]{:S(2)}) collective-permute-start(bf16[272,256]{1,0:T(8,128)(2,1)S(1)} %get-tuple-element.51), channel_id=1, source_target_pairs={{0,2},{1,3},{2,0},{3,1},{4,6},{5,7},{6,4},{7,5},{8,10},{9,11},{10,... | collective-permute-start | bytes 417800 | tf_op jit(solution)/shard_map/ppermute | solution.py:353
  51.9 13.3 %collective-permute-start.35 = (bf16[272,256]{1,0:T(8,128)(2,1)S(1)}, bf16[272,256]{1,0:T(8,128)(2,1)S(1)}, u32[]{:S(2)}, u32[]{:S(2)}) collective-permute-start(bf16[272,256]{1,0:T(8,128)(2,1)S(1)} %get-tuple-element.52), channel_id=1, source_target_pairs={{0,3},{1,2},{2,1},{3,0},{4,7},{5,6},{6,5},{7,4},{8,11},{9,10},{10,... | collective-permute-start | bytes 417800 | tf_op jit(solution)/shard_map/ppermute | solution.py:353
  52.1 18.0 %collective-permute-start.36 = (bf16[128,256]{1,0:T(8,128)(2,1)S(1)}, bf16[128,256]{1,0:T(8,128)(2,1)S(1)}, u32[]{:S(2)}, u32[]{:S(2)}) collective-permute-start(bf16[128,256]{1,0:T(8,128)(2,1)S(1)} %get-tuple-element.54), channel_id=1, source_target_pairs={{0,1},{1,0},{2,3},{3,2},{4,5},{5,4},{6,7},{7,6},{8,9},{9,8},{10,11... | collective-permute-start | bytes 196616 | tf_op jit(solution)/shard_map/ppermute | solution.py:353
  52.8 18.5 %collective-permute-start.37 = (bf16[128,256]{1,0:T(8,128)(2,1)S(1)}, bf16[128,256]{1,0:T(8,128)(2,1)S(1)}, u32[]{:S(2)}, u32[]{:S(2)}) collective-permute-start(bf16[128,256]{1,0:T(8,128)(2,1)S(1)} %get-tuple-element.55), channel_id=1, source_target_pairs={{0,2},{1,3},{2,0},{3,1},{4,6},{5,7},{6,4},{7,5},{8,10},{9,11},{10,... | collective-permute-start | bytes 196616 | tf_op jit(solution)/shard_map/ppermute | solution.py:353
  56.3 15.0 %collective-permute-start.38 = (bf16[128,256]{1,0:T(8,128)(2,1)S(1)}, bf16[128,256]{1,0:T(8,128)(2,1)S(1)}, u32[]{:S(2)}, u32[]{:S(2)}) collective-permute-start(bf16[128,256]{1,0:T(8,128)(2,1)S(1)} %get-tuple-element.56), channel_id=1, source_target_pairs={{0,3},{1,2},{2,1},{3,0},{4,7},{5,6},{6,5},{7,4},{8,11},{9,10},{10,... | collective-permute-start | bytes 196616 | tf_op jit(solution)/shard_map/ppermute | solution.py:353
  64.6 9.4 %collective-permute-start.30 = (bf16[128,256]{1,0:T(8,128)(2,1)S(1)}, bf16[128,256]{1,0:T(8,128)(2,1)S(1)}, u32[]{:S(2)}, u32[]{:S(2)}) collective-permute-start(bf16[128,256]{1,0:T(8,128)(2,1)S(1)} %get-tuple-element.46), channel_id=1, source_target_pairs={{0,1},{1,0},{2,3},{3,2},{4,5},{5,4},{6,7},{7,6},{8,9},{9,8},{10,11... | collective-permute-start | bytes 196616 | tf_op jit(solution)/shard_map/ppermute | solution.py:353
  65.2 9.4 %collective-permute-start.31 = (bf16[128,256]{1,0:T(8,128)(2,1)S(1)}, bf16[128,256]{1,0:T(8,128)(2,1)S(1)}, u32[]{:S(2)}, u32[]{:S(2)}) collective-permute-start(bf16[128,256]{1,0:T(8,128)(2,1)S(1)} %get-tuple-element.47), channel_id=1, source_target_pairs={{0,2},{1,3},{2,0},{3,1},{4,6},{5,7},{6,4},{7,5},{8,10},{9,11},{10,... | collective-permute-start | bytes 196616 | tf_op jit(solution)/shard_map/ppermute | solution.py:353
  70.1 6.1 %collective-permute-start.32 = (bf16[128,256]{1,0:T(8,128)(2,1)S(1)}, bf16[128,256]{1,0:T(8,128)(2,1)S(1)}, u32[]{:S(2)}, u32[]{:S(2)}) collective-permute-start(bf16[128,256]{1,0:T(8,128)(2,1)S(1)} %get-tuple-element.48), channel_id=1, source_target_pairs={{0,3},{1,2},{2,1},{3,0},{4,7},{5,6},{6,5},{7,4},{8,11},{9,10},{10,... | collective-permute-start | bytes 196616 | tf_op jit(solution)/shard_map/ppermute | solution.py:353

commit v6 on v5

--- a/solution.py
+++ b/solution.py
@@ -12,7 +12,7 @@
 SWEEPS = 4
 MAP_W = 128
 SUBLANES = 8
-UNROLL = 16
+UNROLL = 8
 TILE_ROWS = 16
 GRANT = 16 * 1024 * 1024
 
@@ -295,7 +295,7 @@
 
     place(jnp.concatenate([ref[...] for ref in changes], axis=1), targets_of(coefs), rows, put)
     groups = height // SUBLANES
-    together = UNROLL if groups % UNROLL == 0 and rows * UNROLL <= 128 else 1
+    together = UNROLL if groups % UNROLL == 0 and rows * UNROLL <= 64 else 1
     chunk = together * SUBLANES * rows
     start = turns[0] * local_kb * rows
 
@@ -317,7 +317,7 @@
         ).start()
         return carry
 
-    lax.fori_loop(0, groups // together, one, 0)
+    lax.fori_loop(0, groups // together, one, 0, unroll=groups // together <= 2)
     pltpu.make_async_copy(staged, out_ref.at[pl.ds(start, height * rows)], sem).wait()
 
 

time: 79 us -> 78.9 us (level)
  no operation moved by 1% of the time
where the time goes in v6:
time: 78.9 us; the launch traced here: 78.7 us
  starting transfers between devices  36.9 us (47%)
  waiting for transfers between devices  27.7 us (35%)
  Pallas kernels  11.8 us (15%)
  local copies, waits for them, and re-layouts  2 us (3%)
    ppermute x39, starting transfers between devices, exchange(): return lax.ppermute(value, axis, [(i, i ^ distance) for i in range(size)])  36.9 us
    ppermute x39, waiting for transfers between devices, exchange(): return lax.ppermute(value, axis, [(i, i ^ distance) for i in range(size)])  27.7 us
    pallas_call x2, Pallas kernels, run_maps(): pl.pallas_call(functools.partial(map_kernel, turns, parts, local_kb, firs...  5.18 us
    pallas_call x2, Pallas kernels, run_turns(): pl.pallas_call(functools.partial(turn_kernel, turns, chips, parts, last),...  4.28 us
    unnamed x11, local copies, waits for them, and re-layouts  2 us
  transfers between devices with their start and end apart: 39, of which 14 were waited for; matrix products, arithmetic and copies ran while one was open for 0% of the time, Pallas kernels for 11%

profile of v6, /device:TPU:0, one launch (start us, length us, event | category | flops | bytes accessed | tf_op | source)
XLA Modules:
  0.0 78.7 jit_solution(6012287890977829192)
XLA Ops:
  0.0 1.2 %copy-done = bf16[256,2048]{1,0:T(8,128)(2,1)S(1)} copy-done((bf16[256,2048]{1,0:T(8,128)(2,1)S(1)}, bf16[256,2048]{1,0:T(8,128)(2,1)}, u32[]{:S(2)}) %copy-start) | copy-done | bytes 1048600
  1.3 3.0 %collective-permute-start = (bf16[64,1024]{1,0:T(8,128)(2,1)S(1)}, bf16[64,1024]{1,0:T(8,128)(2,1)S(1)}, u32[]{:S(2)}, u32[]{:S(2)}) collective-permute-start(bf16[64,1024]{1,0:T(8,128)(2,1)S(1)} %get-tuple-element.33), channel_id=1, source_target_pairs={{0,8},{4,12},{8,0},{12,4},{16,24},{20,28},{24,16},{28,20},{1,9},{5... | collective-permute-start | bytes 393224 | tf_op jit(solution)/shard_map/ppermute | solution.py:353
  4.3 1.5 %collective-permute-start.1 = (bf16[64,1024]{1,0:T(8,128)(2,1)S(1)}, bf16[64,1024]{1,0:T(8,128)(2,1)S(1)}, u32[]{:S(2)}, u32[]{:S(2)}) collective-permute-start(bf16[64,1024]{1,0:T(8,128)(2,1)S(1)} %get-tuple-element.34), channel_id=1, source_target_pairs={{0,16},{4,20},{8,24},{12,28},{16,0},{20,4},{24,8},{28,12},{1,17},{... | collective-permute-start | bytes 393224 | tf_op jit(solution)/shard_map/ppermute | solution.py:353
  5.9 0.5 collective-permute-start.6
  6.4 1.5 %collective-permute-done.refs_1_ = bf16[64,1024]{1,0:T(8,128)(2,1)S(1)} collective-permute-done((bf16[64,1024]{1,0:T(8,128)(2,1)S(1)}, bf16[64,1024]{1,0:T(8,128)(2,1)S(1)}, u32[]{:S(2)}, u32[]{:S(2)}) %collective-permute-start) | collective-permute-done | bytes 131104 | tf_op jit(solution)/shard_map/ppermute | solution.py:353
  7.8 2.7 %collective-permute-start.2 = (bf16[64,1024]{1,0:T(8,128)(2,1)S(1)}, bf16[64,1024]{1,0:T(8,128)(2,1)S(1)}, u32[]{:S(2)}, u32[]{:S(2)}) collective-permute-start(bf16[64,1024]{1,0:T(8,128)(2,1)S(1)} %get-tuple-element.35), channel_id=1, source_target_pairs={{0,24},{4,28},{8,16},{12,20},{16,8},{20,12},{24,0},{28,4},{1,25},{... | collective-permute-start | bytes 393224 | tf_op jit(solution)/shard_map/ppermute | solution.py:353
  10.5 0.6 collective-permute-start.5
  11.1 0.3 collective-permute-start.7
  11.4 2.7 %collective-permute-start.9 = (bf16[64,1024]{1,0:T(8,128)(2,1)S(1)}, bf16[64,1024]{1,0:T(8,128)(2,1)S(1)}, u32[]{:S(2)}, u32[]{:S(2)}) collective-permute-start(bf16[64,1024]{1,0:T(8,128)(2,1)S(1)} %collective-permute-done.8), channel_id=1, source_target_pairs={{0,24},{4,28},{8,16},{12,20},{16,8},{20,12},{24,0},{28,4},{1,25},{... | collective-permute-start | bytes 393224 | tf_op jit(solution)/shard_map/ppermute | solution.py:353
  14.3 2.8 %collective-permute-done.5.refs_5_ = bf16[64,1024]{1,0:T(8,128)(2,1)S(1)} collective-permute-done((bf16[64,1024]{1,0:T(8,128)(2,1)S(1)}, bf16[64,1024]{1,0:T(8,128)(2,1)S(1)}, u32[]{:S(2)}, u32[]{:S(2)}) %collective-permute-start.5) | collective-permute-done | bytes 131104 | tf_op jit(solution)/shard_map/ppermute | solution.py:353
  17.2 2.3 %collective-permute-done.7.refs_6_ = bf16[64,1024]{1,0:T(8,128)(2,1)S(1)} collective-permute-done((bf16[64,1024]{1,0:T(8,128)(2,1)S(1)}, bf16[64,1024]{1,0:T(8,128)(2,1)S(1)}, u32[]{:S(2)}, u32[]{:S(2)}) %collective-permute-start.7) | collective-permute-done | bytes 131104 | tf_op jit(solution)/shard_map/ppermute | solution.py:353
  19.5 0.7 shard_map.55
  20.2 2.3 %collective-permute-start.10 = (bf16[64,1024]{1,0:T(8,128)(2,1)S(1)}, bf16[64,1024]{1,0:T(8,128)(2,1)S(1)}, u32[]{:S(2)}, u32[]{:S(2)}) collective-permute-start(bf16[64,1024]{1,0:T(8,128)(2,1)S(1)} %get-tuple-element.40.refs_2_), channel_id=1, source_target_pairs={{0,8},{4,12},{8,0},{12,4},{16,24},{20,28},{24,16},{28,20},{1,9},{5... | collective-permute-start | bytes 393224 | tf_op jit(solution)/shard_map/ppermute | solution.py:353
  22.5 1.0 %collective-permute-start.15 = (bf16[64,1024]{1,0:T(8,128)(2,1)S(1)}, bf16[64,1024]{1,0:T(8,128)(2,1)S(1)}, u32[]{:S(2)}, u32[]{:S(2)}) collective-permute-start(bf16[64,1024]{1,0:T(8,128)(2,1)S(1)} %get-tuple-element.41.refs_8_), channel_id=1, source_target_pairs={{0,16},{4,20},{8,24},{12,28},{16,0},{20,4},{24,8},{28,12},{1,17},{... | collective-permute-start | bytes 393224 | tf_op jit(solution)/shard_map/ppermute | solution.py:353
  23.6 0.7 copy-done.2
  24.5 1.7 %collective-permute-start.33 = (bf16[272,256]{1,0:T(8,128)(2,1)S(1)}, bf16[272,256]{1,0:T(8,128)(2,1)S(1)}, u32[]{:S(2)}, u32[]{:S(2)}) collective-permute-start(bf16[272,256]{1,0:T(8,128)(2,1)S(1)} %get-tuple-element.50), channel_id=1, source_target_pairs={{0,1},{1,0},{2,3},{3,2},{4,5},{5,4},{6,7},{7,6},{8,9},{9,8},{10,11... | collective-permute-start | bytes 417800 | tf_op jit(solution)/shard_map/ppermute | solution.py:353
  26.1 0.5 collective-permute-start.17
  26.7 0.7 shard_map.57
  27.3 0.5 collective-permute-start.20
  27.8 0.8 collective-permute-start.25
  28.6 1.0 %collective-permute-done.33.refs_1_.refs_5_ = bf16[272,256]{1,0:T(8,128)(2,1)S(1)} collective-permute-done((bf16[272,256]{1,0:T(8,128)(2,1)S(1)}, bf16[272,256]{1,0:T(8,128)(2,1)S(1)}, u32[]{:S(2)}, u32[]{:S(2)}) %collective-permute-start.33) | collective-permute-done | bytes 139296 | tf_op jit(solution)/shard_map/ppermute | solution.py:353
  29.6 1.1 %collective-permute-start.11 = (bf16[128,1024]{1,0:T(8,128)(2,1)S(1)}, bf16[128,1024]{1,0:T(8,128)(2,1)S(1)}, u32[]{:S(2)}, u32[]{:S(2)}) collective-permute-start(bf16[128,1024]{1,0:T(8,128)(2,1)S(1)} %pad_maximum_fusion), channel_id=1, source_target_pairs={{0,16},{4,20},{8,24},{12,28},{16,0},{20,4},{24,8},{28,12},{1,17},{... | collective-permute-start | bytes 786440 | tf_op jit(solution)/shard_map/ppermute | solution.py:353
  30.7 2.1 %collective-permute-done.20.refs_3_ = bf16[64,1024]{1,0:T(8,128)(2,1)S(1)} collective-permute-done((bf16[64,1024]{1,0:T(8,128)(2,1)S(1)}, bf16[64,1024]{1,0:T(8,128)(2,1)S(1)}, u32[]{:S(2)}, u32[]{:S(2)}) %collective-permute-start.20) | collective-permute-done | bytes 131104 | tf_op jit(solution)/shard_map/ppermute | solution.py:353
  32.8 0.4 collective-permute-start.16
  33.3 1.0 %collective-permute-done.25.refs_9_ = bf16[64,1024]{1,0:T(8,128)(2,1)S(1)} collective-permute-done((bf16[64,1024]{1,0:T(8,128)(2,1)S(1)}, bf16[64,1024]{1,0:T(8,128)(2,1)S(1)}, u32[]{:S(2)}, u32[]{:S(2)}) %collective-permute-start.25) | collective-permute-done | bytes 131104 | tf_op jit(solution)/shard_map/ppermute | solution.py:353
  34.3 0.7 collective-permute-start.21
  35.0 2.0 %collective-permute-start.26 = (bf16[128,1024]{1,0:T(8,128)(2,1)S(1)}, bf16[128,1024]{1,0:T(8,128)(2,1)S(1)}, u32[]{:S(2)}, u32[]{:S(2)}) collective-permute-start(bf16[128,1024]{1,0:T(8,128)(2,1)S(1)} %pad_maximum_fusion.3), channel_id=1, source_target_pairs={{0,8},{4,12},{8,0},{12,4},{16,24},{20,28},{24,16},{28,20},{1,9},{5... | collective-permute-start | bytes 786440 | tf_op jit(solution)/shard_map/ppermute | solution.py:353
  37.0 2.9 %collective-permute-done.11.refs_4_ = bf16[128,1024]{1,0:T(8,128)(2,1)S(1)} collective-permute-done((bf16[128,1024]{1,0:T(8,128)(2,1)S(1)}, bf16[128,1024]{1,0:T(8,128)(2,1)S(1)}, u32[]{:S(2)}, u32[]{:S(2)}) %collective-permute-start.11) | collective-permute-done | bytes 262176 | tf_op jit(solution)/shard_map/ppermute | solution.py:353
  39.9 2.1 %collective-permute-done.16.refs_10_ = bf16[128,1024]{1,0:T(8,128)(2,1)S(1)} collective-permute-done((bf16[128,1024]{1,0:T(8,128)(2,1)S(1)}, bf16[128,1024]{1,0:T(8,128)(2,1)S(1)}, u32[]{:S(2)}, u32[]{:S(2)}) %collective-permute-start.16) | collective-permute-done | bytes 262176 | tf_op jit(solution)/shard_map/ppermute | solution.py:353
  42.0 0.5 collective-permute-start.18
  42.5 1.8 %collective-permute-done.21.refs_4_ = bf16[128,1024]{1,0:T(8,128)(2,1)S(1)} collective-permute-done((bf16[128,1024]{1,0:T(8,128)(2,1)S(1)}, bf16[128,1024]{1,0:T(8,128)(2,1)S(1)}, u32[]{:S(2)}, u32[]{:S(2)}) %collective-permute-start.21) | collective-permute-done | bytes 262176 | tf_op jit(solution)/shard_map/ppermute | solution.py:353
  44.3 1.5 %collective-permute-done.26.refs_10_ = bf16[128,1024]{1,0:T(8,128)(2,1)S(1)} collective-permute-done((bf16[128,1024]{1,0:T(8,128)(2,1)S(1)}, bf16[128,1024]{1,0:T(8,128)(2,1)S(1)}, u32[]{:S(2)}, u32[]{:S(2)}) %collective-permute-start.26) | collective-permute-done | bytes 262176 | tf_op jit(solution)/shard_map/ppermute | solution.py:353
  45.8 0.5 collective-permute-start.27
  46.4 0.4 collective-permute-start.28
  46.8 2.4 %shard_map.56 = (bf16[256,2048]{1,0:T(8,128)(2,1)S(1)}, bf16[128,256]{1,0:T(8,128)(2,1)S(1)}, bf16[128,256]{1,0:T(8,128)(2,1)S(1)}, bf16[128,256]{1,0:T(8,128)(2,1)S(1)}, bf16[128,256]{1,0:T(8,128)(2,1)S(1)}) custom-call(bf16[256,2048]{1,0:T(8,128)(2,1)S(1)} %bitcast.6, bf16[1024,256]{1,0:T(8,128)(2,1)S(1)} %get-tuple-element.31.refs_1_, ...), custom_call_target="tpu_custom_call" | custom-call | flops 1610612736 | bytes 4194304 | tf_op jit(solution)/shard_map/pallas_call | solution.py:185
  49.2 2.7 %collective-permute-start.34 = (bf16[272,256]{1,0:T(8,128)(2,1)S(1)}, bf16[272,256]{1,0:T(8,128)(2,1)S(1)}, u32[]{:S(2)}, u32[]{:S(2)}) collective-permute-start(bf16[272,256]{1,0:T(8,128)(2,1)S(1)} %get-tuple-element.51), channel_id=1, source_target_pairs={{0,2},{1,3},{2,0},{3,1},{4,6},{5,7},{6,4},{7,5},{8,10},{9,11},{10,... | collective-permute-start | bytes 417800 | tf_op jit(solution)/shard_map/ppermute | solution.py:353
  52.1 0.7 collective-permute-start.36
  52.8 3.5 %collective-permute-start.37 = (bf16[128,256]{1,0:T(8,128)(2,1)S(1)}, bf16[128,256]{1,0:T(8,128)(2,1)S(1)}, u32[]{:S(2)}, u32[]{:S(2)}) collective-permute-start(bf16[128,256]{1,0:T(8,128)(2,1)S(1)} %get-tuple-element.55), channel_id=1, source_target_pairs={{0,2},{1,3},{2,0},{3,1},{4,6},{5,7},{6,4},{7,5},{8,10},{9,11},{10,... | collective-permute-start | bytes 196616 | tf_op jit(solution)/shard_map/ppermute | solution.py:353
  56.5 1.9 %shard_map.58 = (bf16[128,256]{1,0:T(8,128)(2,1)S(1)}, bf16[128,256]{1,0:T(8,128)(2,1)S(1)}, bf16[128,256]{1,0:T(8,128)(2,1)S(1)}, bf16[128,256]{1,0:T(8,128)(2,1)S(1)}) custom-call(bf16[256,2048]{1,0:T(8,128)(2,1)S(1)} %get-tuple-element.42.refs_0_, bf16[1024,256]{1,0:T(8,128)(2,1)S(1)} %get-tuple-element.31.refs_1_, ...), custom_call_target="tpu_custom_call" | custom-call | flops 1610612736 | bytes 4194304 | tf_op jit(solution)/shard_map/pallas_call | solution.py:185
  58.4 6.2 %collective-permute-done.34.refs_2_.refs_6_ = bf16[272,256]{1,0:T(8,128)(2,1)S(1)} collective-permute-done((bf16[272,256]{1,0:T(8,128)(2,1)S(1)}, bf16[272,256]{1,0:T(8,128)(2,1)S(1)}, u32[]{:S(2)}, u32[]{:S(2)}) %collective-permute-start.34) | collective-permute-done | bytes 139296 | tf_op jit(solution)/shard_map/ppermute | solution.py:353
  64.6 0.6 collective-permute-start.30
  65.2 4.9 %collective-permute-start.31 = (bf16[128,256]{1,0:T(8,128)(2,1)S(1)}, bf16[128,256]{1,0:T(8,128)(2,1)S(1)}, u32[]{:S(2)}, u32[]{:S(2)}) collective-permute-start(bf16[128,256]{1,0:T(8,128)(2,1)S(1)} %get-tuple-element.47), channel_id=1, source_target_pairs={{0,2},{1,3},{2,0},{3,1},{4,6},{5,7},{6,4},{7,5},{8,10},{9,11},{10,... | collective-permute-start | bytes 196616 | tf_op jit(solution)/shard_map/ppermute | solution.py:353
  70.1 0.4 collective-permute-start.32
  70.5 0.8 place.1.refs_8_
  71.3 2.6 %shard_map.59.refs_9_ = f32[2048,128]{1,0:T(8,128)} custom-call(bf16[128,256]{1,0:T(8,128)(2,1)S(1)} %get-tuple-element.53.refs_0_, bf16[128,256]{1,0:T(8,128)(2,1)S(1)} %collective-permute-done.36.refs_1_, bf16[128,256]{1,0:T(8,128)(2,1)S(1)} %collective-permute-done.37.refs_2_, bf16[128,256]{1,0:T(8,128)(2,1)S(1)} %collective-permute-done.38.refs_3_, ...), custom_call_target="tpu_custom_call" | custom-call | flops 268435456 | bytes 1048576 | tf_op jit(solution)/shard_map/pallas_call | solution.py:332
  73.9 0.6 collective-permute-done.31.refs_2_
  74.6 1.6 %collective-permute-done.32.refs_3_ = bf16[128,256]{1,0:T(8,128)(2,1)S(1)} collective-permute-done((bf16[128,256]{1,0:T(8,128)(2,1)S(1)}, bf16[128,256]{1,0:T(8,128)(2,1)S(1)}, u32[]{:S(2)}, u32[]{:S(2)}) %collective-permute-start.32) | collective-permute-done | bytes 65568 | tf_op jit(solution)/shard_map/ppermute | solution.py:353
  76.1 2.6 %shard_map.60 = f32[2048,128]{1,0:T(8,128)} custom-call(bf16[128,256]{1,0:T(8,128)(2,1)S(1)} %get-tuple-element.45.refs_0_, bf16[128,256]{1,0:T(8,128)(2,1)S(1)} %collective-permute-done.30.refs_1_, bf16[128,256]{1,0:T(8,128)(2,1)S(1)} %collective-permute-done.31.refs_2_, ...), custom_call_target="tpu_custom_call", output_to_operand_aliasing={{}: (9, {})} | custom-call | flops 268435456 | bytes 1048576 | tf_op jit(solution)/shard_map/pallas_call | solution.py:332
  (54 shorter events, 1.4 us)
Async XLA Ops:
  0.0 1.2 %copy-start = (bf16[256,2048]{1,0:T(8,128)(2,1)S(1)}, bf16[256,2048]{1,0:T(8,128)(2,1)}, u32[]{:S(2)}) copy-start(bf16[256,2048]{1,0:T(8,128)(2,1)} %block_ref.1) | copy-start | bytes 3145732
  1.3 6.5 %collective-permute-start = (bf16[64,1024]{1,0:T(8,128)(2,1)S(1)}, bf16[64,1024]{1,0:T(8,128)(2,1)S(1)}, u32[]{:S(2)}, u32[]{:S(2)}) collective-permute-start(bf16[64,1024]{1,0:T(8,128)(2,1)S(1)} %get-tuple-element.33), channel_id=1, source_target_pairs={{0,8},{4,12},{8,0},{12,4},{16,24},{20,28},{24,16},{28,20},{1,9},{5... | collective-permute-start | bytes 393224 | tf_op jit(solution)/shard_map/ppermute | solution.py:353
  4.3 6.2 %collective-permute-start.1 = (bf16[64,1024]{1,0:T(8,128)(2,1)S(1)}, bf16[64,1024]{1,0:T(8,128)(2,1)S(1)}, u32[]{:S(2)}, u32[]{:S(2)}) collective-permute-start(bf16[64,1024]{1,0:T(8,128)(2,1)S(1)} %get-tuple-element.34), channel_id=1, source_target_pairs={{0,16},{4,20},{8,24},{12,28},{16,0},{20,4},{24,8},{28,12},{1,17},{... | collective-permute-start | bytes 393224 | tf_op jit(solution)/shard_map/ppermute | solution.py:353
  5.8 4.7 %collective-permute-start.4 = (bf16[64,1024]{1,0:T(8,128)(2,1)S(1)}, bf16[64,1024]{1,0:T(8,128)(2,1)S(1)}, u32[]{:S(2)}, u32[]{:S(2)}) collective-permute-start(bf16[64,1024]{1,0:T(8,128)(2,1)S(1)} %get-tuple-element.37), channel_id=1, source_target_pairs={{0,4},{4,0},{8,12},{12,8},{16,20},{20,16},{24,28},{28,24},{1,5},{5... | collective-permute-start | bytes 393224 | tf_op jit(solution)/shard_map/ppermute | solution.py:353
  5.9 5.3 %collective-permute-start.6 = (bf16[64,1024]{1,0:T(8,128)(2,1)S(1)}, bf16[64,1024]{1,0:T(8,128)(2,1)S(1)}, u32[]{:S(2)}, u32[]{:S(2)}) collective-permute-start(bf16[64,1024]{1,0:T(8,128)(2,1)S(1)} %get-tuple-element.38), channel_id=1, source_target_pairs={{0,4},{4,0},{8,12},{12,8},{16,20},{20,16},{24,28},{28,24},{1,5},{5... | collective-permute-start | bytes 393224 | tf_op jit(solution)/shard_map/ppermute | solution.py:353
  6.4 5.1 %collective-permute-start.8 = (bf16[64,1024]{1,0:T(8,128)(2,1)S(1)}, bf16[64,1024]{1,0:T(8,128)(2,1)S(1)}, u32[]{:S(2)}, u32[]{:S(2)}) collective-permute-start(bf16[64,1024]{1,0:T(8,128)(2,1)S(1)} %get-tuple-element.39), channel_id=1, source_target_pairs={{0,4},{4,0},{8,12},{12,8},{16,20},{20,16},{24,28},{28,24},{1,5},{5... | collective-permute-start | bytes 393224 | tf_op jit(solution)/shard_map/ppermute | solution.py:353
  7.8 6.5 %collective-permute-start.2 = (bf16[64,1024]{1,0:T(8,128)(2,1)S(1)}, bf16[64,1024]{1,0:T(8,128)(2,1)S(1)}, u32[]{:S(2)}, u32[]{:S(2)}) collective-permute-start(bf16[64,1024]{1,0:T(8,128)(2,1)S(1)} %get-tuple-element.35), channel_id=1, source_target_pairs={{0,24},{4,28},{8,16},{12,20},{16,8},{20,12},{24,0},{28,4},{1,25},{... | collective-permute-start | bytes 393224 | tf_op jit(solution)/shard_map/ppermute | solution.py:353
  10.5 9.0 %copy-start.1 = (s32[8]{0:T(128)S(1)}, s32[8]{0:T(128)}, u32[]{:S(2)}) copy-start(s32[8]{0:T(128)} %order_ref.3) | copy-start | bytes 100
  10.5 3.8 %collective-permute-start.3 = (bf16[64,1024]{1,0:T(8,128)(2,1)S(1)}, bf16[64,1024]{1,0:T(8,128)(2,1)S(1)}, u32[]{:S(2)}, u32[]{:S(2)}) collective-permute-start(bf16[64,1024]{1,0:T(8,128)(2,1)S(1)} %get-tuple-element.36), channel_id=1, source_target_pairs={{0,4},{4,0},{8,12},{12,8},{16,20},{20,16},{24,28},{28,24},{1,5},{5... | collective-permute-start | bytes 393224 | tf_op jit(solution)/shard_map/ppermute | solution.py:353
  10.5 6.6 %collective-permute-start.5 = (bf16[64,1024]{1,0:T(8,128)(2,1)S(1)}, bf16[64,1024]{1,0:T(8,128)(2,1)S(1)}, u32[]{:S(2)}, u32[]{:S(2)}) collective-permute-start(bf16[64,1024]{1,0:T(8,128)(2,1)S(1)} %collective-permute-done.4), channel_id=1, source_target_pairs={{0,8},{4,12},{8,0},{12,4},{16,24},{20,28},{24,16},{28,20},{1,9},{5... | collective-permute-start | bytes 393224 | tf_op jit(solution)/shard_map/ppermute | solution.py:353
  11.1 8.4 %collective-permute-start.7 = (bf16[64,1024]{1,0:T(8,128)(2,1)S(1)}, bf16[64,1024]{1,0:T(8,128)(2,1)S(1)}, u32[]{:S(2)}, u32[]{:S(2)}) collective-permute-start(bf16[64,1024]{1,0:T(8,128)(2,1)S(1)} %collective-permute-done.6), channel_id=1, source_target_pairs={{0,16},{4,20},{8,24},{12,28},{16,0},{20,4},{24,8},{28,12},{1,17},{... | collective-permute-start | bytes 393224 | tf_op jit(solution)/shard_map/ppermute | solution.py:353
  11.4 8.1 %collective-permute-start.9 = (bf16[64,1024]{1,0:T(8,128)(2,1)S(1)}, bf16[64,1024]{1,0:T(8,128)(2,1)S(1)}, u32[]{:S(2)}, u32[]{:S(2)}) collective-permute-start(bf16[64,1024]{1,0:T(8,128)(2,1)S(1)} %collective-permute-done.8), channel_id=1, source_target_pairs={{0,24},{4,28},{8,16},{12,20},{16,8},{20,12},{24,0},{28,4},{1,25},{... | collective-permute-start | bytes 393224 | tf_op jit(solution)/shard_map/ppermute | solution.py:353
  19.5 3.9 %copy-start.4 = (bf16[1,256,4,256]{3,2,1,0:T(4,128)(2,1)S(1)}, bf16[1,256,4,256]{3,2,1,0:T(4,128)(2,1)}, u32[]{:S(2)}) copy-start(bf16[1,256,4,256]{3,2,1,0:T(4,128)(2,1)} %param.6) | copy-start | bytes 1572868
  20.2 7.1 %collective-permute-start.10 = (bf16[64,1024]{1,0:T(8,128)(2,1)S(1)}, bf16[64,1024]{1,0:T(8,128)(2,1)S(1)}, u32[]{:S(2)}, u32[]{:S(2)}) collective-permute-start(bf16[64,1024]{1,0:T(8,128)(2,1)S(1)} %get-tuple-element.40.refs_2_), channel_id=1, source_target_pairs={{0,8},{4,12},{8,0},{12,4},{16,24},{20,28},{24,16},{28,20},{1,9},{5... | collective-permute-start | bytes 393224 | tf_op jit(solution)/shard_map/ppermute | solution.py:353
  22.5 5.4 %collective-permute-start.15 = (bf16[64,1024]{1,0:T(8,128)(2,1)S(1)}, bf16[64,1024]{1,0:T(8,128)(2,1)S(1)}, u32[]{:S(2)}, u32[]{:S(2)}) collective-permute-start(bf16[64,1024]{1,0:T(8,128)(2,1)S(1)} %get-tuple-element.41.refs_8_), channel_id=1, source_target_pairs={{0,16},{4,20},{8,24},{12,28},{16,0},{20,4},{24,8},{28,12},{1,17},{... | collective-permute-start | bytes 393224 | tf_op jit(solution)/shard_map/ppermute | solution.py:353
  23.5 0.7 copy-start.2
  24.5 5.1 %collective-permute-start.33 = (bf16[272,256]{1,0:T(8,128)(2,1)S(1)}, bf16[272,256]{1,0:T(8,128)(2,1)S(1)}, u32[]{:S(2)}, u32[]{:S(2)}) collective-permute-start(bf16[272,256]{1,0:T(8,128)(2,1)S(1)} %get-tuple-element.50), channel_id=1, source_target_pairs={{0,1},{1,0},{2,3},{3,2},{4,5},{5,4},{6,7},{7,6},{8,9},{9,8},{10,11... | collective-permute-start | bytes 417800 | tf_op jit(solution)/shard_map/ppermute | solution.py:353
  26.1 7.1 %collective-permute-start.12 = (bf16[64,1024]{1,0:T(8,128)(2,1)S(1)}, bf16[64,1024]{1,0:T(8,128)(2,1)S(1)}, u32[]{:S(2)}, u32[]{:S(2)}) collective-permute-start(bf16[64,1024]{1,0:T(8,128)(2,1)S(1)} %get-tuple-element.40.refs_2_), channel_id=1, source_target_pairs={{0,4},{4,0},{8,12},{12,8},{16,20},{20,16},{24,28},{28,24},{1,5},{5... | collective-permute-start | bytes 393224 | tf_op jit(solution)/shard_map/ppermute | solution.py:353
  26.1 8.8 %collective-permute-start.17 = (bf16[64,1024]{1,0:T(8,128)(2,1)S(1)}, bf16[64,1024]{1,0:T(8,128)(2,1)S(1)}, u32[]{:S(2)}, u32[]{:S(2)}) collective-permute-start(bf16[64,1024]{1,0:T(8,128)(2,1)S(1)} %get-tuple-element.41.refs_8_), channel_id=1, source_target_pairs={{0,4},{4,0},{8,12},{12,8},{16,20},{20,16},{24,28},{28,24},{1,5},{5... | collective-permute-start | bytes 393224 | tf_op jit(solution)/shard_map/ppermute | solution.py:353
  27.3 19.5 %copy-start.3 = (bf16[1,256,2048]{2,1,0:T(8,128)(2,1)S(1)}, bf16[1,256,2048]{2,1,0:T(8,128)(2,1)}, u32[]{:S(2)}) copy-start(bf16[1,256,2048]{2,1,0:T(8,128)(2,1)} %param.5) | copy-start | bytes 3145732
  27.3 5.5 %collective-permute-start.20 = (bf16[64,1024]{1,0:T(8,128)(2,1)S(1)}, bf16[64,1024]{1,0:T(8,128)(2,1)S(1)}, u32[]{:S(2)}, u32[]{:S(2)}) collective-permute-start(bf16[64,1024]{1,0:T(8,128)(2,1)S(1)} %get-tuple-element.43.refs_2_), channel_id=1, source_target_pairs={{0,8},{4,12},{8,0},{12,4},{16,24},{20,28},{24,16},{28,20},{1,9},{5... | collective-permute-start | bytes 393224 | tf_op jit(solution)/shard_map/ppermute | solution.py:353
  27.8 6.4 %collective-permute-start.25 = (bf16[64,1024]{1,0:T(8,128)(2,1)S(1)}, bf16[64,1024]{1,0:T(8,128)(2,1)S(1)}, u32[]{:S(2)}, u32[]{:S(2)}) collective-permute-start(bf16[64,1024]{1,0:T(8,128)(2,1)S(1)} %get-tuple-element.44.refs_8_), channel_id=1, source_target_pairs={{0,16},{4,20},{8,24},{12,28},{16,0},{20,4},{24,8},{28,12},{1,17},{... | collective-permute-start | bytes 393224 | tf_op jit(solution)/shard_map/ppermute | solution.py:353
  29.6 10.3 %collective-permute-start.11 = (bf16[128,1024]{1,0:T(8,128)(2,1)S(1)}, bf16[128,1024]{1,0:T(8,128)(2,1)S(1)}, u32[]{:S(2)}, u32[]{:S(2)}) collective-permute-start(bf16[128,1024]{1,0:T(8,128)(2,1)S(1)} %pad_maximum_fusion), channel_id=1, source_target_pairs={{0,16},{4,20},{8,24},{12,28},{16,0},{20,4},{24,8},{28,12},{1,17},{... | collective-permute-start | bytes 786440 | tf_op jit(solution)/shard_map/ppermute | solution.py:353
  32.8 9.2 %collective-permute-start.16 = (bf16[128,1024]{1,0:T(8,128)(2,1)S(1)}, bf16[128,1024]{1,0:T(8,128)(2,1)S(1)}, u32[]{:S(2)}, u32[]{:S(2)}) collective-permute-start(bf16[128,1024]{1,0:T(8,128)(2,1)S(1)} %pad_maximum_fusion.1), channel_id=1, source_target_pairs={{0,8},{4,12},{8,0},{12,4},{16,24},{20,28},{24,16},{28,20},{1,9},{5... | collective-permute-start | bytes 786440 | tf_op jit(solution)/shard_map/ppermute | solution.py:353
  33.2 3.8 %collective-permute-start.22 = (bf16[64,1024]{1,0:T(8,128)(2,1)S(1)}, bf16[64,1024]{1,0:T(8,128)(2,1)S(1)}, u32[]{:S(2)}, u32[]{:S(2)}) collective-permute-start(bf16[64,1024]{1,0:T(8,128)(2,1)S(1)} %get-tuple-element.43.refs_2_), channel_id=1, source_target_pairs={{0,4},{4,0},{8,12},{12,8},{16,20},{20,16},{24,28},{28,24},{1,5},{5... | collective-permute-start | bytes 393224 | tf_op jit(solution)/shard_map/ppermute | solution.py:353
  34.3 10.0 %collective-permute-start.21 = (bf16[128,1024]{1,0:T(8,128)(2,1)S(1)}, bf16[128,1024]{1,0:T(8,128)(2,1)S(1)}, u32[]{:S(2)}, u32[]{:S(2)}) collective-permute-start(bf16[128,1024]{1,0:T(8,128)(2,1)S(1)} %pad_maximum_fusion.2), channel_id=1, source_target_pairs={{0,16},{4,20},{8,24},{12,28},{16,0},{20,4},{24,8},{28,12},{1,17},{... | collective-permute-start | bytes 786440 | tf_op jit(solution)/shard_map/ppermute | solution.py:353
  35.0 10.8 %collective-permute-start.26 = (bf16[128,1024]{1,0:T(8,128)(2,1)S(1)}, bf16[128,1024]{1,0:T(8,128)(2,1)S(1)}, u32[]{:S(2)}, u32[]{:S(2)}) collective-permute-start(bf16[128,1024]{1,0:T(8,128)(2,1)S(1)} %pad_maximum_fusion.3), channel_id=1, source_target_pairs={{0,8},{4,12},{8,0},{12,4},{16,24},{20,28},{24,16},{28,20},{1,9},{5... | collective-permute-start | bytes 786440 | tf_op jit(solution)/shard_map/ppermute | solution.py:353
  37.0 5.0 %collective-permute-start.13 = (bf16[64,1024]{1,0:T(8,128)(2,1)S(1)}, bf16[64,1024]{1,0:T(8,128)(2,1)S(1)}, u32[]{:S(2)}, u32[]{:S(2)}) collective-permute-start(bf16[64,1024]{1,0:T(8,128)(2,1)S(1)} %collective-permute-done.10.refs_3_), channel_id=1, source_target_pairs={{0,4},{4,0},{8,12},{12,8},{16,20},{20,16},{24,28},{28,24},{1,5},{5... | collective-permute-start | bytes 393224 | tf_op jit(solution)/shard_map/ppermute | solution.py:353
  39.9 6.4 %collective-permute-start.14 = (bf16[128,1024]{1,0:T(8,128)(2,1)S(1)}, bf16[128,1024]{1,0:T(8,128)(2,1)S(1)}, u32[]{:S(2)}, u32[]{:S(2)}) collective-permute-start(bf16[128,1024]{1,0:T(8,128)(2,1)S(1)} %collective-permute-done.11.refs_4_), channel_id=1, source_target_pairs={{0,4},{4,0},{8,12},{12,8},{16,20},{20,16},{24,28},{28,24},{1,5},{5... | collective-permute-start | bytes 786440 | tf_op jit(solution)/shard_map/ppermute | solution.py:353
  42.0 4.4 %collective-permute-start.19 = (bf16[128,1024]{1,0:T(8,128)(2,1)S(1)}, bf16[128,1024]{1,0:T(8,128)(2,1)S(1)}, u32[]{:S(2)}, u32[]{:S(2)}) collective-permute-start(bf16[128,1024]{1,0:T(8,128)(2,1)S(1)} %collective-permute-done.16.refs_10_), channel_id=1, source_target_pairs={{0,4},{4,0},{8,12},{12,8},{16,20},{20,16},{24,28},{28,24},{1,5},{5... | collective-permute-start | bytes 786440 | tf_op jit(solution)/shard_map/ppermute | solution.py:353
  42.0 3.8 %collective-permute-start.18 = (bf16[64,1024]{1,0:T(8,128)(2,1)S(1)}, bf16[64,1024]{1,0:T(8,128)(2,1)S(1)}, u32[]{:S(2)}, u32[]{:S(2)}) collective-permute-start(bf16[64,1024]{1,0:T(8,128)(2,1)S(1)} %collective-permute-done.15.refs_9_), channel_id=1, source_target_pairs={{0,4},{4,0},{8,12},{12,8},{16,20},{20,16},{24,28},{28,24},{1,5},{5... | collective-permute-start | bytes 393224 | tf_op jit(solution)/shard_map/ppermute | solution.py:353
  44.3 8.5 %collective-permute-start.24 = (bf16[128,1024]{1,0:T(8,128)(2,1)S(1)}, bf16[128,1024]{1,0:T(8,128)(2,1)S(1)}, u32[]{:S(2)}, u32[]{:S(2)}) collective-permute-start(bf16[128,1024]{1,0:T(8,128)(2,1)S(1)} %collective-permute-done.21.refs_4_), channel_id=1, source_target_pairs={{0,4},{4,0},{8,12},{12,8},{16,20},{20,16},{24,28},{28,24},{1,5},{5... | collective-permute-start | bytes 786440 | tf_op jit(solution)/shard_map/ppermute | solution.py:353
  45.8 10.5 %collective-permute-start.29 = (bf16[128,1024]{1,0:T(8,128)(2,1)S(1)}, bf16[128,1024]{1,0:T(8,128)(2,1)S(1)}, u32[]{:S(2)}, u32[]{:S(2)}) collective-permute-start(bf16[128,1024]{1,0:T(8,128)(2,1)S(1)} %collective-permute-done.26.refs_10_), channel_id=1, source_target_pairs={{0,4},{4,0},{8,12},{12,8},{16,20},{20,16},{24,28},{28,24},{1,5},{5... | collective-permute-start | bytes 786440 | tf_op jit(solution)/shard_map/ppermute | solution.py:353
  45.8 3.4 %collective-permute-start.27 = (bf16[64,1024]{1,0:T(8,128)(2,1)S(1)}, bf16[64,1024]{1,0:T(8,128)(2,1)S(1)}, u32[]{:S(2)}, u32[]{:S(2)}) collective-permute-start(bf16[64,1024]{1,0:T(8,128)(2,1)S(1)} %get-tuple-element.44.refs_8_), channel_id=1, source_target_pairs={{0,4},{4,0},{8,12},{12,8},{16,20},{20,16},{24,28},{28,24},{1,5},{5... | collective-permute-start | bytes 393224 | tf_op jit(solution)/shard_map/ppermute | solution.py:353
  46.3 5.5 %collective-permute-start.23 = (bf16[64,1024]{1,0:T(8,128)(2,1)S(1)}, bf16[64,1024]{1,0:T(8,128)(2,1)S(1)}, u32[]{:S(2)}, u32[]{:S(2)}) collective-permute-start(bf16[64,1024]{1,0:T(8,128)(2,1)S(1)} %collective-permute-done.20.refs_3_), channel_id=1, source_target_pairs={{0,4},{4,0},{8,12},{12,8},{16,20},{20,16},{24,28},{28,24},{1,5},{5... | collective-permute-start | bytes 393224 | tf_op jit(solution)/shard_map/ppermute | solution.py:353
  46.4 5.7 %collective-permute-start.28 = (bf16[64,1024]{1,0:T(8,128)(2,1)S(1)}, bf16[64,1024]{1,0:T(8,128)(2,1)S(1)}, u32[]{:S(2)}, u32[]{:S(2)}) collective-permute-start(bf16[64,1024]{1,0:T(8,128)(2,1)S(1)} %collective-permute-done.25.refs_9_), channel_id=1, source_target_pairs={{0,4},{4,0},{8,12},{12,8},{16,20},{20,16},{24,28},{28,24},{1,5},{5... | collective-permute-start | bytes 393224 | tf_op jit(solution)/shard_map/ppermute | solution.py:353
  49.2 15.4 %collective-permute-start.34 = (bf16[272,256]{1,0:T(8,128)(2,1)S(1)}, bf16[272,256]{1,0:T(8,128)(2,1)S(1)}, u32[]{:S(2)}, u32[]{:S(2)}) collective-permute-start(bf16[272,256]{1,0:T(8,128)(2,1)S(1)} %get-tuple-element.51), channel_id=1, source_target_pairs={{0,2},{1,3},{2,0},{3,1},{4,6},{5,7},{6,4},{7,5},{8,10},{9,11},{10,... | collective-permute-start | bytes 417800 | tf_op jit(solution)/shard_map/ppermute | solution.py:353
  51.9 13.3 %collective-permute-start.35 = (bf16[272,256]{1,0:T(8,128)(2,1)S(1)}, bf16[272,256]{1,0:T(8,128)(2,1)S(1)}, u32[]{:S(2)}, u32[]{:S(2)}) collective-permute-start(bf16[272,256]{1,0:T(8,128)(2,1)S(1)} %get-tuple-element.52), channel_id=1, source_target_pairs={{0,3},{1,2},{2,1},{3,0},{4,7},{5,6},{6,5},{7,4},{8,11},{9,10},{10,... | collective-permute-start | bytes 417800 | tf_op jit(solution)/shard_map/ppermute | solution.py:353
  52.1 18.0 %collective-permute-start.36 = (bf16[128,256]{1,0:T(8,128)(2,1)S(1)}, bf16[128,256]{1,0:T(8,128)(2,1)S(1)}, u32[]{:S(2)}, u32[]{:S(2)}) collective-permute-start(bf16[128,256]{1,0:T(8,128)(2,1)S(1)} %get-tuple-element.54), channel_id=1, source_target_pairs={{0,1},{1,0},{2,3},{3,2},{4,5},{5,4},{6,7},{7,6},{8,9},{9,8},{10,11... | collective-permute-start | bytes 196616 | tf_op jit(solution)/shard_map/ppermute | solution.py:353
  52.8 18.5 %collective-permute-start.37 = (bf16[128,256]{1,0:T(8,128)(2,1)S(1)}, bf16[128,256]{1,0:T(8,128)(2,1)S(1)}, u32[]{:S(2)}, u32[]{:S(2)}) collective-permute-start(bf16[128,256]{1,0:T(8,128)(2,1)S(1)} %get-tuple-element.55), channel_id=1, source_target_pairs={{0,2},{1,3},{2,0},{3,1},{4,6},{5,7},{6,4},{7,5},{8,10},{9,11},{10,... | collective-permute-start | bytes 196616 | tf_op jit(solution)/shard_map/ppermute | solution.py:353
  56.3 15.0 %collective-permute-start.38 = (bf16[128,256]{1,0:T(8,128)(2,1)S(1)}, bf16[128,256]{1,0:T(8,128)(2,1)S(1)}, u32[]{:S(2)}, u32[]{:S(2)}) collective-permute-start(bf16[128,256]{1,0:T(8,128)(2,1)S(1)} %get-tuple-element.56), channel_id=1, source_target_pairs={{0,3},{1,2},{2,1},{3,0},{4,7},{5,6},{6,5},{7,4},{8,11},{9,10},{10,... | collective-permute-start | bytes 196616 | tf_op jit(solution)/shard_map/ppermute | solution.py:353
  64.6 9.3 %collective-permute-start.30 = (bf16[128,256]{1,0:T(8,128)(2,1)S(1)}, bf16[128,256]{1,0:T(8,128)(2,1)S(1)}, u32[]{:S(2)}, u32[]{:S(2)}) collective-permute-start(bf16[128,256]{1,0:T(8,128)(2,1)S(1)} %get-tuple-element.46), channel_id=1, source_target_pairs={{0,1},{1,0},{2,3},{3,2},{4,5},{5,4},{6,7},{7,6},{8,9},{9,8},{10,11... | collective-permute-start | bytes 196616 | tf_op jit(solution)/shard_map/ppermute | solution.py:353
  65.2 9.4 %collective-permute-start.31 = (bf16[128,256]{1,0:T(8,128)(2,1)S(1)}, bf16[128,256]{1,0:T(8,128)(2,1)S(1)}, u32[]{:S(2)}, u32[]{:S(2)}) collective-permute-start(bf16[128,256]{1,0:T(8,128)(2,1)S(1)} %get-tuple-element.47), channel_id=1, source_target_pairs={{0,2},{1,3},{2,0},{3,1},{4,6},{5,7},{6,4},{7,5},{8,10},{9,11},{10,... | collective-permute-start | bytes 196616 | tf_op jit(solution)/shard_map/ppermute | solution.py:353
  70.1 6.1 %collective-permute-start.32 = (bf16[128,256]{1,0:T(8,128)(2,1)S(1)}, bf16[128,256]{1,0:T(8,128)(2,1)S(1)}, u32[]{:S(2)}, u32[]{:S(2)}) collective-permute-start(bf16[128,256]{1,0:T(8,128)(2,1)S(1)} %get-tuple-element.48), channel_id=1, source_target_pairs={{0,3},{1,2},{2,1},{3,0},{4,7},{5,6},{6,5},{7,4},{8,11},{9,10},{10,... | collective-permute-start | bytes 196616 | tf_op jit(solution)/shard_map/ppermute | solution.py:353
